TPU v7x, 32 devices: a whole 2x2x4 slice. The times are simulated.
32 devices in a mesh: groups: 2 (over y), shot: 4 (over z), slab: 4 (over x, core).
Axes of the slice: x: 2, y: 2, z: 4, core: 2. Of those that a mesh axis runs over, the one named last changes fastest.
Arguments:
- model: float32 [64, 64, 128], P(('groups', 'slab')), parts along dimension 0, may hold values from 0.05 to 0.3
- fwd_now: float32 [8, 32, 64, 128], P(('groups', 'shot'), 'slab'), parts along dimension 0, may hold values from -6 to 6
- fwd_next: float32 [8, 32, 64, 128], P(('groups', 'shot'), 'slab'), parts along dimension 0, may hold values from -6 to 6
- adj_now: float32 [8, 32, 64, 128], P(('groups', 'shot'), 'slab'), parts along dimension 0, may hold values from -6 to 6
- adj_next: float32 [8, 32, 64, 128], P(('groups', 'shot'), 'slab'), parts along dimension 0, may hold values from -6 to 6
- wavelet: float32 [8, 8], P(('groups', 'shot')), parts along dimension 0, may hold values from -16 to 16
- misfit: float32 [8, 8, 128], P(('groups', 'shot')), parts along dimension 0, may hold values from -6 to 6
- src_index: int32 [8], P(('groups', 'shot')), parts along dimension 0, may hold values from 0 to 262143
- rec_index: int32 [8, 128], P(('groups', 'shot')), parts along dimension 0, may hold values from 0 to 262143
Outputs:
- new_model: float32 [64, 64, 128], P(('groups', 'slab')), parts along dimension 0
- stepped: float32 [8, 32, 64, 128], P(('groups', 'shot'), 'slab'), parts along dimension 0
- adjoint_start: float32 [8, 32, 64, 128], P(('groups', 'shot'), 'slab'), parts along dimension 0
There are 2 independent parts, one for each index of `groups`. A program takes and returns all parts, laid end to end along the dimension named above; each array names one. Nothing has to cross between parts.
All inputs are finite; a program needn't handle non-finite values. Where the computation divides by a largest or mean magnitude, that divisor is 1e-20 or more.
Results may differ from a plain program's by a relative error of at most 0.00002.
Values sent between devices are 32-bit elements; how exact they have to be, the bound alone decides.
No kernel may reach another device: no remote copies, remote signals or barrier semaphores. Data moves between devices by JAX's collectives and lax.ppermute only.
A program may use at most 64 MiB of HBM per device.

v0:
```python
import jax
import jax.numpy as jnp
from jax import lax
from jax.sharding import PartitionSpec as P

ITERS = 8


def extended(block, sides, width):
    for axis, dim in sides:
        count = lax.axis_size(axis)
        forward = [(i, i + 1) for i in range(count - 1)]
        backward = [(target, source) for source, target in forward]
        low = lax.ppermute(
            lax.slice_in_dim(block, block.shape[dim] - width, None, axis=dim), axis, forward
        )
        high = lax.ppermute(lax.slice_in_dim(block, 0, width, axis=dim), axis, backward)
        block = jnp.concatenate([low, block, high], axis=dim)
    return block


def local_laplace(padded):
    full = jnp.pad(padded, ((0, 0), (0, 0), (1, 1), (1, 1)))
    center = full[:, 1:-1, 1:-1, 1:-1]
    beside = full[:, 2:, 1:-1, 1:-1] + full[:, :-2, 1:-1, 1:-1]
    beside = beside + full[:, 1:-1, 2:, 1:-1] + full[:, 1:-1, :-2, 1:-1]
    beside = beside + full[:, 1:-1, 1:-1, 2:] + full[:, 1:-1, 1:-1, :-2]
    return beside - 6.0 * center


def inject(field, index, values, offset):
    shots = field.shape[0]
    cells = field.shape[1] * field.shape[2] * field.shape[3]
    flat = field.reshape(shots, -1)
    local = index - offset
    valid = (local >= 0) & (local < cells)
    local = jnp.clip(local, 0, cells - 1)
    rows = jnp.arange(shots, dtype=jnp.int32).reshape((shots,) + (1,) * (index.ndim - 1))
    rows = jnp.broadcast_to(rows, index.shape)
    flat = flat.at[rows, local].add(jnp.where(valid, values, 0.0))
    return flat.reshape(field.shape)


def update(model, gradient, peak):
    return jnp.clip(model - 0.1 * gradient / (peak + 1e-06), 0.05, 0.3)


def per_device(model, fwd_now, fwd_next, adj_now, adj_next, wavelet, misfit, src_index, rec_index):
    shots = fwd_now.shape[0]
    depth, width, length = model.shape
    offset = lax.axis_index("slab") * (depth * width * length)
    wave, wave_later = (fwd_now, fwd_next)
    adjoint, adjoint_later = (adj_now, adj_next)
    image = jnp.zeros_like(fwd_now)
    for step in range(ITERS):
        stacked = jnp.concatenate([wave, adjoint], axis=0)
        padded = extended(stacked, (("slab", 1),), 1)
        laps = local_laplace(padded)
        lap_wave = laps[:shots]
        lap_adjoint = laps[shots:]
        image = image + adjoint * lap_wave
        wave_prior = 2.0 * wave - wave_later + model[None] * lap_wave
        wave_prior = inject(wave_prior, src_index, wavelet[:, step], offset)
        adjoint_prior = 2.0 * adjoint - adjoint_later + model[None] * lap_adjoint
        adjoint_prior = inject(adjoint_prior, rec_index, misfit[:, step, :], offset)
        wave_later, wave = (wave, wave_prior)
        adjoint_later, adjoint = (adjoint, adjoint_prior)
    local_image = jnp.sum(image, axis=0)
    gradient = lax.psum(local_image, "shot")
    peak = lax.pmax(jnp.max(jnp.abs(gradient)), "slab")
    new_model = update(model, gradient, peak)
    padded_wave = extended(wave, (("slab", 1),), 1)
    stepped = 2.0 * wave - wave_later + new_model[None] * local_laplace(padded_wave)
    return (new_model, stepped, adjoint)


def solution(mesh):
    in_specs = (
        P(("groups", "slab"), None, None),
        P(("groups", "shot"), "slab", None, None),
        P(("groups", "shot"), "slab", None, None),
        P(("groups", "shot"), "slab", None, None),
        P(("groups", "shot"), "slab", None, None),
        P(("groups", "shot"), None),
        P(("groups", "shot"), None, None),
        P(("groups", "shot")),
        P(("groups", "shot"), None),
    )
    out_specs = (
        P(("groups", "slab"), None, None),
        P(("groups", "shot"), "slab", None, None),
        P(("groups", "shot"), "slab", None, None),
    )
    return jax.shard_map(
        per_device, mesh=mesh, in_specs=in_specs, out_specs=out_specs, check_vma=False
    )
```

profile of v0, /device:TPU:0, one launch (start us, length us, event | category | flops | bytes accessed | tf_op | source)
XLA Modules:
  0.0 168.8 jit_solution(971231168128775817)
XLA Ops:
  9.2 2.4 %collective-permute-start.1 = (f32[2,1,64,128]{3,2,1,0:T(8,128)S(1)}, f32[2,1,64,128]{3,2,1,0:T(8,128)S(1)}, u32[]{:S(2)}, u32[]{:S(2)}) collective-permute-start(f32[2,1,64,128]{3,2,1,0:T(8,128)S(1)} %get-tuple-element.133), channel_id=1, source_target_pairs={{0,1},{1,2},{2,3},{4,5},{5,6},{6,7},{8,9},{9,10},{10,11},{12,13},{... | collective-permute-start | bytes 196616 | tf_op jit(solution)/shard_map/ppermute | solution.py:14
  15.9 1.6 fusion.75
  23.4 1.4 scatter_fusion
  24.8 5.1 %collective-permute-start.3 = (f32[2,1,64,128]{3,2,1,0:T(8,128)S(1)}, f32[2,1,64,128]{3,2,1,0:T(8,128)S(1)}, u32[]{:S(2)}, u32[]{:S(2)}) collective-permute-start(f32[2,1,64,128]{3,2,1,0:T(8,128)S(1)} %get-tuple-element.131), channel_id=1, source_target_pairs={{0,1},{1,2},{2,3},{4,5},{5,6},{6,7},{8,9},{9,10},{10,11},{12,13},{... | collective-permute-start | bytes 196616 | tf_op jit(solution)/shard_map/ppermute | solution.py:14
  29.9 1.3 collective-permute-start.2
  31.8 2.4 %collective-permute-done.2 = f32[2,1,64,128]{3,2,1,0:T(8,128)S(1)} collective-permute-done((f32[2,1,64,128]{3,2,1,0:T(8,128)S(1)}, f32[2,1,64,128]{3,2,1,0:T(8,128)S(1)}, u32[]{:S(2)}, u32[]{:S(2)}) %collective-permute-start.2) | collective-permute-done | bytes 65568 | tf_op jit(solution)/shard_map/ppermute | solution.py:17
  38.0 1.4 scatter_fusion.1
  39.4 4.8 %collective-permute-start.5 = (f32[2,1,64,128]{3,2,1,0:T(8,128)S(1)}, f32[2,1,64,128]{3,2,1,0:T(8,128)S(1)}, u32[]{:S(2)}, u32[]{:S(2)}) collective-permute-start(f32[2,1,64,128]{3,2,1,0:T(8,128)S(1)} %get-tuple-element.129), channel_id=1, source_target_pairs={{0,1},{1,2},{2,3},{4,5},{5,6},{6,7},{8,9},{9,10},{10,11},{12,13},{... | collective-permute-start | bytes 196616 | tf_op jit(solution)/shard_map/ppermute | solution.py:14
  51.0 1.4 scatter_fusion.2
  52.4 4.3 %collective-permute-start.7 = (f32[2,1,64,128]{3,2,1,0:T(8,128)S(1)}, f32[2,1,64,128]{3,2,1,0:T(8,128)S(1)}, u32[]{:S(2)}, u32[]{:S(2)}) collective-permute-start(f32[2,1,64,128]{3,2,1,0:T(8,128)S(1)} %get-tuple-element.127), channel_id=1, source_target_pairs={{0,1},{1,2},{2,3},{4,5},{5,6},{6,7},{8,9},{9,10},{10,11},{12,13},{... | collective-permute-start | bytes 196616 | tf_op jit(solution)/shard_map/ppermute | solution.py:14
  63.6 1.4 scatter_fusion.3
  65.0 4.3 %collective-permute-start.9 = (f32[2,1,64,128]{3,2,1,0:T(8,128)S(1)}, f32[2,1,64,128]{3,2,1,0:T(8,128)S(1)}, u32[]{:S(2)}, u32[]{:S(2)}) collective-permute-start(f32[2,1,64,128]{3,2,1,0:T(8,128)S(1)} %get-tuple-element.125), channel_id=1, source_target_pairs={{0,1},{1,2},{2,3},{4,5},{5,6},{6,7},{8,9},{9,10},{10,11},{12,13},{... | collective-permute-start | bytes 196616 | tf_op jit(solution)/shard_map/ppermute | solution.py:14
  76.2 1.4 scatter_fusion.4
  77.6 4.3 %collective-permute-start.11 = (f32[2,1,64,128]{3,2,1,0:T(8,128)S(1)}, f32[2,1,64,128]{3,2,1,0:T(8,128)S(1)}, u32[]{:S(2)}, u32[]{:S(2)}) collective-permute-start(f32[2,1,64,128]{3,2,1,0:T(8,128)S(1)} %get-tuple-element.123), channel_id=1, source_target_pairs={{0,1},{1,2},{2,3},{4,5},{5,6},{6,7},{8,9},{9,10},{10,11},{12,13},{... | collective-permute-start | bytes 196616 | tf_op jit(solution)/shard_map/ppermute | solution.py:14
  81.9 1.5 collective-permute-start.10
  88.8 1.4 scatter_fusion.5
  90.2 4.3 %collective-permute-start.13 = (f32[2,1,64,128]{3,2,1,0:T(8,128)S(1)}, f32[2,1,64,128]{3,2,1,0:T(8,128)S(1)}, u32[]{:S(2)}, u32[]{:S(2)}) collective-permute-start(f32[2,1,64,128]{3,2,1,0:T(8,128)S(1)} %get-tuple-element.121), channel_id=1, source_target_pairs={{0,1},{1,2},{2,3},{4,5},{5,6},{6,7},{8,9},{9,10},{10,11},{12,13},{... | collective-permute-start | bytes 196616 | tf_op jit(solution)/shard_map/ppermute | solution.py:14
  101.4 1.4 scatter_fusion.6
  102.8 4.3 %collective-permute-start.15 = (f32[2,1,64,128]{3,2,1,0:T(8,128)S(1)}, f32[2,1,64,128]{3,2,1,0:T(8,128)S(1)}, u32[]{:S(2)}, u32[]{:S(2)}) collective-permute-start(f32[2,1,64,128]{3,2,1,0:T(8,128)S(1)} %get-tuple-element.119), channel_id=1, source_target_pairs={{0,1},{1,2},{2,3},{4,5},{5,6},{6,7},{8,9},{9,10},{10,11},{12,13},{... | collective-permute-start | bytes 196616 | tf_op jit(solution)/shard_map/ppermute | solution.py:14
  117.6 4.3 %collective-permute-start.17 = (f32[1,1,64,128]{3,2,1,0:T(8,128)S(1)}, f32[1,1,64,128]{3,2,1,0:T(8,128)S(1)}, u32[]{:S(2)}, u32[]{:S(2)}) collective-permute-start(f32[1,1,64,128]{3,2,1,0:T(8,128)S(1)} %get-tuple-element.135), channel_id=1, source_target_pairs={{0,1},{1,2},{2,3},{4,5},{5,6},{6,7},{8,9},{9,10},{10,11},{12,13},{... | collective-permute-start | bytes 98312 | tf_op jit(solution)/shard_map/ppermute | solution.py:14
  123.2 1.4 scatter_fusion.7
  124.6 27.4 %all-reduce.12.cloned.1.call-done = f32[8,64,128]{2,1,0:T(8,128)} async-done(((f32[8,64,128]{2,1,0:T(8,128)}), f32[8,64,128]{2,1,0:T(8,128)}) %all-reduce.12.cloned.1.call-update) | async-done | bytes 262160 | tf_op jit(solution)/shard_map/psum | solution.py:69
  152.0 1.6 abs_reduce_fusion
  154.0 6.3 %pmax.7 = f32[]{:T(128)} all-reduce(f32[]{:T(128)} %abs_reduce_fusion), channel_id=1, replica_groups=mesh['groups'=2,'shot'=4,'slab'=4] {'slab'}, use_global_device_ids=true, to_apply=%region_10.11 | all-reduce | flops 1 | bytes 8 | tf_op jit(solution)/shard_map/pmax | solution.py:70
  (130 shorter events, 41.6 us)
Async XLA Ops:
  7.2 144.9 %all-reduce.12.cloned.1.call-start = ((), (), s32[]{:S(2)}) async-start(), calls=%async_computation | async-start | bytes 524288 | tf_op jit(solution)/shard_map/psum | solution.py:69
  9.2 9.7 %collective-permute-start.1 = (f32[2,1,64,128]{3,2,1,0:T(8,128)S(1)}, f32[2,1,64,128]{3,2,1,0:T(8,128)S(1)}, u32[]{:S(2)}, u32[]{:S(2)}) collective-permute-start(f32[2,1,64,128]{3,2,1,0:T(8,128)S(1)} %get-tuple-element.133), channel_id=1, source_target_pairs={{0,1},{1,2},{2,3},{4,5},{5,6},{6,7},{8,9},{9,10},{10,11},{12,13},{... | collective-permute-start | bytes 196616 | tf_op jit(solution)/shard_map/ppermute | solution.py:14
  11.6 7.3 %collective-permute-start = (f32[2,1,64,128]{3,2,1,0:T(8,128)S(1)}, f32[2,1,64,128]{3,2,1,0:T(8,128)S(1)}, u32[]{:S(2)}, u32[]{:S(2)}) collective-permute-start(f32[2,1,64,128]{3,2,1,0:T(8,128)S(1)} %get-tuple-element.134), channel_id=1, source_target_pairs={{1,0},{2,1},{3,2},{5,4},{6,5},{7,6},{9,8},{10,9},{11,10},{13,12},{... | collective-permute-start | bytes 196616 | tf_op jit(solution)/shard_map/ppermute | solution.py:17
  24.8 7.0 %collective-permute-start.3 = (f32[2,1,64,128]{3,2,1,0:T(8,128)S(1)}, f32[2,1,64,128]{3,2,1,0:T(8,128)S(1)}, u32[]{:S(2)}, u32[]{:S(2)}) collective-permute-start(f32[2,1,64,128]{3,2,1,0:T(8,128)S(1)} %get-tuple-element.131), channel_id=1, source_target_pairs={{0,1},{1,2},{2,3},{4,5},{5,6},{6,7},{8,9},{9,10},{10,11},{12,13},{... | collective-permute-start | bytes 196616 | tf_op jit(solution)/shard_map/ppermute | solution.py:14
  29.9 4.4 %collective-permute-start.2 = (f32[2,1,64,128]{3,2,1,0:T(8,128)S(1)}, f32[2,1,64,128]{3,2,1,0:T(8,128)S(1)}, u32[]{:S(2)}, u32[]{:S(2)}) collective-permute-start(f32[2,1,64,128]{3,2,1,0:T(8,128)S(1)} %get-tuple-element.132), channel_id=1, source_target_pairs={{1,0},{2,1},{3,2},{5,4},{6,5},{7,6},{9,8},{10,9},{11,10},{13,12},{... | collective-permute-start | bytes 196616 | tf_op jit(solution)/shard_map/ppermute | solution.py:17
  39.4 6.7 %collective-permute-start.5 = (f32[2,1,64,128]{3,2,1,0:T(8,128)S(1)}, f32[2,1,64,128]{3,2,1,0:T(8,128)S(1)}, u32[]{:S(2)}, u32[]{:S(2)}) collective-permute-start(f32[2,1,64,128]{3,2,1,0:T(8,128)S(1)} %get-tuple-element.129), channel_id=1, source_target_pairs={{0,1},{1,2},{2,3},{4,5},{5,6},{6,7},{8,9},{9,10},{10,11},{12,13},{... | collective-permute-start | bytes 196616 | tf_op jit(solution)/shard_map/ppermute | solution.py:14
  44.2 3.1 %collective-permute-start.4 = (f32[2,1,64,128]{3,2,1,0:T(8,128)S(1)}, f32[2,1,64,128]{3,2,1,0:T(8,128)S(1)}, u32[]{:S(2)}, u32[]{:S(2)}) collective-permute-start(f32[2,1,64,128]{3,2,1,0:T(8,128)S(1)} %get-tuple-element.130), channel_id=1, source_target_pairs={{1,0},{2,1},{3,2},{5,4},{6,5},{7,6},{9,8},{10,9},{11,10},{13,12},{... | collective-permute-start | bytes 196616 | tf_op jit(solution)/shard_map/ppermute | solution.py:17
  52.4 6.2 %collective-permute-start.7 = (f32[2,1,64,128]{3,2,1,0:T(8,128)S(1)}, f32[2,1,64,128]{3,2,1,0:T(8,128)S(1)}, u32[]{:S(2)}, u32[]{:S(2)}) collective-permute-start(f32[2,1,64,128]{3,2,1,0:T(8,128)S(1)} %get-tuple-element.127), channel_id=1, source_target_pairs={{0,1},{1,2},{2,3},{4,5},{5,6},{6,7},{8,9},{9,10},{10,11},{12,13},{... | collective-permute-start | bytes 196616 | tf_op jit(solution)/shard_map/ppermute | solution.py:14
  56.7 3.1 %collective-permute-start.6 = (f32[2,1,64,128]{3,2,1,0:T(8,128)S(1)}, f32[2,1,64,128]{3,2,1,0:T(8,128)S(1)}, u32[]{:S(2)}, u32[]{:S(2)}) collective-permute-start(f32[2,1,64,128]{3,2,1,0:T(8,128)S(1)} %get-tuple-element.128), channel_id=1, source_target_pairs={{1,0},{2,1},{3,2},{5,4},{6,5},{7,6},{9,8},{10,9},{11,10},{13,12},{... | collective-permute-start | bytes 196616 | tf_op jit(solution)/shard_map/ppermute | solution.py:17
  65.0 6.3 %collective-permute-start.9 = (f32[2,1,64,128]{3,2,1,0:T(8,128)S(1)}, f32[2,1,64,128]{3,2,1,0:T(8,128)S(1)}, u32[]{:S(2)}, u32[]{:S(2)}) collective-permute-start(f32[2,1,64,128]{3,2,1,0:T(8,128)S(1)} %get-tuple-element.125), channel_id=1, source_target_pairs={{0,1},{1,2},{2,3},{4,5},{5,6},{6,7},{8,9},{9,10},{10,11},{12,13},{... | collective-permute-start | bytes 196616 | tf_op jit(solution)/shard_map/ppermute | solution.py:14
  69.3 3.1 %collective-permute-start.8 = (f32[2,1,64,128]{3,2,1,0:T(8,128)S(1)}, f32[2,1,64,128]{3,2,1,0:T(8,128)S(1)}, u32[]{:S(2)}, u32[]{:S(2)}) collective-permute-start(f32[2,1,64,128]{3,2,1,0:T(8,128)S(1)} %get-tuple-element.126), channel_id=1, source_target_pairs={{1,0},{2,1},{3,2},{5,4},{6,5},{7,6},{9,8},{10,9},{11,10},{13,12},{... | collective-permute-start | bytes 196616 | tf_op jit(solution)/shard_map/ppermute | solution.py:17
  77.6 6.5 %collective-permute-start.11 = (f32[2,1,64,128]{3,2,1,0:T(8,128)S(1)}, f32[2,1,64,128]{3,2,1,0:T(8,128)S(1)}, u32[]{:S(2)}, u32[]{:S(2)}) collective-permute-start(f32[2,1,64,128]{3,2,1,0:T(8,128)S(1)} %get-tuple-element.123), channel_id=1, source_target_pairs={{0,1},{1,2},{2,3},{4,5},{5,6},{6,7},{8,9},{9,10},{10,11},{12,13},{... | collective-permute-start | bytes 196616 | tf_op jit(solution)/shard_map/ppermute | solution.py:14
  81.9 3.1 %collective-permute-start.10 = (f32[2,1,64,128]{3,2,1,0:T(8,128)S(1)}, f32[2,1,64,128]{3,2,1,0:T(8,128)S(1)}, u32[]{:S(2)}, u32[]{:S(2)}) collective-permute-start(f32[2,1,64,128]{3,2,1,0:T(8,128)S(1)} %get-tuple-element.124), channel_id=1, source_target_pairs={{1,0},{2,1},{3,2},{5,4},{6,5},{7,6},{9,8},{10,9},{11,10},{13,12},{... | collective-permute-start | bytes 196616 | tf_op jit(solution)/shard_map/ppermute | solution.py:17
  90.2 6.3 %collective-permute-start.13 = (f32[2,1,64,128]{3,2,1,0:T(8,128)S(1)}, f32[2,1,64,128]{3,2,1,0:T(8,128)S(1)}, u32[]{:S(2)}, u32[]{:S(2)}) collective-permute-start(f32[2,1,64,128]{3,2,1,0:T(8,128)S(1)} %get-tuple-element.121), channel_id=1, source_target_pairs={{0,1},{1,2},{2,3},{4,5},{5,6},{6,7},{8,9},{9,10},{10,11},{12,13},{... | collective-permute-start | bytes 196616 | tf_op jit(solution)/shard_map/ppermute | solution.py:14
  94.5 3.1 %collective-permute-start.12 = (f32[2,1,64,128]{3,2,1,0:T(8,128)S(1)}, f32[2,1,64,128]{3,2,1,0:T(8,128)S(1)}, u32[]{:S(2)}, u32[]{:S(2)}) collective-permute-start(f32[2,1,64,128]{3,2,1,0:T(8,128)S(1)} %get-tuple-element.122), channel_id=1, source_target_pairs={{1,0},{2,1},{3,2},{5,4},{6,5},{7,6},{9,8},{10,9},{11,10},{13,12},{... | collective-permute-start | bytes 196616 | tf_op jit(solution)/shard_map/ppermute | solution.py:17
  102.8 6.3 %collective-permute-start.15 = (f32[2,1,64,128]{3,2,1,0:T(8,128)S(1)}, f32[2,1,64,128]{3,2,1,0:T(8,128)S(1)}, u32[]{:S(2)}, u32[]{:S(2)}) collective-permute-start(f32[2,1,64,128]{3,2,1,0:T(8,128)S(1)} %get-tuple-element.119), channel_id=1, source_target_pairs={{0,1},{1,2},{2,3},{4,5},{5,6},{6,7},{8,9},{9,10},{10,11},{12,13},{... | collective-permute-start | bytes 196616 | tf_op jit(solution)/shard_map/ppermute | solution.py:14
  107.1 3.1 %collective-permute-start.14 = (f32[2,1,64,128]{3,2,1,0:T(8,128)S(1)}, f32[2,1,64,128]{3,2,1,0:T(8,128)S(1)}, u32[]{:S(2)}, u32[]{:S(2)}) collective-permute-start(f32[2,1,64,128]{3,2,1,0:T(8,128)S(1)} %get-tuple-element.120), channel_id=1, source_target_pairs={{1,0},{2,1},{3,2},{5,4},{6,5},{7,6},{9,8},{10,9},{11,10},{13,12},{... | collective-permute-start | bytes 196616 | tf_op jit(solution)/shard_map/ppermute | solution.py:17
  110.8 1.5 copy-start.10
  110.8 1.7 copy-start.12
  110.8 1.8 %copy-start.14 = (f32[2,8,64,128]{3,2,1,0:T(8,128)S(1)}, f32[2,8,64,128]{3,2,1,0:T(8,128)}, u32[]{:S(2)}) copy-start(f32[2,8,64,128]{3,2,1,0:T(8,128)} %copy-done.13) | copy-start | bytes 1572868
  117.6 36.1 %collective-permute-start.17 = (f32[1,1,64,128]{3,2,1,0:T(8,128)S(1)}, f32[1,1,64,128]{3,2,1,0:T(8,128)S(1)}, u32[]{:S(2)}, u32[]{:S(2)}) collective-permute-start(f32[1,1,64,128]{3,2,1,0:T(8,128)S(1)} %get-tuple-element.135), channel_id=1, source_target_pairs={{0,1},{1,2},{2,3},{4,5},{5,6},{6,7},{8,9},{9,10},{10,11},{12,13},{... | collective-permute-start | bytes 98312 | tf_op jit(solution)/shard_map/ppermute | solution.py:14
  121.9 31.8 %collective-permute-start.16 = (f32[1,1,64,128]{3,2,1,0:T(8,128)S(1)}, f32[1,1,64,128]{3,2,1,0:T(8,128)S(1)}, u32[]{:S(2)}, u32[]{:S(2)}) collective-permute-start(f32[1,1,64,128]{3,2,1,0:T(8,128)S(1)} %get-tuple-element.136), channel_id=1, source_target_pairs={{1,0},{2,1},{3,2},{5,4},{6,5},{7,6},{9,8},{10,9},{11,10},{13,12},{... | collective-permute-start | bytes 98312 | tf_op jit(solution)/shard_map/ppermute | solution.py:17
  124.6 37.4 %copy-start.18 = (f32[65536]{0:T(1024)}, f32[65536]{0:T(1024)S(1)}, u32[]{:S(2)}) copy-start(f32[65536]{0:T(1024)S(1)} %scatter_fusion.7) | copy-start | bytes 786436
  152.0 8.9 %copy-start.19 = (f32[8,64,128]{2,1,0:T(8,128)S(1)}, f32[8,64,128]{2,1,0:T(8,128)}, u32[]{:S(2)}) copy-start(f32[8,64,128]{2,1,0:T(8,128)} %all-reduce.12.cloned.1.call-done) | copy-start | bytes 786436
  (17 other events, 17.0 us)
Sparse Core Ops, SparseCore 0:
  113.9 38.0 all-reduce.11
where the time goes:
time: 170 us; the launch traced here: 169 us
  starting transfers between devices  49.9 us (29%)
  waiting for transfers between devices  36.9 us (22%)
  between operations  36 us (21%)
  other arithmetic  33 us (19%)
  local copies, waits for them, and re-layouts  6.66 us (4%)
  blocking collectives  6.3 us (4%)
    ppermute x9, starting transfers between devices, extended(): lax.ppermute(lax.slice_in_dim(block, block.shape[dim] - width, None, axis...  38 us
    psum x1, waiting for transfers between devices, per_device(): gradient = lax.psum(local_image, 'shot')  27.4 us
    ppermute x9, starting transfers between devices, extended(): lax.ppermute(lax.slice_in_dim(block, 0, width, axis=dim), axis, backward)  11.8 us
    scatter-add x8, other arithmetic, inject(): flat = flat.at[rows, local].add(jnp.where(valid, values, 0.0))  11 us
    ppermute x9, waiting for transfers between devices, extended(): lax.ppermute(lax.slice_in_dim(block, 0, width, axis=dim), axis, backward)  9.5 us
    pmax x1, blocking collectives, per_device(): peak = lax.pmax(jnp.max(jnp.abs(gradient)), 'slab')  6.3 us
    add x8, other arithmetic, inject(): flat = flat.at[rows, local].add(jnp.where(valid, values, 0.0))  5.13 us
    sub x8, other arithmetic, local_laplace(): return beside - 6.0 * center  4.02 us
  transfers between devices with their start and end apart: 19, of which 8 were waited for; matrix products, arithmetic and copies ran while one was open for 6% of the time, Pallas kernels for 0%

commit v1 on v0

v1 whole, which is shorter than its diff:
```python
import functools

import jax
import jax.numpy as jnp
from jax import lax
from jax.experimental import pallas as pl
from jax.experimental.pallas import tpu as pltpu
from jax.sharding import PartitionSpec as P

ITERS = 8
GUARD = 8
LANES = 128
VMEM = pltpu.VMEM
SMEM = pltpu.SMEM
HBM = pl.ANY


def pairs(count, start):
    low = [(i, i + 1) for i in range(start, count - 1, 2)]
    return low + [(b, a) for a, b in low]


def partner_perms(count):
    if count & (count - 1) == 0:
        return [[(i, i ^ m) for i in range(count)] for m in range(1, count)]
    return [[(i, (i + m) % count) for i in range(count)] for m in range(1, count)]


def send_slot(me, m, count):
    return me ^ m if count & (count - 1) == 0 else lax.rem(me + m, count)


def from_slot(me, m, count):
    return me ^ m if count & (count - 1) == 0 else lax.rem(me - m + count, count)


def spec(space):
    return pl.BlockSpec(memory_space=space)


def cost(flops, nbytes):
    return pl.CostEstimate(flops=int(flops), bytes_accessed=int(nbytes), transcendentals=0)


def inject_kernel(depth, width, meta, rec_ref, misfit_ref, out_ref, left, right):
    rows = left.shape[0]
    index = rec_ref[...] - (meta[0] - depth) * (width * LANES)
    row_of = index // LANES
    row_of = jnp.where(index < 0, -1, row_of)
    lane_of = index - row_of * LANES
    group = 2 * width
    for first in range(0, rows, group):
        at = lax.broadcasted_iota(jnp.int32, (group, LANES), 0) + first
        hot = jnp.where(at == row_of, 1.0, 0.0).astype(jnp.bfloat16)
        for part in range(3):
            left[pl.ds(first, group), pl.ds(part * LANES, LANES)] = hot
    lane = lax.broadcasted_iota(jnp.int32, (LANES, LANES), 0)
    mine = lane == lane_of
    for k in range(ITERS):
        value = misfit_ref[pl.ds(k, 1), :]
        for part in range(3):
            piece = value.astype(jnp.bfloat16).astype(jnp.float32)
            value = value - piece
            right[pl.ds(k * LANES, LANES), pl.ds(part * LANES, LANES)] = jnp.where(
                mine, piece, 0.0
            ).astype(jnp.bfloat16)

    def pair(j, carry):
        cols = right[pl.ds(pl.multiple_of(j * 2 * LANES, 2 * LANES), 2 * LANES), :]
        both = lax.dot_general(
            left[...], cols, (((1,), (1,)), ((), ())), preferred_element_type=jnp.float32
        )
        out_ref[2 * j] = both[:, :LANES].reshape(out_ref.shape[1:])
        out_ref[2 * j + 1] = both[:, LANES:].reshape(out_ref.shape[1:])
        return carry

    lax.fori_loop(0, ITERS // 2, pair, 0)


def lap_block(src, p, r, first, last):
    c = src[p, pl.ds(r, 8), :]
    s = src[p + 1, pl.ds(r, 8), :] + src[p - 1, pl.ds(r, 8), :]
    s = s + src[p, pl.ds(r + 1, 8), :]
    s = s + src[p, pl.ds(r - 1, 8), :]
    s = s + jnp.where(last, 0.0, pltpu.roll(c, LANES - 1, 1))
    s = s + jnp.where(first, 0.0, pltpu.roll(c, 1, 1))
    return c, s - 6.0 * c


def load_field(depth, width, even, now, later, a_in, b_in, at_now, at_later, cur, old, sem):
    rows = pl.ds(GUARD, width)
    out = []

    def own(src, dst, i):
        c = pltpu.make_async_copy(src, dst.at[pl.ds(depth, depth), rows], sem.at[i])
        c.start()
        out.append(c)

    own(now, cur, 0)
    own(later, old, 1)

    def halo(low, high, i):
        n = depth - 1
        for j, (src, dst, off, size, where) in enumerate(
            (
                (low, cur, at_now, depth, 0),
                (low, old, at_later, n, 1),
                (high, cur, at_now, depth, 2 * depth),
                (high, old, at_later, n, 2 * depth),
            )
        ):
            pltpu.make_async_copy(
                src.at[pl.ds(off, size)], dst.at[pl.ds(where, size), rows], sem.at[i + j]
            ).start()

    @pl.when(even)
    def _():
        halo(b_in, a_in, 2)

    @pl.when(jnp.logical_not(even))
    def _():
        halo(a_in, b_in, 2)

    n = depth - 1
    for j, (dst, size, where) in enumerate(
        ((cur, depth, 0), (old, n, 1), (cur, depth, 2 * depth), (old, n, 2 * depth))
    ):
        out.append(
            pltpu.make_async_copy(
                a_in.at[pl.ds(0, size)], dst.at[pl.ds(where, size), rows], sem.at[2 + j]
            )
        )
    return out


def load_model(depth, even, model, a_in, b_in, at, mod, sem):
    n = depth - 1
    own = pltpu.make_async_copy(model, mod.at[pl.ds(depth, depth)], sem.at[6])
    own.start()

    def halo(low, high):
        pltpu.make_async_copy(low.at[pl.ds(at, n)], mod.at[pl.ds(1, n)], sem.at[7]).start()
        pltpu.make_async_copy(high.at[pl.ds(at, n)], mod.at[pl.ds(2 * depth, n)], sem.at[8]).start()

    @pl.when(even)
    def _():
        halo(b_in, a_in)

    @pl.when(jnp.logical_not(even))
    def _():
        halo(a_in, b_in)

    return [
        own,
        pltpu.make_async_copy(a_in.at[pl.ds(at, n)], mod.at[pl.ds(1, n)], sem.at[7]),
        pltpu.make_async_copy(a_in.at[pl.ds(at, n)], mod.at[pl.ds(2 * depth, n)], sem.at[8]),
    ]


def clear_guards(field):
    planes, rows, _ = field.shape

    def one(p, carry):
        field[p, pl.ds(0, GUARD), :] = jnp.zeros((GUARD, LANES), jnp.float32)
        field[p, pl.ds(rows - GUARD, GUARD), :] = jnp.zeros((GUARD, LANES), jnp.float32)
        return carry

    lax.fori_loop(0, planes, one, 0)


def forward_kernel(
    depth, width, meta, wavelet, src_index, model, now, later, a_in, b_in,
    last_out, base_out, lap_out, a_edge, b_edge,
    cur, old, mod, sem,
):
    even = meta[1] == 0
    waits = load_field(depth, width, even, now, later, a_in, b_in, 0, depth, cur, old, sem)
    waits += load_model(depth, even, model, a_in, b_in, 2 * depth - 1, mod, sem)
    clear_guards(cur)
    clear_guards(old)
    for w in waits:
        w.wait()
    lane = lax.broadcasted_iota(jnp.int32, (8, LANES), 1)
    first, last = lane == 0, lane == LANES - 1
    source = src_index[0] - (meta[0] - depth) * (width * LANES)
    src_row = jnp.maximum(source, 0) // LANES
    src_plane = jnp.where(source < 0, -1, src_row // width)
    src_y = lax.rem(src_row, width)
    src_lane = lax.rem(jnp.maximum(source, 0), LANES)
    bufs = (cur, old)
    for k in range(ITERS):
        s, d = bufs[k % 2], bufs[(k + 1) % 2]

        def plane(p, carry, keep):
            for r in range(0, width, 8):
                c, lap = lap_block(s, p, GUARD + r, first, last)
                here = (p, pl.ds(GUARD + r, 8), slice(None))
                d[here] = 2.0 * c - d[here] + mod[p, pl.ds(r, 8), :] * lap
                if keep:
                    lap_out[k, p - depth, pl.ds(r, 8), :] = lap
            return carry

        low, high = k + 1, 3 * depth - 1 - k
        lax.fori_loop(low, depth, functools.partial(plane, keep=False), 0)
        lax.fori_loop(depth, 2 * depth, functools.partial(plane, keep=True), 0)
        lax.fori_loop(2 * depth, high, functools.partial(plane, keep=False), 0)

        @pl.when((src_plane >= low) & (src_plane < high))
        def _():
            here = (src_plane, pl.ds(GUARD + src_y, 1), slice(None))
            at = lax.broadcasted_iota(jnp.int32, (1, LANES), 1) == src_lane
            d[here] = d[here] + jnp.where(at, wavelet[0, k], 0.0)

    u, u_later = bufs[ITERS % 2], bufs[(ITERS + 1) % 2]
    rows = pl.ds(GUARD, width)

    def finish(p, carry):
        c = u[depth + p, rows, :]
        last_out[p] = c
        base_out[p] = 2.0 * c - u_later[depth + p, rows, :]
        return carry

    lax.fori_loop(0, depth, finish, 0)
    a_edge[0] = u[jnp.where(even, 2 * depth - 1, depth), rows, :]
    b_edge[0] = u[jnp.where(even, depth, 2 * depth - 1), rows, :]


def adjoint_kernel(
    depth, width, shots, meta, model, now, later, fa_in, fb_in, a_in, b_in, laps, extra,
    last_out, *rest,
):
    pieces = rest[:shots]
    image, cur, old, mod, sem = rest[shots:]
    even = meta[1] == 0
    waits = load_field(depth, width, even, now, later, a_in, b_in, 0, depth, cur, old, sem)
    waits += load_model(depth, even, model, fa_in, fb_in, 2 * depth - 1, mod, sem)
    clear_guards(cur)
    clear_guards(old)
    for w in waits:
        w.wait()
    lane = lax.broadcasted_iota(jnp.int32, (8, LANES), 1)
    first, last = lane == 0, lane == LANES - 1
    bufs = (cur, old)
    for k in range(ITERS):
        s, d = bufs[k % 2], bufs[(k + 1) % 2]

        def plane(p, carry, keep):
            for r in range(0, width, 8):
                c, lap = lap_block(s, p, GUARD + r, first, last)
                here = (p, pl.ds(GUARD + r, 8), slice(None))
                rows = pl.ds(r, 8)
                new = 2.0 * c - d[here] + mod[p, rows, :] * lap
                d[here] = new + extra[k, p, rows, :]
                if keep:
                    q = p - depth
                    add = c * laps[k, q, rows, :]
                    into = pl.ds(pl.multiple_of(q * width + r, 8), 8)
                    image[into, :] = add if k == 0 else image[into, :] + add
            return carry

        low, high = k + 1, 3 * depth - 1 - k
        lax.fori_loop(low, depth, functools.partial(plane, keep=False), 0)
        lax.fori_loop(depth, 2 * depth, functools.partial(plane, keep=True), 0)
        lax.fori_loop(2 * depth, high, functools.partial(plane, keep=False), 0)

    a = bufs[ITERS % 2]

    def finish(p, carry):
        last_out[p] = a[depth + p, pl.ds(GUARD, width), :]
        return carry

    lax.fori_loop(0, depth, finish, 0)
    n = depth * width // shots
    for m in range(shots):
        to = meta[2] if m == 0 else send_slot(meta[2], m, shots)
        pieces[m][...] = image[pl.ds(pl.multiple_of(to * n, n), n), :]


def sum_kernel(*refs):
    *parts, grad, top = refs
    total = parts[0][...]
    for part in parts[1:]:
        total = total + part[...]
    grad[...] = total
    top[...] = jnp.broadcast_to(jnp.max(jnp.abs(total)), top.shape)


def final_kernel(depth, width, shots, meta, *refs):
    n = depth * width // shots
    grads = refs[:shots]
    tops, model, u, base, a_edge, b_edge, new_model, stepped, pad, grad = refs[shots:]
    even = meta[1] == 0
    rows = pl.ds(GUARD, width)
    clear_guards(pad)
    low, high = jnp.where(even, 0, depth + 1), jnp.where(even, depth + 1, 0)
    pad[low, rows, :] = b_edge[0]
    pad[high, rows, :] = a_edge[0]

    def place(p, carry):
        pad[p + 1, rows, :] = u[p]
        return carry

    lax.fori_loop(0, depth, place, 0)
    for m in range(shots):
        owner = meta[2] if m == 0 else from_slot(meta[2], m, shots)
        grad[pl.ds(pl.multiple_of(owner * n, n), n), :] = grads[m][...]
    peak = jnp.max(tops[...])
    lane = lax.broadcasted_iota(jnp.int32, (8, LANES), 1)
    first, last = lane == 0, lane == LANES - 1

    def plane(p, carry):
        for r in range(0, width, 8):
            g = grad[pl.ds(pl.multiple_of(p * width + r, 8), 8), :]
            new = jnp.clip(model[p, pl.ds(r, 8), :] - 0.1 * g / (peak + 1e-06), 0.05, 0.3)
            new_model[p, pl.ds(r, 8), :] = new
            _, lap = lap_block(pad, p + 1, GUARD + r, first, last)
            stepped[p, pl.ds(r, 8), :] = base[p, pl.ds(r, 8), :] + new * lap
        return carry

    lax.fori_loop(0, depth, plane, 0)


def per_device(model, fwd_now, fwd_next, adj_now, adj_next, wavelet, misfit, src_index, rec_index):
    f32 = jnp.float32
    depth, width, length = model.shape
    assert length == LANES and fwd_now.shape[0] == 1 and width % 8 == 0
    u0, u1, a0, a1 = fwd_now[0], fwd_next[0], adj_now[0], adj_next[0]
    slabs, shots = lax.axis_size("slab"), lax.axis_size("shot")
    slab, shot = lax.axis_index("slab"), lax.axis_index("shot")
    parity = lax.rem(slab, 2)
    meta = jnp.stack([slab * depth, parity, shot]).astype(jnp.int32)
    perm_a, perm_b = pairs(slabs, 0), pairs(slabs, 1)

    def short(x, up):
        return lax.dynamic_slice_in_dim(x, up, depth - 1, 0)

    def packed(fields, up):
        return jnp.concatenate([fields[0]] + [short(x, up) for x in fields[1:]], axis=0)

    fb = lax.ppermute(packed((u0, u1, model), parity), "slab", perm_b)
    fa = lax.ppermute(packed((u0, u1, model), 1 - parity), "slab", perm_a)
    gb = lax.ppermute(packed((a0, a1), parity), "slab", perm_b)
    ga = lax.ppermute(packed((a0, a1), 1 - parity), "slab", perm_a)

    plane = (depth, width, LANES)
    planes = 3 * depth
    shape = jax.ShapeDtypeStruct
    extra = pl.pallas_call(
        functools.partial(inject_kernel, depth, width),
        out_shape=shape((ITERS, planes, width, LANES), f32),
        in_specs=[spec(SMEM), spec(VMEM), spec(VMEM)],
        out_specs=spec(VMEM),
        scratch_shapes=[
            VMEM((planes * width, 3 * LANES), jnp.bfloat16),
            VMEM((ITERS * LANES, 3 * LANES), jnp.bfloat16),
        ],
        cost_estimate=cost(2 * planes * width * 3 * LANES * ITERS * LANES, 4 * ITERS * planes * width * LANES),
        name="inject",
    )(meta, rec_index, misfit[0])

    def work():
        field = (planes, width + 2 * GUARD, LANES)
        return [VMEM(field, f32), VMEM(field, f32), VMEM((planes, width, LANES), f32), pltpu.SemaphoreType.DMA((9,))]

    cells = depth * width * LANES
    u, base, laps, a_edge, b_edge = pl.pallas_call(
        functools.partial(forward_kernel, depth, width),
        out_shape=[
            shape(plane, f32), shape(plane, f32), shape((ITERS, *plane), f32),
            shape((1, width, LANES), f32), shape((1, width, LANES), f32),
        ],
        in_specs=[spec(SMEM)] * 3 + [spec(HBM)] * 5,
        out_specs=[spec(VMEM)] * 5,
        scratch_shapes=work(),
        cost_estimate=cost(15 * ITERS * 2 * cells, 4 * cells * 20),
        name="forward",
    )(meta, wavelet, src_index, model, u0, u1, fa, fb)

    a_edge = lax.ppermute(a_edge, "slab", perm_a)
    b_edge = lax.ppermute(b_edge, "slab", perm_b)

    n = depth * width // shots
    a, *pieces = pl.pallas_call(
        functools.partial(adjoint_kernel, depth, width, shots),
        out_shape=[shape(plane, f32)] + [shape((n, LANES), f32)] * shots,
        in_specs=[spec(SMEM)] + [spec(HBM)] * 7 + [spec(VMEM)] * 2,
        out_specs=[spec(VMEM)] * (1 + shots),
        scratch_shapes=[VMEM((depth * width, LANES), f32), *work()],
        cost_estimate=cost(18 * ITERS * 2 * cells, 4 * cells * 40),
        name="adjoint",
    )(meta, model, a0, a1, fa, fb, ga, gb, laps, extra)

    perms = partner_perms(shots)
    parts = [pieces[0]] + [lax.ppermute(x, "shot", q) for x, q in zip(pieces[1:], perms)]
    grad, top = pl.pallas_call(
        sum_kernel,
        out_shape=[shape((n, LANES), f32), shape((8, LANES), f32)],
        in_specs=[spec(VMEM)] * shots,
        out_specs=[spec(VMEM)] * 2,
        cost_estimate=cost(shots * n * LANES, 4 * shots * n * LANES),
        name="total",
    )(*parts)
    grads = [grad] + [lax.ppermute(grad, "shot", q) for q in perms]
    tops = [top] + [lax.ppermute(top, "slab", q) for q in partner_perms(slabs)]
    top = functools.reduce(jnp.maximum, tops)
    tops = jnp.concatenate([top] + [lax.ppermute(top, "shot", q) for q in perms], axis=0)

    new_model, stepped = pl.pallas_call(
        functools.partial(final_kernel, depth, width, shots),
        out_shape=[shape(plane, f32), shape(plane, f32)],
        in_specs=[spec(SMEM)] + [spec(VMEM)] * (shots + 6),
        out_specs=[spec(VMEM)] * 2,
        scratch_shapes=[VMEM((depth + 2, width + 2 * GUARD, LANES), f32), VMEM((depth * width, LANES), f32)],
        cost_estimate=cost(20 * cells, 4 * 6 * cells),
        name="update",
    )(meta, *grads, tops, model, u, base, a_edge, b_edge)
    return new_model, stepped[None], a[None]


def solution(mesh):
    in_specs = (
        P(("groups", "slab"), None, None),
        P(("groups", "shot"), "slab", None, None),
        P(("groups", "shot"), "slab", None, None),
        P(("groups", "shot"), "slab", None, None),
        P(("groups", "shot"), "slab", None, None),
        P(("groups", "shot"), None),
        P(("groups", "shot"), None, None),
        P(("groups", "shot")),
        P(("groups", "shot"), None),
    )
    out_specs = (
        P(("groups", "slab"), None, None),
        P(("groups", "shot"), "slab", None, None),
        P(("groups", "shot"), "slab", None, None),
    )
    return jax.shard_map(
        per_device, mesh=mesh, in_specs=in_specs, out_specs=out_specs, check_vma=False
    )
```

time: 170 us -> 91.4 us (0.54)
  Pallas kernels: 0 us -> 42.6 us
  between operations: 36 us -> 1.46 us
  other arithmetic: 33 us -> 5.04 us
  starting transfers between devices: 49.9 us -> 22.8 us
  waiting for transfers between devices: 36.9 us -> 13.3 us
  blocking collectives: 6.3 us -> 0 us
    pallas_call x0 -> x5, Pallas kernels: none -> 42.6 us  [the longest x1 17 us: per_device(): pl.pallas_call(functools.partial(adjoint_kernel, depth, width, shots), ou...]
    psum x1 -> x0, waiting for transfers between devices: 27.4 us -> none  [per_device(): gradient = lax.psum(local_image, 'shot')]
    ppermute x18, starting transfers between devices: 49.8 us -> 22.8 us  [the longest x3 4.45 us: per_device(): lax.ppermute(x, 'shot', q)]
    scatter-add x8 -> x0, other arithmetic: 11 us -> none  [inject(): flat = flat.at[rows, local].add(jnp.where(valid, values, 0.0))]
    add x18 -> x0, other arithmetic: 9.38 us -> none  [the longest x8 5.13 us: inject(): flat = flat.at[rows, local].add(jnp.where(valid, values, 0.0))]
    pmax x1 -> x0, blocking collectives: 6.3 us -> none  [per_device(): peak = lax.pmax(jnp.max(jnp.abs(gradient)), 'slab')]
    sub x8 -> x0, other arithmetic: 4.02 us -> none  [local_laplace(): return beside - 6.0 * center]
    ppermute x18, waiting for transfers between devices: 9.52 us -> 13.3 us  [the longest x3 6.16 us: per_device(): lax.ppermute(x, 'shot', q)]
  transfers between devices with their start and end apart: 19 -> 18, of which waited for: 8 -> 8; matrix products, arithmetic and copies ran while one was open for 6% -> 4% of each run, Pallas kernels for 0% -> 23%
where the time goes in v1:
time: 91.4 us; the launch traced here: 90.9 us
  Pallas kernels  42.6 us (47%)
  starting transfers between devices  22.8 us (25%)
  waiting for transfers between devices  13.3 us (15%)
  local copies, waits for them, and re-layouts  5.63 us (6%)
  other arithmetic  5.04 us (6%)
  between operations  1.46 us (2%)
    pallas_call x1, Pallas kernels, per_device(): pl.pallas_call(functools.partial(adjoint_kernel, depth, width, shots), ou...  17 us
    pallas_call x1, Pallas kernels, per_device(): pl.pallas_call(functools.partial(forward_kernel, depth, width), out_shape...  15 us
    ppermute x3, waiting for transfers between devices, per_device(): lax.ppermute(x, 'shot', q)  6.16 us
    pallas_call x1, Pallas kernels, per_device(): pl.pallas_call(functools.partial(inject_kernel, depth, width), out_shape=...  6.01 us
    ppermute x3, waiting for transfers between devices, per_device(): grads = [grad] + [lax.ppermute(grad, 'shot', q) for q in perms]  4.86 us
    ppermute x3, starting transfers between devices, per_device(): lax.ppermute(x, 'shot', q)  4.45 us
    ppermute x3, starting transfers between devices, per_device(): grads = [grad] + [lax.ppermute(grad, 'shot', q) for q in perms]  4.39 us
    ppermute x3, starting transfers between devices, per_device(): lax.ppermute(top, 'shot', q)  4.39 us
  transfers between devices with their start and end apart: 18, of which 8 were waited for; matrix products, arithmetic and copies ran while one was open for 4% of the time, Pallas kernels for 23%

profile of v1, /device:TPU:0, one launch (start us, length us, event | category | flops | bytes accessed | tf_op | source)
XLA Modules:
  0.0 90.9 jit_solution(2879231753599873292)
XLA Ops:
  0.6 1.1 %constant_dynamic-slice_fusion = (f32[7,64,128]{2,1,0:T(8,128)S(1)}, f32[7,64,128]{2,1,0:T(8,128)S(1)}) fusion(f32[8,64,128]{2,1,0:T(8,128)} %refs_5_.1, s32[]{:T(128)S(6)} %select_n.5, s32[]{:T(128)S(6)} %select_n.4), kind=kLoop, calls=%fused_computation.12 | loop fusion | bytes 917512 | tf_op jit(solution)/shard_map/dynamic_slice | solution.py:335
  1.7 1.4 %dynamic-slice_bitcast_fusion = (f32[7,64,128]{2,1,0:T(8,128)S(1)}, f32[7,64,128]{2,1,0:T(8,128)S(1)}, f32[7,64,128]{2,1,0:T(8,128)S(1)}, f32[7,64,128]{2,1,0:T(8,128)S(1)}) fusion(f32[1,8,64,128]{3,2,1,0:T(8,128)} %param.13, s32[]{:T(128)S(6)} %select_n.5, s32[]{:T(128)S(6)} %select_n.4, f32[1,8,64,128]{3,2,1,0:T(8,128)} %param.11), kind=kLoop, calls=%fused_computation.6 | loop fusion | bytes 1835016 | tf_op jit(solution)/shard_map/dynamic_slice | solution.py:335
  3.1 1.2 %fusion.1 = (f32[22,64,128]{2,1,0:T(8,128)S(1)}, f32[22,64,128]{2,1,0:T(8,128)S(1)}) fusion(f32[8,64,128]{2,1,0:T(8,128)} %bitcast.20, f32[7,64,128]{2,1,0:T(8,128)S(1)} %get-tuple-element.39, f32[7,64,128]{2,1,0:T(8,128)S(1)} %get-tuple-element.42, f32[7,64,128]{2,1,0:T(8,128)S(1)} %get-tuple-element.40, f32[7,64,128]{2,1,0:T(8,128)S(1)} %get-tuple-element.41), kind=kLoop, calls=%fused_computation.3 | loop fusion | flops 720896 | bytes 2621440 | tf_op jit(solution)/shard_map/concatenate | solution.py:338
  5.0 4.3 %collective-permute-start = (f32[22,64,128]{2,1,0:T(8,128)S(1)}, f32[22,64,128]{2,1,0:T(8,128)S(1)}, u32[]{:S(2)}, u32[]{:S(2)}) collective-permute-start(f32[22,64,128]{2,1,0:T(8,128)S(1)} %get-tuple-element.36), channel_id=1, source_target_pairs={{0,1},{2,3},{1,0},{3,2},{4,5},{6,7},{5,4},{7,6},{8,9},{10,11},{9,8... | collective-permute-start | bytes 2162696 | tf_op jit(solution)/shard_map/ppermute | solution.py:341
  9.3 2.0 %pad_maximum_fusion.2 = (f32[15,64,128]{2,1,0:T(8,128)}, f32[15,64,128]{2,1,0:T(8,128)}) fusion(f32[8,64,128]{2,1,0:T(8,128)} %bitcast.22, f32[7,64,128]{2,1,0:T(8,128)S(1)} %get-tuple-element.33, f32[7,64,128]{2,1,0:T(8,128)S(1)} %get-tuple-element.34), kind=kLoop, calls=%fused_computation.4 | loop fusion | flops 245760 | bytes 1703936 | tf_op jit(solution)/shard_map/concatenate | solution.py:338
  12.0 1.3 %collective-permute-start.2 = (f32[15,64,128]{2,1,0:T(8,128)}, f32[15,64,128]{2,1,0:T(8,128)}, u32[]{:S(2)}, u32[]{:S(2)}) collective-permute-start(f32[15,64,128]{2,1,0:T(8,128)} %get-tuple-element.32), channel_id=1, source_target_pairs={{0,1},{2,3},{1,0},{3,2},{4,5},{6,7},{5,4},{7,6},{8,9},{10,11},{9,8... | collective-permute-start | bytes 1474568 | tf_op jit(solution)/shard_map/ppermute | solution.py:343
  14.6 6.0 %inject.1.extra = f32[8,24,64,128]{3,2,1,0:T(8,128)} custom-call(s32[3]{0:T(128)} %pad_add_fusion.meta, s32[1,128]{1,0:T(1,128)} %rec_ref.1, f32[8,128]{1,0:T(8,128)} %bitcast.24), custom_call_target="tpu_custom_call" | custom-call | flops 1207959552 | bytes 6291456 | tf_op jit(solution)/shard_map/inject/pallas_call | solution.py:348
  20.6 0.9 copy-done
  21.8 15.0 %forward.1 = (f32[8,64,128]{2,1,0:T(8,128)}, f32[8,64,128]{2,1,0:T(8,128)}, f32[8,8,64,128]{3,2,1,0:T(8,128)}, f32[1,64,128]{2,1,0:T(8,128)}, f32[1,64,128]{2,1,0:T(8,128)}) custom-call(s32[3]{0:T(128)} %pad_add_fusion.meta, f32[1,8]{1,0:T(1,128)} %wavelet.1, s32[1]{0:T(128)S(6)} %copy.12.src_index, f32[8,64,128]{2,1,0:T(8,128)} %refs_5_.1, ...), custom_call_target="tpu_custom_call" | custom-call | flops 15728640 | bytes 5242880 | tf_op jit(solution)/shard_map/forward/pallas_call | solution.py:366
  37.6 17.0 %adjoint.1 = (f32[8,64,128]{2,1,0:T(8,128)}, f32[128,128]{1,0:T(8,128)}, f32[128,128]{1,0:T(8,128)}, f32[128,128]{1,0:T(8,128)}, f32[128,128]{1,0:T(8,128)}) custom-call(s32[3]{0:T(128)} %pad_add_fusion.meta, f32[8,64,128]{2,1,0:T(8,128)} %refs_5_.1, f32[8,64,128]{2,1,0:T(8,128)} %bitcast.23, f32[8,64,128]{2,1,0:T(8,128)} %bitcast.19, ...), custom_call_target="tpu_custom_call" | custom-call | flops 18874368 | bytes 10485760 | tf_op jit(solution)/shard_map/adjoint/pallas_call | solution.py:383
  54.6 1.6 %collective-permute-start.4 = (f32[128,128]{1,0:T(8,128)}, f32[128,128]{1,0:T(8,128)S(1)}, u32[]{:S(2)}, u32[]{:S(2)}) collective-permute-start(f32[128,128]{1,0:T(8,128)} %get-tuple-element.19), channel_id=1, source_target_pairs={{0,4},{4,0},{8,12},{12,8},{1,5},{5,1},{9,13},{13,9},{2,6},{6,2},{1... | collective-permute-start | bytes 196616 | tf_op jit(solution)/shard_map/ppermute | solution.py:394
  56.3 2.6 %collective-permute-start.5 = (f32[128,128]{1,0:T(8,128)}, f32[128,128]{1,0:T(8,128)S(1)}, u32[]{:S(2)}, u32[]{:S(2)}) collective-permute-start(f32[128,128]{1,0:T(8,128)} %get-tuple-element.20), channel_id=1, source_target_pairs={{0,8},{4,12},{8,0},{12,4},{1,9},{5,13},{9,1},{13,5},{2,10},{6,14},... | collective-permute-start | bytes 196616 | tf_op jit(solution)/shard_map/ppermute | solution.py:394
  59.2 4.8 %collective-permute-done.5.refs_2_ = f32[128,128]{1,0:T(8,128)S(1)} collective-permute-done((f32[128,128]{1,0:T(8,128)}, f32[128,128]{1,0:T(8,128)S(1)}, u32[]{:S(2)}, u32[]{:S(2)}) %collective-permute-start.5) | collective-permute-done | bytes 65568 | tf_op jit(solution)/shard_map/ppermute | solution.py:394
  64.0 1.3 %collective-permute-done.6.refs_3_ = f32[128,128]{1,0:T(8,128)S(1)} collective-permute-done((f32[128,128]{1,0:T(8,128)}, f32[128,128]{1,0:T(8,128)S(1)}, u32[]{:S(2)}, u32[]{:S(2)}) %collective-permute-start.6) | collective-permute-done | bytes 65568 | tf_op jit(solution)/shard_map/ppermute | solution.py:394
  65.9 1.7 %total.1 = (f32[128,128]{1,0:T(8,128)}, f32[8,128]{1,0:T(8,128)}) custom-call(f32[128,128]{1,0:T(8,128)} %get-tuple-element.18.refs_0_, f32[128,128]{1,0:T(8,128)} %copy-done.6, f32[128,128]{1,0:T(8,128)} %copy-done.7, f32[128,128]{1,0:T(8,128)} %copy-done.8), custom_call_target="tpu_custom_call" | custom-call | flops 65536 | bytes 262144 | tf_op jit(solution)/shard_map/total/pallas_call | solution.py:395
  67.5 1.5 %collective-permute-start.11 = (f32[8,128]{1,0:T(8,128)}, f32[8,128]{1,0:T(8,128)S(1)}, u32[]{:S(2)}, u32[]{:S(2)}) collective-permute-start(f32[8,128]{1,0:T(8,128)} %get-tuple-element.23), channel_id=1, source_target_pairs={{0,2},{1,3},{2,0},{3,1},{4,6},{5,7},{6,4},{7,5},{8,10},{9,11},{10,... | collective-permute-start | bytes 12296 | tf_op jit(solution)/shard_map/ppermute | solution.py:404
  69.4 1.4 %collective-permute-done.12 = f32[8,128]{1,0:T(8,128)S(1)} collective-permute-done((f32[8,128]{1,0:T(8,128)}, f32[8,128]{1,0:T(8,128)S(1)}, u32[]{:S(2)}, u32[]{:S(2)}) %collective-permute-start.12) | collective-permute-done | bytes 4128 | tf_op jit(solution)/shard_map/ppermute | solution.py:404
  72.0 2.0 %collective-permute-start.15 = (f32[8,128]{1,0:T(8,128)S(1)}, f32[8,128]{1,0:T(8,128)S(1)}, u32[]{:S(2)}, u32[]{:S(2)}) collective-permute-start(f32[8,128]{1,0:T(8,128)S(1)} %maximum_maximum_fusion), channel_id=1, source_target_pairs={{0,12},{4,8},{8,4},{12,0},{1,13},{5,9},{9,5},{13,1},{2,14},{6,10},... | collective-permute-start | bytes 12296 | tf_op jit(solution)/shard_map/ppermute | solution.py:406
  74.0 1.5 %collective-permute-start.14 = (f32[8,128]{1,0:T(8,128)S(1)}, f32[8,128]{1,0:T(8,128)S(1)}, u32[]{:S(2)}, u32[]{:S(2)}) collective-permute-start(f32[8,128]{1,0:T(8,128)S(1)} %maximum_maximum_fusion), channel_id=1, source_target_pairs={{0,8},{4,12},{8,0},{12,4},{1,9},{5,13},{9,1},{13,5},{2,10},{6,14},... | collective-permute-start | bytes 12296 | tf_op jit(solution)/shard_map/ppermute | solution.py:406
  77.5 2.0 %collective-permute-start.9 = (f32[128,128]{1,0:T(8,128)}, f32[128,128]{1,0:T(8,128)S(1)}, u32[]{:S(2)}, u32[]{:S(2)}) collective-permute-start(f32[128,128]{1,0:T(8,128)} %get-tuple-element.22.refs_0_), channel_id=1, source_target_pairs={{0,12},{4,8},{8,4},{12,0},{1,13},{5,9},{9,5},{13,1},{2,14},{6,10},... | collective-permute-start | bytes 196616 | tf_op jit(solution)/shard_map/ppermute | solution.py:403
  80.1 1.7 %collective-permute-start.7 = (f32[128,128]{1,0:T(8,128)}, f32[128,128]{1,0:T(8,128)S(1)}, u32[]{:S(2)}, u32[]{:S(2)}) collective-permute-start(f32[128,128]{1,0:T(8,128)} %get-tuple-element.22.refs_0_), channel_id=1, source_target_pairs={{0,4},{4,0},{8,12},{12,8},{1,5},{5,1},{9,13},{13,9},{2,6},{6,2},{1... | collective-permute-start | bytes 196616 | tf_op jit(solution)/shard_map/ppermute | solution.py:403
  82.5 1.4 %collective-permute-done.9.refs_3_ = f32[128,128]{1,0:T(8,128)S(1)} collective-permute-done((f32[128,128]{1,0:T(8,128)}, f32[128,128]{1,0:T(8,128)S(1)}, u32[]{:S(2)}, u32[]{:S(2)}) %collective-permute-start.9) | collective-permute-done | bytes 65568 | tf_op jit(solution)/shard_map/ppermute | solution.py:403
  83.8 3.5 %collective-permute-done.8.refs_2_ = f32[128,128]{1,0:T(8,128)S(1)} collective-permute-done((f32[128,128]{1,0:T(8,128)}, f32[128,128]{1,0:T(8,128)S(1)}, u32[]{:S(2)}, u32[]{:S(2)}) %collective-permute-start.8) | collective-permute-done | bytes 65568 | tf_op jit(solution)/shard_map/ppermute | solution.py:403
  88.0 2.9 %update.1 = (f32[8,64,128]{2,1,0:T(8,128)}, f32[8,64,128]{2,1,0:T(8,128)}) custom-call(s32[3]{0:T(128)} %pad_add_fusion.meta, f32[128,128]{1,0:T(8,128)} %get-tuple-element.22.refs_0_, f32[128,128]{1,0:T(8,128)} %copy-done.5, f32[128,128]{1,0:T(8,128)} %copy-done.4, f32[128,128]{1,0:T(8,128)} %copy-done.3, f32[32,128]{1,0:T(8,128)} %pad_maximum_fusion.4.refs_4_, ...), custom_call_target="tpu_custom_call" | custom-call | flops 1310720 | bytes 1572864 | tf_op jit(solution)/shard_map/update/pallas_call | solution.py:408
  (50 shorter events, 9.3 us)
Async XLA Ops:
  4.2 16.3 %collective-permute-start.1 = (f32[22,64,128]{2,1,0:T(8,128)S(1)}, f32[22,64,128]{2,1,0:T(8,128)S(1)}, u32[]{:S(2)}, u32[]{:S(2)}) collective-permute-start(f32[22,64,128]{2,1,0:T(8,128)S(1)} %get-tuple-element.35), channel_id=1, source_target_pairs={{1,2},{2,1},{5,6},{6,5},{9,10},{10,9},{13,14},{14,13},{17,18},{18,... | collective-permute-start | bytes 2162696 | tf_op jit(solution)/shard_map/ppermute | solution.py:340
  5.0 15.6 %collective-permute-start = (f32[22,64,128]{2,1,0:T(8,128)S(1)}, f32[22,64,128]{2,1,0:T(8,128)S(1)}, u32[]{:S(2)}, u32[]{:S(2)}) collective-permute-start(f32[22,64,128]{2,1,0:T(8,128)S(1)} %get-tuple-element.36), channel_id=1, source_target_pairs={{0,1},{2,3},{1,0},{3,2},{4,5},{6,7},{5,4},{7,6},{8,9},{10,11},{9,8... | collective-permute-start | bytes 2162696 | tf_op jit(solution)/shard_map/ppermute | solution.py:341
  11.3 25.5 %collective-permute-start.3 = (f32[15,64,128]{2,1,0:T(8,128)}, f32[15,64,128]{2,1,0:T(8,128)S(1)}, u32[]{:S(2)}, u32[]{:S(2)}) collective-permute-start(f32[15,64,128]{2,1,0:T(8,128)} %get-tuple-element.31), channel_id=1, source_target_pairs={{1,2},{2,1},{5,6},{6,5},{9,10},{10,9},{13,14},{14,13},{17,18},{18,... | collective-permute-start | bytes 1474568 | tf_op jit(solution)/shard_map/ppermute | solution.py:342
  12.0 24.8 %collective-permute-start.2 = (f32[15,64,128]{2,1,0:T(8,128)}, f32[15,64,128]{2,1,0:T(8,128)}, u32[]{:S(2)}, u32[]{:S(2)}) collective-permute-start(f32[15,64,128]{2,1,0:T(8,128)} %get-tuple-element.32), channel_id=1, source_target_pairs={{0,1},{2,3},{1,0},{3,2},{4,5},{6,7},{5,4},{7,6},{8,9},{10,11},{9,8... | collective-permute-start | bytes 1474568 | tf_op jit(solution)/shard_map/ppermute | solution.py:343
  36.8 39.7 %copy-start.12 = (f32[1,64,128]{2,1,0:T(8,128)S(1)}, f32[1,64,128]{2,1,0:T(8,128)}, u32[]{:S(2)}) copy-start(f32[1,64,128]{2,1,0:T(8,128)} %get-tuple-element.26) | copy-start | bytes 98308
  36.8 39.7 %copy-start.11 = (f32[1,64,128]{2,1,0:T(8,128)S(1)}, f32[1,64,128]{2,1,0:T(8,128)}, u32[]{:S(2)}) copy-start(f32[1,64,128]{2,1,0:T(8,128)} %get-tuple-element.27) | copy-start | bytes 98308
  54.6 4.5 %collective-permute-start.4 = (f32[128,128]{1,0:T(8,128)}, f32[128,128]{1,0:T(8,128)S(1)}, u32[]{:S(2)}, u32[]{:S(2)}) collective-permute-start(f32[128,128]{1,0:T(8,128)} %get-tuple-element.19), channel_id=1, source_target_pairs={{0,4},{4,0},{8,12},{12,8},{1,5},{5,1},{9,13},{13,9},{2,6},{6,2},{1... | collective-permute-start | bytes 196616 | tf_op jit(solution)/shard_map/ppermute | solution.py:394
  56.3 7.7 %collective-permute-start.5 = (f32[128,128]{1,0:T(8,128)}, f32[128,128]{1,0:T(8,128)S(1)}, u32[]{:S(2)}, u32[]{:S(2)}) collective-permute-start(f32[128,128]{1,0:T(8,128)} %get-tuple-element.20), channel_id=1, source_target_pairs={{0,8},{4,12},{8,0},{12,4},{1,9},{5,13},{9,1},{13,5},{2,10},{6,14},... | collective-permute-start | bytes 196616 | tf_op jit(solution)/shard_map/ppermute | solution.py:394
  58.9 6.4 %collective-permute-start.6 = (f32[128,128]{1,0:T(8,128)}, f32[128,128]{1,0:T(8,128)S(1)}, u32[]{:S(2)}, u32[]{:S(2)}) collective-permute-start(f32[128,128]{1,0:T(8,128)} %get-tuple-element.21), channel_id=1, source_target_pairs={{0,12},{4,8},{8,4},{12,0},{1,13},{5,9},{9,5},{13,1},{2,14},{6,10},... | collective-permute-start | bytes 196616 | tf_op jit(solution)/shard_map/ppermute | solution.py:394
  59.2 6.1 %copy-start.6 = (f32[128,128]{1,0:T(8,128)}, f32[128,128]{1,0:T(8,128)S(1)}, u32[]{:S(2)}) copy-start(f32[128,128]{1,0:T(8,128)S(1)} %collective-permute-done.4.refs_1_) | copy-start | bytes 196612
  67.5 3.2 %collective-permute-start.12 = (f32[8,128]{1,0:T(8,128)}, f32[8,128]{1,0:T(8,128)S(1)}, u32[]{:S(2)}, u32[]{:S(2)}) collective-permute-start(f32[8,128]{1,0:T(8,128)} %get-tuple-element.23), channel_id=1, source_target_pairs={{0,3},{1,2},{2,1},{3,0},{4,7},{5,6},{6,5},{7,4},{8,11},{9,10},{10,... | collective-permute-start | bytes 12296 | tf_op jit(solution)/shard_map/ppermute | solution.py:404
  67.5 3.8 %collective-permute-start.11 = (f32[8,128]{1,0:T(8,128)}, f32[8,128]{1,0:T(8,128)S(1)}, u32[]{:S(2)}, u32[]{:S(2)}) collective-permute-start(f32[8,128]{1,0:T(8,128)} %get-tuple-element.23), channel_id=1, source_target_pairs={{0,2},{1,3},{2,0},{3,1},{4,6},{5,7},{6,4},{7,5},{8,10},{9,11},{10,... | collective-permute-start | bytes 12296 | tf_op jit(solution)/shard_map/ppermute | solution.py:404
  69.1 2.3 %collective-permute-start.10 = (f32[8,128]{1,0:T(8,128)}, f32[8,128]{1,0:T(8,128)S(1)}, u32[]{:S(2)}, u32[]{:S(2)}) collective-permute-start(f32[8,128]{1,0:T(8,128)} %get-tuple-element.23), channel_id=1, source_target_pairs={{0,1},{1,0},{2,3},{3,2},{4,5},{5,4},{6,7},{7,6},{8,9},{9,8},{10,11... | collective-permute-start | bytes 12296 | tf_op jit(solution)/shard_map/ppermute | solution.py:404
  72.0 5.4 %collective-permute-start.15 = (f32[8,128]{1,0:T(8,128)S(1)}, f32[8,128]{1,0:T(8,128)S(1)}, u32[]{:S(2)}, u32[]{:S(2)}) collective-permute-start(f32[8,128]{1,0:T(8,128)S(1)} %maximum_maximum_fusion), channel_id=1, source_target_pairs={{0,12},{4,8},{8,4},{12,0},{1,13},{5,9},{9,5},{13,1},{2,14},{6,10},... | collective-permute-start | bytes 12296 | tf_op jit(solution)/shard_map/ppermute | solution.py:406
  74.0 5.5 %collective-permute-start.14 = (f32[8,128]{1,0:T(8,128)S(1)}, f32[8,128]{1,0:T(8,128)S(1)}, u32[]{:S(2)}, u32[]{:S(2)}) collective-permute-start(f32[8,128]{1,0:T(8,128)S(1)} %maximum_maximum_fusion), channel_id=1, source_target_pairs={{0,8},{4,12},{8,0},{12,4},{1,9},{5,13},{9,1},{13,5},{2,10},{6,14},... | collective-permute-start | bytes 12296 | tf_op jit(solution)/shard_map/ppermute | solution.py:406
  75.6 4.5 %collective-permute-start.13 = (f32[8,128]{1,0:T(8,128)S(1)}, f32[8,128]{1,0:T(8,128)S(1)}, u32[]{:S(2)}, u32[]{:S(2)}) collective-permute-start(f32[8,128]{1,0:T(8,128)S(1)} %maximum_maximum_fusion), channel_id=1, source_target_pairs={{0,4},{4,0},{8,12},{12,8},{1,5},{5,1},{9,13},{13,9},{2,6},{6,2},{1... | collective-permute-start | bytes 12296 | tf_op jit(solution)/shard_map/ppermute | solution.py:406
  76.4 6.0 %collective-permute-start.16 = (f32[1,64,128]{2,1,0:T(8,128)S(1)}, f32[1,64,128]{2,1,0:T(8,128)S(1)}, u32[]{:S(2)}, u32[]{:S(2)}) collective-permute-start(f32[1,64,128]{2,1,0:T(8,128)S(1)} %copy-done.12), channel_id=1, source_target_pairs={{0,1},{2,3},{1,0},{3,2},{4,5},{6,7},{5,4},{7,6},{8,9},{10,11},{9,8... | collective-permute-start | bytes 98312 | tf_op jit(solution)/shard_map/ppermute | solution.py:379
  76.4 6.0 %collective-permute-start.17 = (f32[1,64,128]{2,1,0:T(8,128)S(1)}, f32[1,64,128]{2,1,0:T(8,128)S(1)}, u32[]{:S(2)}, u32[]{:S(2)}) collective-permute-start(f32[1,64,128]{2,1,0:T(8,128)S(1)} %copy-done.11), channel_id=1, source_target_pairs={{1,2},{2,1},{5,6},{6,5},{9,10},{10,9},{13,14},{14,13},{17,18},{18,... | collective-permute-start | bytes 98312 | tf_op jit(solution)/shard_map/ppermute | solution.py:380
  77.5 6.4 %collective-permute-start.9 = (f32[128,128]{1,0:T(8,128)}, f32[128,128]{1,0:T(8,128)S(1)}, u32[]{:S(2)}, u32[]{:S(2)}) collective-permute-start(f32[128,128]{1,0:T(8,128)} %get-tuple-element.22.refs_0_), channel_id=1, source_target_pairs={{0,12},{4,8},{8,4},{12,0},{1,13},{5,9},{9,5},{13,1},{2,14},{6,10},... | collective-permute-start | bytes 196616 | tf_op jit(solution)/shard_map/ppermute | solution.py:403
  79.5 7.8 %collective-permute-start.8 = (f32[128,128]{1,0:T(8,128)}, f32[128,128]{1,0:T(8,128)S(1)}, u32[]{:S(2)}, u32[]{:S(2)}) collective-permute-start(f32[128,128]{1,0:T(8,128)} %get-tuple-element.22.refs_0_), channel_id=1, source_target_pairs={{0,8},{4,12},{8,0},{12,4},{1,9},{5,13},{9,1},{13,5},{2,10},{6,14},... | collective-permute-start | bytes 196616 | tf_op jit(solution)/shard_map/ppermute | solution.py:403
  80.1 7.2 %collective-permute-start.7 = (f32[128,128]{1,0:T(8,128)}, f32[128,128]{1,0:T(8,128)S(1)}, u32[]{:S(2)}, u32[]{:S(2)}) collective-permute-start(f32[128,128]{1,0:T(8,128)} %get-tuple-element.22.refs_0_), channel_id=1, source_target_pairs={{0,4},{4,0},{8,12},{12,8},{1,5},{5,1},{9,13},{13,9},{2,6},{6,2},{1... | collective-permute-start | bytes 196616 | tf_op jit(solution)/shard_map/ppermute | solution.py:403
  82.5 4.9 %copy-start.9 = (f32[1,64,128]{2,1,0:T(8,128)}, f32[1,64,128]{2,1,0:T(8,128)S(1)}, u32[]{:S(2)}) copy-start(f32[1,64,128]{2,1,0:T(8,128)S(1)} %collective-permute-done.16.refs_8_) | copy-start | bytes 98308
  82.5 4.9 %copy-start.10 = (f32[1,64,128]{2,1,0:T(8,128)}, f32[1,64,128]{2,1,0:T(8,128)S(1)}, u32[]{:S(2)}) copy-start(f32[1,64,128]{2,1,0:T(8,128)S(1)} %collective-permute-done.17.refs_9_) | copy-start | bytes 98308
  83.8 3.5 %copy-start.3 = (f32[128,128]{1,0:T(8,128)}, f32[128,128]{1,0:T(8,128)S(1)}, u32[]{:S(2)}) copy-start(f32[128,128]{1,0:T(8,128)S(1)} %collective-permute-done.9.refs_3_) | copy-start | bytes 196612
  (7 other events, 6.0 us)

commit v2 on v0

v2 whole, which is shorter than its diff:
```python
import functools

import jax
import jax.numpy as jnp
from jax import lax
from jax.experimental import pallas as pl
from jax.experimental.pallas import tpu as pltpu
from jax.sharding import PartitionSpec as P

ITERS = 8
GUARD = 8
LANES = 128
LIMIT = 16 * 2**20
VMEM = pltpu.VMEM
SMEM = pltpu.SMEM
HBM = pl.ANY


def pairs(count, start):
    low = [(i, i + 1) for i in range(start, count - 1, 2)]
    return low + [(b, a) for a, b in low]


def partner_perms(count):
    if count & (count - 1) == 0:
        return [[(i, i ^ m) for i in range(count)] for m in range(1, count)]
    return [[(i, (i + m) % count) for i in range(count)] for m in range(1, count)]


def send_slot(me, m, count):
    return me ^ m if count & (count - 1) == 0 else lax.rem(me + m, count)


def from_slot(me, m, count):
    return me ^ m if count & (count - 1) == 0 else lax.rem(me - m + count, count)


def spec(space):
    return pl.BlockSpec(memory_space=space)


def cost(flops, nbytes):
    return pl.CostEstimate(flops=int(flops), bytes_accessed=int(nbytes), transcendentals=0)


def pack_kernel(depth, short, *refs):
    fields, (to_a, to_b, sem) = refs[: 1 + short], refs[1 + short :]
    odd = lax.rem(lax.axis_index("slab"), 2)
    n = depth - 1

    def copies(up_a, up_b):
        out = []
        for j, (dst, up) in enumerate(((to_a, up_a), (to_b, up_b))):
            at = 0
            for i, field in enumerate(fields):
                size, skip = (depth, 0) if i == 0 else (n, up)
                out.append(
                    pltpu.make_async_copy(
                        field.at[pl.ds(skip, size)], dst.at[pl.ds(at, size)], sem.at[j, i]
                    )
                )
                at += size
        return out

    @pl.when(odd == 0)
    def _():
        for c in copies(1, 0):
            c.start()

    @pl.when(odd != 0)
    def _():
        for c in copies(0, 1):
            c.start()

    for c in copies(0, 0):
        c.wait()


def inject_kernel(depth, width, rec_ref, misfit_ref, out_ref, left, right):
    rows = left.shape[0]
    base = (lax.axis_index("slab") * depth - depth) * width
    index = rec_ref[...]
    row_of = index // LANES
    lane_of = index - row_of * LANES
    row_of = row_of - base
    group = 2 * width
    for first in range(0, rows, group):
        at = lax.broadcasted_iota(jnp.int32, (group, LANES), 0) + first
        hot = jnp.where(at == row_of, 1.0, 0.0).astype(jnp.bfloat16)
        for part in range(3):
            left[pl.ds(first, group), pl.ds(part * LANES, LANES)] = hot
    lane = lax.broadcasted_iota(jnp.int32, (LANES, LANES), 0)
    mine = lane == lane_of
    for k in range(ITERS):
        value = misfit_ref[pl.ds(k, 1), :]
        for part in range(3):
            piece = value.astype(jnp.bfloat16).astype(jnp.float32)
            value = value - piece
            right[pl.ds(k * LANES, LANES), pl.ds(part * LANES, LANES)] = jnp.where(
                mine, piece, 0.0
            ).astype(jnp.bfloat16)

    def pair(j, carry):
        cols = right[pl.ds(pl.multiple_of(j * 2 * LANES, 2 * LANES), 2 * LANES), :]
        both = lax.dot_general(
            left[...], cols, (((1,), (1,)), ((), ())), preferred_element_type=jnp.float32
        )
        out_ref[2 * j] = both[:, :LANES].reshape(out_ref.shape[1:])
        out_ref[2 * j + 1] = both[:, LANES:].reshape(out_ref.shape[1:])
        return carry

    lax.fori_loop(0, ITERS // 2, pair, 0)


def lap_block(src, p, r, first, last):
    c = src[p, pl.ds(r, 8), :]
    s = src[p + 1, pl.ds(r, 8), :] + src[p - 1, pl.ds(r, 8), :]
    s = s + src[p, pl.ds(r + 1, 8), :]
    s = s + src[p, pl.ds(r - 1, 8), :]
    s = s + jnp.where(last, 0.0, pltpu.roll(c, LANES - 1, 1))
    s = s + jnp.where(first, 0.0, pltpu.roll(c, 1, 1))
    return c, s - 6.0 * c


def edges():
    lane = lax.broadcasted_iota(jnp.int32, (8, LANES), 1)
    return lane == 0, lane == LANES - 1


def clear_guards(field):
    planes, rows, _ = field.shape
    zero = jnp.zeros((GUARD, LANES), jnp.float32)
    for p in range(planes):
        field[p, pl.ds(0, GUARD), :] = zero
        field[p, pl.ds(rows - GUARD, GUARD), :] = zero


def fill(depth, width, own, a_in, b_in, at, bufs, guard):
    rows = [pl.ds(GUARD if g else 0, width) for g in guard]

    def main(p, carry):
        for src, dst, r in zip(own, bufs, rows):
            dst[depth + 1 + p, r, :] = src[p]
        return carry

    lax.fori_loop(0, depth, main, 0)

    def sides(low, high):
        def one(p, carry):
            for start, whole, dst, r in zip(at[0], at[1], bufs, rows):
                if not whole:
                    dst[2 + p, r, :] = low[start[0]][start[1] + p]
                    dst[2 * depth + 1 + p, r, :] = high[start[0]][start[1] + p]
                else:
                    dst[1 + p, r, :] = low[start[0]][start[1] + p]
                    dst[2 * depth + 1 + p, r, :] = high[start[0]][start[1] + p]
            return carry

        lax.fori_loop(0, depth - 1, one, 0)
        for start, whole, dst, r in zip(at[0], at[1], bufs, rows):
            if whole:
                dst[depth, r, :] = low[start[0]][start[1] + depth - 1]
                dst[3 * depth, r, :] = high[start[0]][start[1] + depth - 1]

    even = lax.rem(lax.axis_index("slab"), 2) == 0

    @pl.when(even)
    def _():
        sides(b_in, a_in)

    @pl.when(jnp.logical_not(even))
    def _():
        sides(a_in, b_in)

    return even


def sweep(depth, k, body):
    outer = (depth - k) // 2

    def halo(j, carry):
        body((depth - 1 - 2 * j, depth - 2 - 2 * j, 2 * depth + 2 * j, 2 * depth + 1 + 2 * j), False)
        return carry

    lax.fori_loop(0, outer, halo, 0)
    assert depth % 4 == 0

    def inner(j, carry):
        body(tuple(depth + 4 * j + i for i in range(4)), True)
        return carry

    lax.fori_loop(0, depth // 4, inner, 0)


def forward_kernel(
    depth, width, wavelet, src_index, model, now, later, a_in, b_in,
    last_out, base_out, lap_out, a_edge, b_edge,
    cur, old, mod,
):
    clear_guards(cur)
    clear_guards(old)
    even = fill(
        depth, width, (now, later, model), (a_in,), (b_in,),
        (((0, 0), (0, depth), (0, 2 * depth - 1)), (True, False, False)),
        (cur, old, mod), (True, True, False),
    )
    first, last = edges()
    source = src_index[0]
    src_row = source // LANES
    src_lane = source - src_row * LANES
    src_row = src_row - (lax.axis_index("slab") * depth - depth) * width
    bufs = (cur, old)
    for k in range(ITERS):
        s, d = bufs[k % 2], bufs[(k + 1) % 2]

        def body(planes, keep):
            for p in planes:
                for r in range(0, width, 8):
                    c, lap = lap_block(s, p + 1, GUARD + r, first, last)
                    here = (p + 1, pl.ds(GUARD + r, 8), slice(None))
                    d[here] = 2.0 * c - d[here] + mod[p + 1, pl.ds(r, 8), :] * lap
                    if keep:
                        lap_out[k, p - depth, pl.ds(r, 8), :] = lap

        sweep(depth, k, body)

        @pl.when((src_row >= (k + 1) * width) & (src_row < (3 * depth - 1 - k) * width))
        def _():
            plane = src_row // width
            here = (plane + 1, pl.ds(GUARD + src_row - plane * width, 1), slice(None))
            at = lax.broadcasted_iota(jnp.int32, (1, LANES), 1) == src_lane
            d[here] = d[here] + jnp.where(at, wavelet[0, k], 0.0)

    u, u_later = bufs[ITERS % 2], bufs[(ITERS + 1) % 2]
    rows = pl.ds(GUARD, width)

    def finish(p, carry):
        c = u[depth + 1 + p, rows, :]
        last_out[p] = c
        base_out[p] = 2.0 * c - u_later[depth + 1 + p, rows, :]
        return carry

    lax.fori_loop(0, depth, finish, 0)
    a_edge[0] = u[jnp.where(even, 2 * depth, depth + 1), rows, :]
    b_edge[0] = u[jnp.where(even, depth + 1, 2 * depth), rows, :]


def adjoint_kernel(
    depth, width, shots, model, now, later, fa_in, fb_in, a_in, b_in, laps, extra,
    last_out, *rest,
):
    pieces = rest[:shots]
    image, cur, old, mod = rest[shots:]
    clear_guards(cur)
    clear_guards(old)
    fill(
        depth, width, (now, later, model), (a_in, fa_in), (b_in, fb_in),
        (((0, 0), (0, depth), (1, 2 * depth - 1)), (True, False, False)),
        (cur, old, mod), (True, True, False),
    )
    first, last = edges()
    bufs = (cur, old)
    for k in range(ITERS):
        s, d = bufs[k % 2], bufs[(k + 1) % 2]

        def body(planes, keep):
            for p in planes:
                for r in range(0, width, 8):
                    c, lap = lap_block(s, p + 1, GUARD + r, first, last)
                    here = (p + 1, pl.ds(GUARD + r, 8), slice(None))
                    rows = pl.ds(r, 8)
                    new = 2.0 * c - d[here] + mod[p + 1, rows, :] * lap
                    d[here] = new + extra[k, p, rows, :]
                    if keep:
                        q = p - depth
                        add = c * laps[k, q, rows, :]
                        into = pl.ds(pl.multiple_of(q * width + r, 8), 8)
                        image[into, :] = add if k == 0 else image[into, :] + add

        sweep(depth, k, body)

    a = bufs[ITERS % 2]

    def finish(p, carry):
        last_out[p] = a[depth + 1 + p, pl.ds(GUARD, width), :]
        return carry

    lax.fori_loop(0, depth, finish, 0)
    n = depth * width // shots
    me = lax.axis_index("shot")
    for m in range(shots):
        to = me if m == 0 else send_slot(me, m, shots)
        pieces[m][...] = image[pl.ds(pl.multiple_of(to * n, n), n), :]


def sum_kernel(*refs):
    *parts, out = refs
    n = parts[0].shape[0]
    top = jnp.zeros((8, LANES), jnp.float32)
    for r in range(0, n, 8):
        total = parts[0][pl.ds(r, 8), :]
        for part in parts[1:]:
            total = total + part[pl.ds(r, 8), :]
        out[pl.ds(r, 8), :] = total
        top = jnp.maximum(top, jnp.abs(total))
    out[pl.ds(n, 8), :] = top


def top_kernel(*refs):
    *parts, out = refs
    n = parts[0].shape[0] - 8
    top = parts[0][pl.ds(n, 8), :]
    for part in parts[1:]:
        top = jnp.maximum(top, part[pl.ds(n, 8), :])
    out[...] = top


def final_kernel(depth, width, shots, slabs, *refs):
    n = depth * width // shots
    grads, tops = refs[:shots], refs[shots : shots + slabs]
    model, u, base, a_edge, b_edge, new_model, stepped, pad, grad = refs[shots + slabs :]
    even = lax.rem(lax.axis_index("slab"), 2) == 0
    me = lax.axis_index("shot")
    rows = pl.ds(GUARD, width)
    clear_guards(pad)
    low, high = jnp.where(even, 0, depth + 1), jnp.where(even, depth + 1, 0)
    pad[low, rows, :] = b_edge[0]
    pad[high, rows, :] = a_edge[0]

    def place(p, carry):
        pad[p + 1, rows, :] = u[p]
        return carry

    lax.fori_loop(0, depth, place, 0)
    for m in range(shots):
        owner = me if m == 0 else from_slot(me, m, shots)
        grad[pl.ds(pl.multiple_of(owner * n, n), n), :] = grads[m][pl.ds(0, n), :]
    top = tops[0][...]
    for other in tops[1:]:
        top = jnp.maximum(top, other[...])
    peak = jnp.max(top)
    first, last = edges()

    def planes(j, carry):
        for i in range(4):
            p = 4 * j + i
            for r in range(0, width, 8):
                g = grad[pl.ds(pl.multiple_of(p * width + r, 8), 8), :]
                new = jnp.clip(model[p, pl.ds(r, 8), :] - 0.1 * g / (peak + 1e-06), 0.05, 0.3)
                new_model[p, pl.ds(r, 8), :] = new
                _, lap = lap_block(pad, p + 1, GUARD + r, first, last)
                stepped[p, pl.ds(r, 8), :] = base[p, pl.ds(r, 8), :] + new * lap
        return carry

    lax.fori_loop(0, depth // 4, planes, 0)


def on_chip(x):
    return pltpu.with_memory_space_constraint(x, VMEM)


def call(kernel, out_shape, args, spaces, scratch, flops, nbytes, name):
    args = [on_chip(x) if space is VMEM else x for x, space in zip(args, spaces)]
    return pl.pallas_call(
        kernel,
        out_shape=out_shape,
        in_specs=[spec(space) for space in spaces],
        out_specs=[spec(VMEM)] * len(out_shape),
        scratch_shapes=scratch,
        cost_estimate=cost(flops, nbytes),
        compiler_params=pltpu.CompilerParams(vmem_limit_bytes=LIMIT),
        name=name,
    )(*args)


def per_device(model, fwd_now, fwd_next, adj_now, adj_next, wavelet, misfit, src_index, rec_index):
    f32 = jnp.float32
    depth, width, length = model.shape
    assert length == LANES and fwd_now.shape[0] == 1 and width % 8 == 0
    u0, u1, a0, a1 = fwd_now[0], fwd_next[0], adj_now[0], adj_next[0]
    slabs, shots = lax.axis_size("slab"), lax.axis_size("shot")
    perm_a, perm_b = pairs(slabs, 0), pairs(slabs, 1)
    plane = (depth, width, LANES)
    planes = 3 * depth
    cells = depth * width * LANES
    shape = jax.ShapeDtypeStruct

    def packed(fields, name):
        size = depth + (len(fields) - 1) * (depth - 1)
        return call(
            functools.partial(pack_kernel, depth, len(fields) - 1),
            [VMEM((size, width, LANES), f32)] * 2,
            fields, [HBM] * len(fields), [pltpu.SemaphoreType.DMA((2, len(fields)))],
            0, 16 * len(fields) * cells, name,
        )

    fa, fb = packed((u0, u1, model), "pack_forward")
    fb = lax.ppermute(fb, "slab", perm_b)
    fa = lax.ppermute(fa, "slab", perm_a)
    ga, gb = packed((a0, a1), "pack_adjoint")
    gb = lax.ppermute(gb, "slab", perm_b)
    ga = lax.ppermute(ga, "slab", perm_a)

    (extra,) = call(
        functools.partial(inject_kernel, depth, width),
        [VMEM((ITERS, planes, width, LANES), f32)],
        (rec_index, misfit[0]), (VMEM, VMEM),
        [
            VMEM((planes * width, 3 * LANES), jnp.bfloat16),
            VMEM((ITERS * LANES, 3 * LANES), jnp.bfloat16),
        ],
        2 * planes * width * 3 * LANES * ITERS * LANES, 4 * ITERS * planes * width * LANES, "inject",
    )

    field = VMEM((planes + 2, width + 2 * GUARD, LANES), f32)
    work = [field, field, VMEM((planes + 2, width, LANES), f32)]
    edge = VMEM((1, width, LANES), f32)
    u, base, laps, a_edge, b_edge = call(
        functools.partial(forward_kernel, depth, width),
        [VMEM(plane, f32), VMEM(plane, f32), VMEM((ITERS, *plane), f32), edge, edge],
        (wavelet, src_index, model, u0, u1, fa, fb), [SMEM] * 2 + [VMEM] * 5,
        work, 15 * ITERS * 2 * cells, 4 * cells * 20, "forward",
    )

    a_edge = lax.ppermute(a_edge, "slab", perm_a)
    b_edge = lax.ppermute(b_edge, "slab", perm_b)

    n = depth * width // shots
    a, *pieces = call(
        functools.partial(adjoint_kernel, depth, width, shots),
        [shape(plane, f32)] + [VMEM((n, LANES), f32)] * shots,
        (model, a0, a1, fa, fb, ga, gb, laps, extra), [VMEM] * 9,
        [VMEM((depth * width, LANES), f32), *work],
        18 * ITERS * 2 * cells, 4 * cells * 40, "adjoint",
    )

    perms = partner_perms(shots)
    parts = [pieces[0]] + [lax.ppermute(x, "shot", q) for x, q in zip(pieces[1:], perms)]
    (grad,) = call(
        sum_kernel, [VMEM((n + 8, LANES), f32)], parts, [VMEM] * shots, [],
        shots * n * LANES, 4 * shots * n * LANES, "total",
    )
    grads = [grad] + [lax.ppermute(grad, "shot", q) for q in perms]
    (top,) = call(
        top_kernel, [VMEM((8, LANES), f32)], grads, [VMEM] * shots, [], 0, 4096 * shots, "top"
    )
    tops = [top] + [lax.ppermute(top, "slab", q) for q in partner_perms(slabs)]

    new_model, stepped = call(
        functools.partial(final_kernel, depth, width, shots, slabs),
        [shape(plane, f32), shape(plane, f32)],
        (*grads, *tops, model, u, base, a_edge, b_edge), [VMEM] * (shots + slabs + 5),
        [VMEM((depth + 2, width + 2 * GUARD, LANES), f32), VMEM((depth * width, LANES), f32)],
        20 * cells, 4 * 6 * cells, "update",
    )
    return new_model, stepped[None], a[None]


def solution(mesh):
    in_specs = (
        P(("groups", "slab"), None, None),
        P(("groups", "shot"), "slab", None, None),
        P(("groups", "shot"), "slab", None, None),
        P(("groups", "shot"), "slab", None, None),
        P(("groups", "shot"), "slab", None, None),
        P(("groups", "shot"), None),
        P(("groups", "shot"), None, None),
        P(("groups", "shot")),
        P(("groups", "shot"), None),
    )
    out_specs = (
        P(("groups", "slab"), None, None),
        P(("groups", "shot"), "slab", None, None),
        P(("groups", "shot"), "slab", None, None),
    )
    return jax.shard_map(
        per_device, mesh=mesh, in_specs=in_specs, out_specs=out_specs, check_vma=False
    )
```

time: 170 us -> 54.6 us (0.32)
  between operations: 36 us -> 1.47 us
  other arithmetic: 33 us -> 0 us
  starting transfers between devices: 49.9 us -> 17.2 us
  waiting for transfers between devices: 36.9 us -> 12.4 us
  Pallas kernels: 0 us -> 17.1 us
  blocking collectives: 6.3 us -> 0 us
    ppermute x18 -> x15, starting transfers between devices: 49.8 us -> 17.2 us  [the longest x3 4.45 us: per_device(): grads = [grad] + [lax.ppermute(grad, 'shot', q) for q in perms]]
    psum x1 -> x0, waiting for transfers between devices: 27.4 us -> none  [per_device(): gradient = lax.psum(local_image, 'shot')]
    pallas_call x0 -> x8, Pallas kernels: none -> 17.1 us  [call(): pl.pallas_call(kernel, out_shape=out_shape, in_specs=[spec(space) for spa...]
    scatter-add x8 -> x0, other arithmetic: 11 us -> none  [inject(): flat = flat.at[rows, local].add(jnp.where(valid, values, 0.0))]
    add x18 -> x0, other arithmetic: 9.38 us -> none  [the longest x8 5.13 us: inject(): flat = flat.at[rows, local].add(jnp.where(valid, values, 0.0))]
    pmax x1 -> x0, blocking collectives: 6.3 us -> none  [per_device(): peak = lax.pmax(jnp.max(jnp.abs(gradient)), 'slab')]
    sub x8 -> x0, other arithmetic: 4.02 us -> none  [local_laplace(): return beside - 6.0 * center]
    concatenate x17 -> x0, other arithmetic: 3.93 us -> none  [the longest x9 3.85 us: extended(): block = jnp.concatenate([low, block, high], axis=dim)]
  transfers between devices with their start and end apart: 19 -> 15, of which waited for: 8 -> 6; matrix products, arithmetic and copies ran while one was open for 6% -> 0% of each run, Pallas kernels for 0% -> 16%
where the time goes in v2:
time: 54.6 us; the launch traced here: 54.3 us
  starting transfers between devices  17.2 us (32%)
  Pallas kernels  17.1 us (31%)
  waiting for transfers between devices  12.4 us (23%)
  local copies, waits for them, and re-layouts  6.1 us (11%)
  between operations  1.47 us (3%)
    pallas_call x8, Pallas kernels, call(): pl.pallas_call(kernel, out_shape=out_shape, in_specs=[spec(space) for spa...  17.1 us
    ppermute x3, waiting for transfers between devices, per_device(): lax.ppermute(x, 'shot', q)  6.25 us
    unnamed x26, local copies, waits for them, and re-layouts  6.1 us
    ppermute x3, starting transfers between devices, per_device(): grads = [grad] + [lax.ppermute(grad, 'shot', q) for q in perms]  4.45 us
    ppermute x3, starting transfers between devices, per_device(): lax.ppermute(x, 'shot', q)  4.39 us
    ppermute x3, waiting for transfers between devices, per_device(): grads = [grad] + [lax.ppermute(grad, 'shot', q) for q in perms]  4.33 us
    ppermute x1, starting transfers between devices, per_device(): ga = lax.ppermute(ga, 'slab', perm_a)  3.88 us
    ppermute x3, starting transfers between devices, per_device(): tops = [top] + [lax.ppermute(top, 'slab', q) for q in partner_perms(slabs)]  1.92 us
  transfers between devices with their start and end apart: 15, of which 6 were waited for; matrix products, arithmetic and copies ran while one was open for 0% of the time, Pallas kernels for 16%

profile of v2, /device:TPU:0, one launch (start us, length us, event | category | flops | bytes accessed | tf_op | source)
XLA Modules:
  0.0 54.3 jit_solution(18306904545868171646)
XLA Ops:
  0.6 0.9 %copy-done = f32[8,64,128]{2,1,0:T(8,128)S(1)} copy-done((f32[8,64,128]{2,1,0:T(8,128)S(1)}, f32[8,64,128]{2,1,0:T(8,128)}, u32[]{:S(2)}) %copy-start) | copy-done | bytes 262168
  1.6 0.9 %copy-done.6 = f32[1,8,64,128]{3,2,1,0:T(8,128)S(1)} copy-done((f32[1,8,64,128]{3,2,1,0:T(8,128)S(1)}, f32[1,8,64,128]{3,2,1,0:T(8,128)}, u32[]{:S(2)}) %copy-start.6) | copy-done | bytes 262168
  2.5 0.9 %copy-done.8 = f32[1,8,64,128]{3,2,1,0:T(8,128)S(1)} copy-done((f32[1,8,64,128]{3,2,1,0:T(8,128)S(1)}, f32[1,8,64,128]{3,2,1,0:T(8,128)}, u32[]{:S(2)}) %copy-start.8) | copy-done | bytes 262168
  3.5 1.3 %pack_forward.1 = (f32[22,64,128]{2,1,0:T(8,128)S(1)}, f32[22,64,128]{2,1,0:T(8,128)S(1)}) custom-call(f32[8,64,128]{2,1,0:T(8,128)S(1)} %bitcast.11, f32[8,64,128]{2,1,0:T(8,128)S(1)} %bitcast.13, f32[8,64,128]{2,1,0:T(8,128)S(1)} %copy-done), custom_call_target="tpu_custom_call" | custom-call | bytes 3145728 | tf_op jit(solution)/shard_map/pack_forward/pallas_call | solution.py:364
  5.3 0.7 %collective-permute-start.1 = (f32[22,64,128]{2,1,0:T(8,128)S(1)}, f32[22,64,128]{2,1,0:T(8,128)S(1)}, u32[]{:S(2)}, u32[]{:S(2)}) collective-permute-start(f32[22,64,128]{2,1,0:T(8,128)S(1)} %get-tuple-element.20), channel_id=1, source_target_pairs={{1,2},{2,1},{5,6},{6,5},{9,10},{10,9},{13,14},{14,13},{17,18},{18,... | collective-permute-start | bytes 2162696 | tf_op jit(solution)/shard_map/ppermute | solution.py:398
  6.1 0.9 %copy-done.2 = f32[1,8,64,128]{3,2,1,0:T(8,128)S(1)} copy-done((f32[1,8,64,128]{3,2,1,0:T(8,128)S(1)}, f32[1,8,64,128]{3,2,1,0:T(8,128)}, u32[]{:S(2)}) %copy-start.2) | copy-done | bytes 262168
  7.0 0.9 %copy-done.4 = f32[1,8,64,128]{3,2,1,0:T(8,128)S(1)} copy-done((f32[1,8,64,128]{3,2,1,0:T(8,128)S(1)}, f32[1,8,64,128]{3,2,1,0:T(8,128)}, u32[]{:S(2)}) %copy-start.4) | copy-done | bytes 262168
  8.6 3.9 %collective-permute-start.2 = (f32[15,64,128]{2,1,0:T(8,128)S(1)}, f32[15,64,128]{2,1,0:T(8,128)S(1)}, u32[]{:S(2)}, u32[]{:S(2)}) collective-permute-start(f32[15,64,128]{2,1,0:T(8,128)S(1)} %get-tuple-element.21), channel_id=1, source_target_pairs={{0,1},{2,3},{1,0},{3,2},{4,5},{6,7},{5,4},{7,6},{8,9},{10,11},{9,8... | collective-permute-start | bytes 1474568 | tf_op jit(solution)/shard_map/ppermute | solution.py:402
  12.5 0.7 %collective-permute-start.3 = (f32[15,64,128]{2,1,0:T(8,128)S(1)}, f32[15,64,128]{2,1,0:T(8,128)S(1)}, u32[]{:S(2)}, u32[]{:S(2)}) collective-permute-start(f32[15,64,128]{2,1,0:T(8,128)S(1)} %get-tuple-element.22), channel_id=1, source_target_pairs={{1,2},{2,1},{5,6},{6,5},{9,10},{10,9},{13,14},{14,13},{17,18},{18,... | collective-permute-start | bytes 1474568 | tf_op jit(solution)/shard_map/ppermute | solution.py:401
  15.2 2.7 %inject.1.extra = f32[8,24,64,128]{3,2,1,0:T(8,128)S(1)} custom-call(s32[1,128]{1,0:T(1,128)S(1)} %copy-done.11, f32[8,128]{1,0:T(8,128)S(1)} %bitcast.15), custom_call_target="tpu_custom_call" | custom-call | flops 1207959552 | bytes 6291456 | tf_op jit(solution)/shard_map/inject/pallas_call | solution.py:364
  17.9 5.5 %forward.1 = (f32[8,64,128]{2,1,0:T(8,128)S(1)}, f32[8,64,128]{2,1,0:T(8,128)S(1)}, f32[8,8,64,128]{3,2,1,0:T(8,128)S(1)}, f32[1,64,128]{2,1,0:T(8,128)S(1)}, f32[1,64,128]{2,1,0:T(8,128)S(1)}) custom-call(f32[1,8]{1,0:T(1,128)S(1)} %copy-done.12, s32[1]{0:T(128)S(6)} %copy.12.src_index, f32[8,64,128]{2,1,0:T(8,128)S(1)} %copy-done.1, ...), custom_call_target="tpu_custom_call" | custom-call | flops 15728640 | bytes 5242880 | tf_op jit(solution)/shard_map/forward/pallas_call | solution.py:364
  23.5 5.7 %adjoint.1 = (f32[8,64,128]{2,1,0:T(8,128)}, f32[128,128]{1,0:T(8,128)S(1)}, f32[128,128]{1,0:T(8,128)S(1)}, f32[128,128]{1,0:T(8,128)S(1)}, f32[128,128]{1,0:T(8,128)S(1)}) custom-call(f32[8,64,128]{2,1,0:T(8,128)S(1)} %copy-done.1, f32[8,64,128]{2,1,0:T(8,128)S(1)} %bitcast.8, f32[8,64,128]{2,1,0:T(8,128)S(1)} %bitcast.10, ...), custom_call_target="tpu_custom_call" | custom-call | flops 18874368 | bytes 10485760 | tf_op jit(solution)/shard_map/adjoint/pallas_call | solution.py:364
  29.2 1.5 %collective-permute-start.4 = (f32[128,128]{1,0:T(8,128)S(1)}, f32[128,128]{1,0:T(8,128)S(1)}, u32[]{:S(2)}, u32[]{:S(2)}) collective-permute-start(f32[128,128]{1,0:T(8,128)S(1)} %get-tuple-element.25), channel_id=1, source_target_pairs={{0,4},{4,0},{8,12},{12,8},{1,5},{5,1},{9,13},{13,9},{2,6},{6,2},{1... | collective-permute-start | bytes 196616 | tf_op jit(solution)/shard_map/ppermute | solution.py:438
  30.8 2.6 %collective-permute-start.5 = (f32[128,128]{1,0:T(8,128)S(1)}, f32[128,128]{1,0:T(8,128)S(1)}, u32[]{:S(2)}, u32[]{:S(2)}) collective-permute-start(f32[128,128]{1,0:T(8,128)S(1)} %get-tuple-element.26), channel_id=1, source_target_pairs={{0,8},{4,12},{8,0},{12,4},{1,9},{5,13},{9,1},{13,5},{2,10},{6,14},... | collective-permute-start | bytes 196616 | tf_op jit(solution)/shard_map/ppermute | solution.py:438
  33.6 4.0 %collective-permute-done.5.refs_2_ = f32[128,128]{1,0:T(8,128)S(1)} collective-permute-done((f32[128,128]{1,0:T(8,128)S(1)}, f32[128,128]{1,0:T(8,128)S(1)}, u32[]{:S(2)}, u32[]{:S(2)}) %collective-permute-start.5) | collective-permute-done | bytes 65568 | tf_op jit(solution)/shard_map/ppermute | solution.py:438
  37.7 2.2 %collective-permute-done.6.refs_3_ = f32[128,128]{1,0:T(8,128)S(1)} collective-permute-done((f32[128,128]{1,0:T(8,128)S(1)}, f32[128,128]{1,0:T(8,128)S(1)}, u32[]{:S(2)}, u32[]{:S(2)}) %collective-permute-start.6) | collective-permute-done | bytes 65568 | tf_op jit(solution)/shard_map/ppermute | solution.py:438
  39.9 1.2 %collective-permute-start.9 = (f32[136,128]{1,0:T(8,128)S(1)}, f32[136,128]{1,0:T(8,128)S(1)}, u32[]{:S(2)}, u32[]{:S(2)}) collective-permute-start(f32[136,128]{1,0:T(8,128)S(1)} %total.1.refs_0_), channel_id=1, source_target_pairs={{0,12},{4,8},{8,4},{12,0},{1,13},{5,9},{9,5},{13,1},{2,14},{6,10},... | collective-permute-start | bytes 208904 | tf_op jit(solution)/shard_map/ppermute | solution.py:443
  41.1 1.5 %collective-permute-start.8 = (f32[136,128]{1,0:T(8,128)S(1)}, f32[136,128]{1,0:T(8,128)S(1)}, u32[]{:S(2)}, u32[]{:S(2)}) collective-permute-start(f32[136,128]{1,0:T(8,128)S(1)} %total.1.refs_0_), channel_id=1, source_target_pairs={{0,8},{4,12},{8,0},{12,4},{1,9},{5,13},{9,1},{13,5},{2,10},{6,14},... | collective-permute-start | bytes 208904 | tf_op jit(solution)/shard_map/ppermute | solution.py:443
  42.6 1.8 %collective-permute-start.7 = (f32[136,128]{1,0:T(8,128)S(1)}, f32[136,128]{1,0:T(8,128)S(1)}, u32[]{:S(2)}, u32[]{:S(2)}) collective-permute-start(f32[136,128]{1,0:T(8,128)S(1)} %total.1.refs_0_), channel_id=1, source_target_pairs={{0,4},{4,0},{8,12},{12,8},{1,5},{5,1},{9,13},{13,9},{2,6},{6,2},{1... | collective-permute-start | bytes 208904 | tf_op jit(solution)/shard_map/ppermute | solution.py:443
  45.0 1.6 %collective-permute-done.9.refs_3_ = f32[136,128]{1,0:T(8,128)S(1)} collective-permute-done((f32[136,128]{1,0:T(8,128)S(1)}, f32[136,128]{1,0:T(8,128)S(1)}, u32[]{:S(2)}, u32[]{:S(2)}) %collective-permute-start.9) | collective-permute-done | bytes 69664 | tf_op jit(solution)/shard_map/ppermute | solution.py:443
  46.6 2.7 %collective-permute-done.8.refs_2_ = f32[136,128]{1,0:T(8,128)S(1)} collective-permute-done((f32[136,128]{1,0:T(8,128)S(1)}, f32[136,128]{1,0:T(8,128)S(1)}, u32[]{:S(2)}, u32[]{:S(2)}) %collective-permute-start.8) | collective-permute-done | bytes 69664 | tf_op jit(solution)/shard_map/ppermute | solution.py:443
  49.4 1.5 %collective-permute-start.11 = (f32[8,128]{1,0:T(8,128)S(1)}, f32[8,128]{1,0:T(8,128)S(1)}, u32[]{:S(2)}, u32[]{:S(2)}) collective-permute-start(f32[8,128]{1,0:T(8,128)S(1)} %top.1.refs_4_), channel_id=1, source_target_pairs={{0,2},{1,3},{2,0},{3,1},{4,6},{5,7},{6,4},{7,5},{8,10},{9,11},{10,... | collective-permute-start | bytes 12296 | tf_op jit(solution)/shard_map/ppermute | solution.py:447
  51.3 1.2 %collective-permute-done.12.refs_7_ = f32[8,128]{1,0:T(8,128)S(1)} collective-permute-done((f32[8,128]{1,0:T(8,128)S(1)}, f32[8,128]{1,0:T(8,128)S(1)}, u32[]{:S(2)}, u32[]{:S(2)}) %collective-permute-start.12) | collective-permute-done | bytes 4128 | tf_op jit(solution)/shard_map/ppermute | solution.py:447
  53.1 1.2 %update.1 = (f32[8,64,128]{2,1,0:T(8,128)}, f32[8,64,128]{2,1,0:T(8,128)}) custom-call(f32[136,128]{1,0:T(8,128)S(1)} %total.1.refs_0_, f32[136,128]{1,0:T(8,128)S(1)} %collective-permute-done.7.refs_1_, f32[136,128]{1,0:T(8,128)S(1)} %collective-permute-done.8.refs_2_, f32[136,128]{1,0:T(8,128)S(1)} %collective-permute-done.9.refs_3_, ...), custom_call_target="tpu_custom_call" | custom-call | flops 1310720 | bytes 1572864 | tf_op jit(solution)/shard_map/update/pallas_call | solution.py:364
  (40 shorter events, 4.7 us)
Async XLA Ops:
  0.6 17.3 %copy-start.12 = (f32[1,8]{1,0:T(1,128)S(1)}, f32[1,8]{1,0:T(1,128)}, u32[]{:S(2)}) copy-start(f32[1,8]{1,0:T(1,128)} %wavelet.1) | copy-start | bytes 100
  0.6 1.0 %copy-start = (f32[8,64,128]{2,1,0:T(8,128)S(1)}, f32[8,64,128]{2,1,0:T(8,128)}, u32[]{:S(2)}) copy-start(f32[8,64,128]{2,1,0:T(8,128)} %refs_8_.1) | copy-start | bytes 786436
  1.6 0.9 %copy-start.6 = (f32[1,8,64,128]{3,2,1,0:T(8,128)S(1)}, f32[1,8,64,128]{3,2,1,0:T(8,128)}, u32[]{:S(2)}) copy-start(f32[1,8,64,128]{3,2,1,0:T(8,128)} %param.10) | copy-start | bytes 786436
  3.5 14.4 %copy-start.1 = (f32[8,64,128]{2,1,0:T(8,128)S(1)}, f32[8,64,128]{2,1,0:T(8,128)}, u32[]{:S(2)}) copy-start(f32[8,64,128]{2,1,0:T(8,128)} %refs_8_.1) | copy-start | bytes 786436
  3.5 20.0 %copy-start.3 = (f32[1,8,64,128]{3,2,1,0:T(8,128)S(1)}, f32[1,8,64,128]{3,2,1,0:T(8,128)}, u32[]{:S(2)}) copy-start(f32[1,8,64,128]{3,2,1,0:T(8,128)} %param.12) | copy-start | bytes 786436
  3.5 20.0 %copy-start.5 = (f32[1,8,64,128]{3,2,1,0:T(8,128)S(1)}, f32[1,8,64,128]{3,2,1,0:T(8,128)}, u32[]{:S(2)}) copy-start(f32[1,8,64,128]{3,2,1,0:T(8,128)} %param.13) | copy-start | bytes 786436
  4.8 13.1 %collective-permute-start = (f32[22,64,128]{2,1,0:T(8,128)S(1)}, f32[22,64,128]{2,1,0:T(8,128)S(1)}, u32[]{:S(2)}, u32[]{:S(2)}) collective-permute-start(f32[22,64,128]{2,1,0:T(8,128)S(1)} %get-tuple-element.19), channel_id=1, source_target_pairs={{0,1},{2,3},{1,0},{3,2},{4,5},{6,7},{5,4},{7,6},{8,9},{10,11},{9,8... | collective-permute-start | bytes 2162696 | tf_op jit(solution)/shard_map/ppermute | solution.py:399
  5.3 12.5 %collective-permute-start.1 = (f32[22,64,128]{2,1,0:T(8,128)S(1)}, f32[22,64,128]{2,1,0:T(8,128)S(1)}, u32[]{:S(2)}, u32[]{:S(2)}) collective-permute-start(f32[22,64,128]{2,1,0:T(8,128)S(1)} %get-tuple-element.20), channel_id=1, source_target_pairs={{1,2},{2,1},{5,6},{6,5},{9,10},{10,9},{13,14},{14,13},{17,18},{18,... | collective-permute-start | bytes 2162696 | tf_op jit(solution)/shard_map/ppermute | solution.py:398
  6.0 1.0 %copy-start.2 = (f32[1,8,64,128]{3,2,1,0:T(8,128)S(1)}, f32[1,8,64,128]{3,2,1,0:T(8,128)}, u32[]{:S(2)}) copy-start(f32[1,8,64,128]{3,2,1,0:T(8,128)} %param.12) | copy-start | bytes 786436
  8.0 10.0 %copy-start.7 = (f32[1,8,64,128]{3,2,1,0:T(8,128)S(1)}, f32[1,8,64,128]{3,2,1,0:T(8,128)}, u32[]{:S(2)}) copy-start(f32[1,8,64,128]{3,2,1,0:T(8,128)} %param.10) | copy-start | bytes 786436
  8.0 10.0 %copy-start.9 = (f32[1,8,64,128]{3,2,1,0:T(8,128)S(1)}, f32[1,8,64,128]{3,2,1,0:T(8,128)}, u32[]{:S(2)}) copy-start(f32[1,8,64,128]{3,2,1,0:T(8,128)} %param.11) | copy-start | bytes 786436
  8.6 14.8 %collective-permute-start.2 = (f32[15,64,128]{2,1,0:T(8,128)S(1)}, f32[15,64,128]{2,1,0:T(8,128)S(1)}, u32[]{:S(2)}, u32[]{:S(2)}) collective-permute-start(f32[15,64,128]{2,1,0:T(8,128)S(1)} %get-tuple-element.21), channel_id=1, source_target_pairs={{0,1},{2,3},{1,0},{3,2},{4,5},{6,7},{5,4},{7,6},{8,9},{10,11},{9,8... | collective-permute-start | bytes 1474568 | tf_op jit(solution)/shard_map/ppermute | solution.py:402
  12.5 10.9 %collective-permute-start.3 = (f32[15,64,128]{2,1,0:T(8,128)S(1)}, f32[15,64,128]{2,1,0:T(8,128)S(1)}, u32[]{:S(2)}, u32[]{:S(2)}) collective-permute-start(f32[15,64,128]{2,1,0:T(8,128)S(1)} %get-tuple-element.22), channel_id=1, source_target_pairs={{1,2},{2,1},{5,6},{6,5},{9,10},{10,9},{13,14},{14,13},{17,18},{18,... | collective-permute-start | bytes 1474568 | tf_op jit(solution)/shard_map/ppermute | solution.py:401
  29.2 4.4 %collective-permute-start.4 = (f32[128,128]{1,0:T(8,128)S(1)}, f32[128,128]{1,0:T(8,128)S(1)}, u32[]{:S(2)}, u32[]{:S(2)}) collective-permute-start(f32[128,128]{1,0:T(8,128)S(1)} %get-tuple-element.25), channel_id=1, source_target_pairs={{0,4},{4,0},{8,12},{12,8},{1,5},{5,1},{9,13},{13,9},{2,6},{6,2},{1... | collective-permute-start | bytes 196616 | tf_op jit(solution)/shard_map/ppermute | solution.py:438
  30.8 6.9 %collective-permute-start.5 = (f32[128,128]{1,0:T(8,128)S(1)}, f32[128,128]{1,0:T(8,128)S(1)}, u32[]{:S(2)}, u32[]{:S(2)}) collective-permute-start(f32[128,128]{1,0:T(8,128)S(1)} %get-tuple-element.26), channel_id=1, source_target_pairs={{0,8},{4,12},{8,0},{12,4},{1,9},{5,13},{9,1},{13,5},{2,10},{6,14},... | collective-permute-start | bytes 196616 | tf_op jit(solution)/shard_map/ppermute | solution.py:438
  33.3 6.5 %collective-permute-start.6 = (f32[128,128]{1,0:T(8,128)S(1)}, f32[128,128]{1,0:T(8,128)S(1)}, u32[]{:S(2)}, u32[]{:S(2)}) collective-permute-start(f32[128,128]{1,0:T(8,128)S(1)} %get-tuple-element.27), channel_id=1, source_target_pairs={{0,12},{4,8},{8,4},{12,0},{1,13},{5,9},{9,5},{13,1},{2,14},{6,10},... | collective-permute-start | bytes 196616 | tf_op jit(solution)/shard_map/ppermute | solution.py:438
  39.9 6.7 %collective-permute-start.9 = (f32[136,128]{1,0:T(8,128)S(1)}, f32[136,128]{1,0:T(8,128)S(1)}, u32[]{:S(2)}, u32[]{:S(2)}) collective-permute-start(f32[136,128]{1,0:T(8,128)S(1)} %total.1.refs_0_), channel_id=1, source_target_pairs={{0,12},{4,8},{8,4},{12,0},{1,13},{5,9},{9,5},{13,1},{2,14},{6,10},... | collective-permute-start | bytes 208904 | tf_op jit(solution)/shard_map/ppermute | solution.py:443
  41.1 8.3 %collective-permute-start.8 = (f32[136,128]{1,0:T(8,128)S(1)}, f32[136,128]{1,0:T(8,128)S(1)}, u32[]{:S(2)}, u32[]{:S(2)}) collective-permute-start(f32[136,128]{1,0:T(8,128)S(1)} %total.1.refs_0_), channel_id=1, source_target_pairs={{0,8},{4,12},{8,0},{12,4},{1,9},{5,13},{9,1},{13,5},{2,10},{6,14},... | collective-permute-start | bytes 208904 | tf_op jit(solution)/shard_map/ppermute | solution.py:443
  42.6 6.8 %collective-permute-start.7 = (f32[136,128]{1,0:T(8,128)S(1)}, f32[136,128]{1,0:T(8,128)S(1)}, u32[]{:S(2)}, u32[]{:S(2)}) collective-permute-start(f32[136,128]{1,0:T(8,128)S(1)} %total.1.refs_0_), channel_id=1, source_target_pairs={{0,4},{4,0},{8,12},{12,8},{1,5},{5,1},{9,13},{13,9},{2,6},{6,2},{1... | collective-permute-start | bytes 208904 | tf_op jit(solution)/shard_map/ppermute | solution.py:443
  44.3 6.9 %collective-permute-start.13 = (f32[1,64,128]{2,1,0:T(8,128)S(1)}, f32[1,64,128]{2,1,0:T(8,128)S(1)}, u32[]{:S(2)}, u32[]{:S(2)}) collective-permute-start(f32[1,64,128]{2,1,0:T(8,128)S(1)} %get-tuple-element.30), channel_id=1, source_target_pairs={{0,1},{2,3},{1,0},{3,2},{4,5},{6,7},{5,4},{7,6},{8,9},{10,11},{9,8... | collective-permute-start | bytes 98312 | tf_op jit(solution)/shard_map/ppermute | solution.py:425
  44.3 6.9 %collective-permute-start.14 = (f32[1,64,128]{2,1,0:T(8,128)S(1)}, f32[1,64,128]{2,1,0:T(8,128)S(1)}, u32[]{:S(2)}, u32[]{:S(2)}) collective-permute-start(f32[1,64,128]{2,1,0:T(8,128)S(1)} %get-tuple-element.31), channel_id=1, source_target_pairs={{1,2},{2,1},{5,6},{6,5},{9,10},{10,9},{13,14},{14,13},{17,18},{18,... | collective-permute-start | bytes 98312 | tf_op jit(solution)/shard_map/ppermute | solution.py:426
  49.4 3.1 %collective-permute-start.12 = (f32[8,128]{1,0:T(8,128)S(1)}, f32[8,128]{1,0:T(8,128)S(1)}, u32[]{:S(2)}, u32[]{:S(2)}) collective-permute-start(f32[8,128]{1,0:T(8,128)S(1)} %top.1.refs_4_), channel_id=1, source_target_pairs={{0,3},{1,2},{2,1},{3,0},{4,7},{5,6},{6,5},{7,4},{8,11},{9,10},{10,... | collective-permute-start | bytes 12296 | tf_op jit(solution)/shard_map/ppermute | solution.py:447
  49.4 3.7 %collective-permute-start.11 = (f32[8,128]{1,0:T(8,128)S(1)}, f32[8,128]{1,0:T(8,128)S(1)}, u32[]{:S(2)}, u32[]{:S(2)}) collective-permute-start(f32[8,128]{1,0:T(8,128)S(1)} %top.1.refs_4_), channel_id=1, source_target_pairs={{0,2},{1,3},{2,0},{3,1},{4,6},{5,7},{6,4},{7,5},{8,10},{9,11},{10,... | collective-permute-start | bytes 12296 | tf_op jit(solution)/shard_map/ppermute | solution.py:447
  50.9 2.2 %collective-permute-start.10 = (f32[8,128]{1,0:T(8,128)S(1)}, f32[8,128]{1,0:T(8,128)S(1)}, u32[]{:S(2)}, u32[]{:S(2)}) collective-permute-start(f32[8,128]{1,0:T(8,128)S(1)} %top.1.refs_4_), channel_id=1, source_target_pairs={{0,1},{1,0},{2,3},{3,2},{4,5},{5,4},{6,7},{7,6},{8,9},{9,8},{10,11... | collective-permute-start | bytes 12296 | tf_op jit(solution)/shard_map/ppermute | solution.py:447
  (4 other events, 3.2 us)

commit v3 on v2

v3 whole, which is shorter than its diff:
```python
import functools

import jax
import jax.numpy as jnp
from jax import lax
from jax.experimental import pallas as pl
from jax.experimental.pallas import tpu as pltpu
from jax.sharding import PartitionSpec as P

ITERS = 8
REACH = 4
GUARD = 8
LANES = 128
LIMIT = 16 * 2**20
VMEM = pltpu.VMEM
SMEM = pltpu.SMEM
HBM = pl.ANY


def pairs(count, start):
    low = [(i, i + 1) for i in range(start, count - 1, 2)]
    return low + [(b, a) for a, b in low]


def partner_perms(count):
    if count & (count - 1) == 0:
        return {m: [(i, i ^ m) for i in range(count)] for m in range(1, count)}
    return {m: [(i, (i + m) % count) for i in range(count)] for m in range(1, count)}


def far_first(count):
    half = count // 2
    return [*range(half, count), *range(1, half)]


def send_slot(me, m, count):
    return me ^ m if count & (count - 1) == 0 else lax.rem(me + m, count)


def from_slot(me, m, count):
    return me ^ m if count & (count - 1) == 0 else lax.rem(me - m + count, count)


def spec(space):
    return pl.BlockSpec(memory_space=space)


def cost(flops, nbytes):
    return pl.CostEstimate(flops=int(flops), bytes_accessed=int(nbytes), transcendentals=0)


def is_even():
    return lax.rem(lax.axis_index("slab"), 2) == 0


def pack_kernel(depth, *refs):
    *fields, to_a, to_b, sem = refs

    def copies(up_a, up_b):
        out = []
        for j, (dst, up) in enumerate(((to_a, up_a), (to_b, up_b))):
            at = 0
            for i, field in enumerate(fields):
                size = REACH if i == 0 else REACH - 1
                out.append(
                    pltpu.make_async_copy(
                        field.at[pl.ds(depth - size if up else 0, size)],
                        dst.at[pl.ds(at, size)],
                        sem.at[j, i],
                    )
                )
                at += size
        return out

    even = is_even()

    @pl.when(even)
    def _():
        for c in copies(True, False):
            c.start()

    @pl.when(jnp.logical_not(even))
    def _():
        for c in copies(False, True):
            c.start()

    for c in copies(False, False):
        c.wait()


def inject_kernel(depth, width, rec_ref, misfit_ref, out_ref, left, right):
    rows = left.shape[0]
    base = (lax.axis_index("slab") * depth - REACH) * width
    index = rec_ref[...]
    row_of = index // LANES
    lane_of = index - row_of * LANES
    row_of = row_of - base
    group = 2 * width
    for first in range(0, rows, group):
        at = lax.broadcasted_iota(jnp.int32, (group, LANES), 0) + first
        hot = jnp.where(at == row_of, 1.0, 0.0).astype(jnp.bfloat16)
        for part in range(3):
            left[pl.ds(first, group), pl.ds(part * LANES, LANES)] = hot
    lane = lax.broadcasted_iota(jnp.int32, (LANES, LANES), 0)
    mine = lane == lane_of
    for k in range(ITERS):
        value = misfit_ref[pl.ds(k, 1), :]
        for part in range(3):
            piece = value.astype(jnp.bfloat16).astype(jnp.float32)
            value = value - piece
            right[pl.ds(k * LANES, LANES), pl.ds(part * LANES, LANES)] = jnp.where(
                mine, piece, 0.0
            ).astype(jnp.bfloat16)

    def pair(j, carry):
        cols = right[pl.ds(pl.multiple_of(j * 2 * LANES, 2 * LANES), 2 * LANES), :]
        both = lax.dot_general(
            left[...], cols, (((1,), (1,)), ((), ())), preferred_element_type=jnp.float32
        )
        out_ref[2 * j] = both[:, :LANES].reshape(out_ref.shape[1:])
        out_ref[2 * j + 1] = both[:, LANES:].reshape(out_ref.shape[1:])
        return carry

    lax.fori_loop(0, ITERS // 2, pair, 0)


def neighbours(src, p, r, first, last):
    c = src[p, pl.ds(r, 8), :]
    s = src[p + 1, pl.ds(r, 8), :] + src[p - 1, pl.ds(r, 8), :]
    s = s + src[p, pl.ds(r + 1, 8), :]
    s = s + src[p, pl.ds(r - 1, 8), :]
    s = s + jnp.where(last, 0.0, pltpu.roll(c, LANES - 1, 1))
    s = s + jnp.where(first, 0.0, pltpu.roll(c, 1, 1))
    return c, s


def edges():
    lane = lax.broadcasted_iota(jnp.int32, (8, LANES), 1)
    return lane == 0, lane == LANES - 1


def clear_guards(field):
    planes, rows, _ = field.shape
    zero = jnp.zeros((GUARD, LANES), jnp.float32)
    for p in range(planes):
        field[p, pl.ds(0, GUARD), :] = zero
        field[p, pl.ds(rows - GUARD, GUARD), :] = zero


def halo_sides(a_in, b_in, put):
    even = is_even()

    @pl.when(even)
    def _():
        put(b_in, a_in)

    @pl.when(jnp.logical_not(even))
    def _():
        put(a_in, b_in)


def fill(depth, width, now, later, cur, old):
    rows = pl.ds(GUARD, width)
    for p in range(depth):
        cur[REACH + p, rows, :] = now[p]
        old[REACH + p, rows, :] = later[p]

    def put(low, high):
        for p in range(REACH):
            cur[p, rows, :] = low[p]
            cur[REACH + depth + p, rows, :] = high[p]
        for p in range(REACH - 1):
            old[1 + p, rows, :] = low[REACH + p]
            old[REACH + depth + p, rows, :] = high[REACH + p]

    return put


def send(depth, width, u, u_later, to_a, to_b):
    even = is_even()
    rows = pl.ds(GUARD, width)
    for out, up in ((to_a, even), (to_b, jnp.logical_not(even))):
        for p in range(REACH):
            out[p] = u[jnp.where(up, depth, REACH) + p, rows, :]
        for p in range(REACH - 1):
            out[REACH + p] = u_later[jnp.where(up, depth + 1, REACH) + p, rows, :]


def blocks(depth, width, j):
    for p in range(j + 1, depth + 2 * REACH - 1 - j):
        for r in range(0, width, 8):
            yield p, r, REACH <= p < REACH + depth


def forward_kernel(depth, width, stage, *refs):
    wavelet, src_index, now, later, a_in, b_in = refs[:6]
    if stage == 0:
        model, u_out, later_out, lap_out, to_a, to_b, mod, weight, cur, old = refs[6:]
    else:
        mod, u_out, base_out, lap_out, to_a, to_b, cur, old = refs[6:]
    clear_guards(cur)
    clear_guards(old)
    put = fill(depth, width, now, later, cur, old)
    if stage == 0:
        n = REACH - 1

        def put_all(low, high):
            put(low, high)
            for p in range(n):
                mod[1 + p] = low[REACH + n + p]
                mod[REACH + depth + p] = high[REACH + n + p]

        halo_sides(a_in, b_in, put_all)
        for p in range(depth):
            mod[REACH + p] = model[p]
        for p in range(1, depth + 2 * REACH - 1):
            weight[p] = 2.0 - 6.0 * mod[p]
    else:
        halo_sides(a_in, b_in, put)
    first, last = edges()
    source = src_index[0]
    src_row = source // LANES
    src_lane = source - src_row * LANES
    src_row = src_row - (lax.axis_index("slab") * depth - REACH) * width
    bufs = (cur, old)
    for j in range(REACH):
        s, d = bufs[j % 2], bufs[(j + 1) % 2]
        for p, r, own in blocks(depth, width, j):
            c, around = neighbours(s, p, GUARD + r, first, last)
            lap = around - 6.0 * c
            here = (p, pl.ds(GUARD + r, 8), slice(None))
            d[here] = 2.0 * c - d[here] + mod[p, pl.ds(r, 8), :] * lap
            if own:
                lap_out[j, p - REACH, pl.ds(r, 8), :] = lap

        @pl.when((src_row >= (j + 1) * width) & (src_row < (depth + 2 * REACH - 1 - j) * width))
        def _():
            plane = src_row // width
            here = (plane, pl.ds(GUARD + src_row - plane * width, 1), slice(None))
            at = lax.broadcasted_iota(jnp.int32, (1, LANES), 1) == src_lane
            d[here] = d[here] + jnp.where(at, wavelet[0, stage * REACH + j], 0.0)

    u, u_later = bufs[REACH % 2], bufs[(REACH + 1) % 2]
    rows = pl.ds(GUARD, width)
    if stage == 0:
        send(depth, width, u, u_later, to_a, to_b)
        for p in range(depth):
            u_out[p] = u[REACH + p, rows, :]
            later_out[p] = u_later[REACH + p, rows, :]
    else:
        even = is_even()
        to_a[0] = u[jnp.where(even, REACH + depth - 1, REACH), rows, :]
        to_b[0] = u[jnp.where(even, REACH, REACH + depth - 1), rows, :]
        for p in range(depth):
            c = u[REACH + p, rows, :]
            u_out[p] = c
            base_out[p] = 2.0 * c - u_later[REACH + p, rows, :]


def adjoint_kernel(depth, width, shots, stage, *refs):
    now, later, a_in, b_in, mod, weight, laps, extra = refs[:8]
    if stage == 0:
        a_out, later_out, image, to_a, to_b, cur, old = refs[8:]
    else:
        so_far, a_out, *pieces, image, cur, old = refs[8:]
    clear_guards(cur)
    clear_guards(old)
    halo_sides(a_in, b_in, fill(depth, width, now, later, cur, old))
    first, last = edges()
    bufs = (cur, old)
    for j in range(REACH):
        s, d = bufs[j % 2], bufs[(j + 1) % 2]
        for p, r, own in blocks(depth, width, j):
            c, around = neighbours(s, p, GUARD + r, first, last)
            here = (p, pl.ds(GUARD + r, 8), slice(None))
            rows = pl.ds(r, 8)
            new = weight[p, rows, :] * c - d[here] + mod[p, rows, :] * around
            d[here] = new + extra[stage * REACH + j, p, rows, :]
            if own:
                q = p - REACH
                into = pl.ds(q * width + r, 8)
                add = c * laps[j, q, rows, :]
                if j > 0:
                    add = image[into, :] + add
                elif stage > 0:
                    add = so_far[into, :] + add
                image[into, :] = add

    a, a_later = bufs[REACH % 2], bufs[(REACH + 1) % 2]
    rows = pl.ds(GUARD, width)
    for p in range(depth):
        a_out[p] = a[REACH + p, rows, :]
    if stage == 0:
        send(depth, width, a, a_later, to_a, to_b)
        for p in range(depth):
            later_out[p] = a_later[REACH + p, rows, :]
    else:
        n = depth * width // shots
        me = lax.axis_index("shot")
        for m in range(shots):
            to = me if m == 0 else send_slot(me, m, shots)
            pieces[m][...] = image[pl.ds(pl.multiple_of(to * n, n), n), :]


def sum_kernel(*refs):
    *parts, out = refs
    n = parts[0].shape[0]
    top = jnp.zeros((8, LANES), jnp.float32)
    for r in range(0, n, 8):
        total = parts[0][pl.ds(r, 8), :]
        for part in parts[1:]:
            total = total + part[pl.ds(r, 8), :]
        out[pl.ds(r, 8), :] = total
        top = jnp.maximum(top, jnp.abs(total))
    out[pl.ds(n, 8), :] = top


def top_kernel(*refs):
    *parts, out = refs
    n = parts[0].shape[0] - 8
    top = parts[0][pl.ds(n, 8), :]
    for part in parts[1:]:
        top = jnp.maximum(top, part[pl.ds(n, 8), :])
    out[...] = top


def final_kernel(depth, width, shots, slabs, *refs):
    n = depth * width // shots
    grads, tops = refs[:shots], refs[shots : shots + slabs]
    model, u, base, a_edge, b_edge, new_model, stepped, pad, grad = refs[shots + slabs :]
    even = lax.rem(lax.axis_index("slab"), 2) == 0
    me = lax.axis_index("shot")
    rows = pl.ds(GUARD, width)
    clear_guards(pad)
    low, high = jnp.where(even, 0, depth + 1), jnp.where(even, depth + 1, 0)
    pad[low, rows, :] = b_edge[0]
    pad[high, rows, :] = a_edge[0]

    def place(p, carry):
        pad[p + 1, rows, :] = u[p]
        return carry

    lax.fori_loop(0, depth, place, 0)
    for m in range(shots):
        owner = me if m == 0 else from_slot(me, m, shots)
        grad[pl.ds(pl.multiple_of(owner * n, n), n), :] = grads[m][pl.ds(0, n), :]
    top = tops[0][...]
    for other in tops[1:]:
        top = jnp.maximum(top, other[...])
    peak = jnp.max(top)
    first, last = edges()

    def planes(j, carry):
        for i in range(4):
            p = 4 * j + i
            for r in range(0, width, 8):
                g = grad[pl.ds(pl.multiple_of(p * width + r, 8), 8), :]
                new = jnp.clip(model[p, pl.ds(r, 8), :] - 0.1 * g / (peak + 1e-06), 0.05, 0.3)
                new_model[p, pl.ds(r, 8), :] = new
                c, around = neighbours(pad, p + 1, GUARD + r, first, last)
                lap = around - 6.0 * c
                stepped[p, pl.ds(r, 8), :] = base[p, pl.ds(r, 8), :] + new * lap
        return carry

    lax.fori_loop(0, depth // 4, planes, 0)


def placed(x, space):
    if space is VMEM or space is pltpu.HBM:
        return pltpu.with_memory_space_constraint(x, space)
    return x


def call(kernel, outs, args, spaces, scratch, flops, nbytes, name):
    args = [placed(x, space) for x, space in zip(args, spaces)]
    return pl.pallas_call(
        kernel,
        out_shape=outs,
        in_specs=[spec(space) for space in spaces],
        out_specs=[spec(VMEM)] * len(outs),
        scratch_shapes=scratch,
        cost_estimate=cost(flops, nbytes),
        compiler_params=pltpu.CompilerParams(vmem_limit_bytes=LIMIT),
        name=name,
    )(*args)


def per_device(model, fwd_now, fwd_next, adj_now, adj_next, wavelet, misfit, src_index, rec_index):
    f32 = jnp.float32
    depth, width, length = model.shape
    assert length == LANES and fwd_now.shape[0] == 1 and width % 8 == 0 and depth >= REACH
    assert ITERS == 2 * REACH and REACH % 2 == 0
    u0, u1, a0, a1 = fwd_now[0], fwd_next[0], adj_now[0], adj_next[0]
    slabs, shots = lax.axis_size("slab"), lax.axis_size("shot")
    perm_a, perm_b = pairs(slabs, 0), pairs(slabs, 1)
    planes = depth + 2 * REACH
    cells = depth * width * LANES
    own = VMEM((depth, width, LANES), f32)
    wide = VMEM((planes, width, LANES), f32)
    field = VMEM((planes, width + 2 * GUARD, LANES), f32)
    halo = VMEM((2 * REACH - 1, width, LANES), f32)
    edge = VMEM((1, width, LANES), f32)
    laps = VMEM((REACH, depth, width, LANES), f32)
    out = jax.ShapeDtypeStruct((depth, width, LANES), f32)

    def exchange(to_a, to_b):
        b = lax.ppermute(to_b, "slab", perm_b)
        return lax.ppermute(to_a, "slab", perm_a), b

    def packed(fields, name):
        size = REACH + (len(fields) - 1) * (REACH - 1)
        return call(
            functools.partial(pack_kernel, depth),
            [VMEM((size, width, LANES), f32)] * 2,
            fields, [pltpu.HBM] * len(fields), [pltpu.SemaphoreType.DMA((2, len(fields)))],
            0, 4 * 4 * size * width * LANES, name,
        )

    def forward(stage, args, outs, name):
        return call(
            functools.partial(forward_kernel, depth, width, stage), outs, (wavelet, src_index, *args),
            [SMEM] * 2 + [VMEM] * len(args), [field] * 2, 15 * REACH * 2 * cells, 40 * cells, name,
        )

    def adjoint(stage, args, outs, scratch, name):
        return call(
            functools.partial(adjoint_kernel, depth, width, shots, stage), outs, args,
            [VMEM] * len(args), scratch + [field] * 2, 18 * REACH * 2 * cells, 40 * cells, name,
        )

    fa, fb = exchange(*packed((u0, u1, model), "pack_forward"))
    ga, gb = exchange(*packed((a0, a1), "pack_adjoint"))
    (extra,) = call(
        functools.partial(inject_kernel, depth, width),
        [VMEM((ITERS, planes, width, LANES), f32)],
        (rec_index, misfit[0]), (VMEM, VMEM),
        [
            VMEM((planes * width, 3 * LANES), jnp.bfloat16),
            VMEM((ITERS * LANES, 3 * LANES), jnp.bfloat16),
        ],
        2 * planes * width * 3 * LANES * ITERS * LANES, 4 * ITERS * planes * width * LANES, "inject",
    )

    u, u_later, lap, *to, mod, weight = forward(
        0, (u0, u1, fa, fb, model), [own, own, laps, halo, halo, wide, wide], "forward_first"
    )
    fa, fb = exchange(*to)
    image = VMEM((depth * width, LANES), f32)
    a, a_later, so_far, *to = adjoint(
        0, (a0, a1, ga, gb, mod, weight, lap, extra), [own, own, image, halo, halo], [], "adjoint_first"
    )
    ga, gb = exchange(*to)
    u, base, lap, *to = forward(
        1, (u, u_later, fa, fb, mod), [own, own, laps, edge, edge], "forward_second"
    )
    a_edge, b_edge = exchange(*to)
    n = depth * width // shots
    a, *pieces = adjoint(
        1, (a, a_later, ga, gb, mod, weight, lap, extra, so_far),
        [out] + [VMEM((n, LANES), f32)] * shots, [image], "adjoint_second",
    )

    perms = partner_perms(shots)
    order = far_first(shots)

    def with_others(own_one, pieces):
        got = {m: lax.ppermute(pieces[m], "shot", perms[m]) for m in order}
        return [own_one] + [got[m] for m in range(1, shots)]

    parts = with_others(pieces[0], pieces)
    (grad,) = call(
        sum_kernel, [VMEM((n + 8, LANES), f32)], parts, [VMEM] * shots, [],
        shots * n * LANES, 4 * shots * n * LANES, "total",
    )
    grads = with_others(grad, [grad] * shots)
    (top,) = call(
        top_kernel, [VMEM((8, LANES), f32)], grads, [VMEM] * shots, [], 0, 4096 * shots, "top"
    )
    tops = [top] + [lax.ppermute(top, "slab", q) for q in partner_perms(slabs).values()]

    new_model, stepped = call(
        functools.partial(final_kernel, depth, width, shots, slabs),
        [out, out],
        (*grads, *tops, model, u, base, a_edge, b_edge), [VMEM] * (shots + slabs + 5),
        [VMEM((depth + 2, width + 2 * GUARD, LANES), f32), VMEM((depth * width, LANES), f32)],
        20 * cells, 4 * 6 * cells, "update",
    )
    return new_model, stepped[None], a[None]


def solution(mesh):
    in_specs = (
        P(("groups", "slab"), None, None),
        P(("groups", "shot"), "slab", None, None),
        P(("groups", "shot"), "slab", None, None),
        P(("groups", "shot"), "slab", None, None),
        P(("groups", "shot"), "slab", None, None),
        P(("groups", "shot"), None),
        P(("groups", "shot"), None, None),
        P(("groups", "shot")),
        P(("groups", "shot"), None),
    )
    out_specs = (
        P(("groups", "slab"), None, None),
        P(("groups", "shot"), "slab", None, None),
        P(("groups", "shot"), "slab", None, None),
    )
    return jax.shard_map(
        per_device, mesh=mesh, in_specs=in_specs, out_specs=out_specs, check_vma=False
    )
```

time: 54.6 us -> 54.6 us (level)
  starting transfers between devices: 17.2 us -> 27.9 us
  local copies, waits for them, and re-layouts: 6.1 us -> 1.37 us
  Pallas kernels: 17.1 us -> 12.6 us
  waiting for transfers between devices: 12.4 us -> 10.8 us
    ppermute x15 -> x19, starting transfers between devices: 17.2 us -> 27.9 us  [the longest x5 10.4 us: exchange(): return (lax.ppermute(to_a, 'slab', perm_a), b)]
    unnamed x26 -> x16, local copies, waits for them, and re-layouts: 6.1 us -> 1.37 us
    pallas_call x8 -> x10, Pallas kernels: 17.1 us -> 12.6 us  [call(): pl.pallas_call(kernel, out_shape=outs, in_specs=[spec(space) for space in...]
    ppermute x15 -> x19, waiting for transfers between devices: 12.4 us -> 10.8 us  [the longest x6 7.95 us: with_others(): got = {m: lax.ppermute(pieces[m], 'shot', perms[m]) for m in order}]
  transfers between devices with their start and end apart: 15 -> 19, of which waited for: 6 -> 5; matrix products, arithmetic and copies ran while one was open for 0% -> 0% of each run, Pallas kernels for 16% -> 15%
where the time goes in v3:
time: 54.6 us; the launch traced here: 54.3 us
  starting transfers between devices  27.9 us (51%)
  Pallas kernels  12.6 us (23%)
  waiting for transfers between devices  10.8 us (20%)
  between operations  1.56 us (3%)
  local copies, waits for them, and re-layouts  1.37 us (3%)
    pallas_call x10, Pallas kernels, call(): pl.pallas_call(kernel, out_shape=outs, in_specs=[spec(space) for space in...  12.6 us
    ppermute x5, starting transfers between devices, exchange(): return (lax.ppermute(to_a, 'slab', perm_a), b)  10.4 us
    ppermute x6, starting transfers between devices, with_others(): got = {m: lax.ppermute(pieces[m], 'shot', perms[m]) for m in order}  8.83 us
    ppermute x6, waiting for transfers between devices, with_others(): got = {m: lax.ppermute(pieces[m], 'shot', perms[m]) for m in order}  7.95 us
    ppermute x3, starting transfers between devices, per_device(): lax.ppermute(top, 'slab', q)  5.4 us
    ppermute x5, starting transfers between devices, exchange(): b = lax.ppermute(to_b, 'slab', perm_b)  3.31 us
    ppermute x3, waiting for transfers between devices, per_device(): lax.ppermute(top, 'slab', q)  2.83 us
    unnamed x16, local copies, waits for them, and re-layouts  1.37 us
  transfers between devices with their start and end apart: 19, of which 5 were waited for; matrix products, arithmetic and copies ran while one was open for 0% of the time, Pallas kernels for 15%

profile of v3, /device:TPU:0, one launch (start us, length us, event | category | flops | bytes accessed | tf_op | source)
XLA Modules:
  0.0 54.3 jit_solution(17360740582992694146)
XLA Ops:
  0.7 1.3 %pack_forward.1 = (f32[10,64,128]{2,1,0:T(8,128)S(1)}, f32[10,64,128]{2,1,0:T(8,128)S(1)}) custom-call(f32[8,64,128]{2,1,0:T(8,128)} %bitcast.11, f32[8,64,128]{2,1,0:T(8,128)} %bitcast.13, f32[8,64,128]{2,1,0:T(8,128)} %refs_8_.1), custom_call_target="tpu_custom_call" | custom-call | bytes 1310720 | tf_op jit(solution)/shard_map/pack_forward/pallas_call | solution.py:376
  2.6 0.7 %collective-permute-start.3 = (f32[10,64,128]{2,1,0:T(8,128)S(1)}, f32[10,64,128]{2,1,0:T(8,128)S(1)}, u32[]{:S(2)}, u32[]{:S(2)}) collective-permute-start(f32[10,64,128]{2,1,0:T(8,128)S(1)} %get-tuple-element.34), channel_id=1, source_target_pairs={{1,2},{2,1},{5,6},{6,5},{9,10},{10,9},{13,14},{14,13},{17,18},{18,... | collective-permute-start | bytes 983048 | tf_op jit(solution)/shard_map/ppermute | solution.py:407
  3.3 1.1 %pack_adjoint.1 = (f32[7,64,128]{2,1,0:T(8,128)S(1)}, f32[7,64,128]{2,1,0:T(8,128)S(1)}) custom-call(f32[8,64,128]{2,1,0:T(8,128)} %bitcast.7, f32[8,64,128]{2,1,0:T(8,128)} %bitcast.9), custom_call_target="tpu_custom_call" | custom-call | bytes 917504 | tf_op jit(solution)/shard_map/pack_adjoint/pallas_call | solution.py:376
  4.4 3.9 %collective-permute-start = (f32[7,64,128]{2,1,0:T(8,128)S(1)}, f32[7,64,128]{2,1,0:T(8,128)S(1)}, u32[]{:S(2)}, u32[]{:S(2)}) collective-permute-start(f32[7,64,128]{2,1,0:T(8,128)S(1)} %get-tuple-element.31), channel_id=1, source_target_pairs={{0,1},{2,3},{1,0},{3,2},{4,5},{6,7},{5,4},{7,6},{8,9},{10,11},{9,8... | collective-permute-start | bytes 688136 | tf_op jit(solution)/shard_map/ppermute | solution.py:408
  9.6 0.7 %copy-done.5 = f32[1,8,128]{2,1,0:T(8,128)S(1)} copy-done((f32[1,8,128]{2,1,0:T(8,128)S(1)}, f32[1,8,128]{2,1,0:T(8,128)}, u32[]{:S(2)}) %copy-start.5) | copy-done | bytes 4120
  10.9 2.1 %inject.1.refs_7_ = f32[8,16,64,128]{3,2,1,0:T(8,128)S(1)} custom-call(s32[1,128]{1,0:T(1,128)S(1)} %copy-done.7, f32[8,128]{1,0:T(8,128)S(1)} %bitcast.15), custom_call_target="tpu_custom_call" | custom-call | flops 805306368 | bytes 4194304 | tf_op jit(solution)/shard_map/inject/pallas_call | solution.py:376
  13.1 1.8 %forward_first.1 = (f32[8,64,128]{2,1,0:T(8,128)S(1)}, f32[8,64,128]{2,1,0:T(8,128)S(1)}, f32[4,8,64,128]{3,2,1,0:T(8,128)S(1)}, f32[7,64,128]{2,1,0:T(8,128)S(1...) custom-call(f32[1,8]{1,0:T(1,128)S(1)} %copy-done.6, s32[1]{0:T(128)S(6)} %copy.12.refs_1_, ...), custom_call_target="tpu_custom_call" | custom-call | flops 7864320 | bytes 2621440 | tf_op jit(solution)/shard_map/forward_first/pallas_call | solution.py:376
  14.9 1.3 %collective-permute-start.6 = (f32[7,64,128]{2,1,0:T(8,128)S(1)}, f32[7,64,128]{2,1,0:T(8,128)S(1)}, u32[]{:S(2)}, u32[]{:S(2)}) collective-permute-start(f32[7,64,128]{2,1,0:T(8,128)S(1)} %get-tuple-element.44), channel_id=1, source_target_pairs={{0,1},{2,3},{1,0},{3,2},{4,5},{6,7},{5,4},{7,6},{8,9},{10,11},{9,8... | collective-permute-start | bytes 688136 | tf_op jit(solution)/shard_map/ppermute | solution.py:408
  17.0 1.3 %adjoint_first.1 = (f32[8,64,128]{2,1,0:T(8,128)S(1)}, f32[8,64,128]{2,1,0:T(8,128)S(1)}, f32[512,128]{1,0:T(8,128)S(1)}, f32[7,64,128]{2,1,0:T(8,128)S(1)}, f32[7,64,128]{2,1,0:T(8,128)S(1)}) custom-call(f32[8,64,128]{2,1,0:T(8,128)S(1)} %bitcast.8, f32[8,64,128]{2,1,0:T(8,128)S(1)} %bitcast.10, f32[7,64,128]{2,1,0:T(8,128)S(1)} %collective-permute-done.refs_2_, ...), custom_call_target="tpu_custom_call" | custom-call | flops 9437184 | bytes 2621440 | tf_op jit(solution)/shard_map/adjoint_first/pallas_call | solution.py:376
  18.3 3.1 %collective-permute-start.4 = (f32[7,64,128]{2,1,0:T(8,128)S(1)}, f32[7,64,128]{2,1,0:T(8,128)S(1)}, u32[]{:S(2)}, u32[]{:S(2)}) collective-permute-start(f32[7,64,128]{2,1,0:T(8,128)S(1)} %get-tuple-element.40), channel_id=1, source_target_pairs={{0,1},{2,3},{1,0},{3,2},{4,5},{6,7},{5,4},{7,6},{8,9},{10,11},{9,8... | collective-permute-start | bytes 688136 | tf_op jit(solution)/shard_map/ppermute | solution.py:408
  22.0 1.8 %forward_second.1 = (f32[8,64,128]{2,1,0:T(8,128)S(1)}, f32[8,64,128]{2,1,0:T(8,128)S(1)}, f32[4,8,64,128]{3,2,1,0:T(8,128)S(1)}, f32[1,64,128]{2,1,0:T(8,128)S(1)}, f32[1,64,128]{2,1,0:T(8,128)S(1)}) custom-call(f32[1,8]{1,0:T(1,128)S(1)} %copy-done.6, s32[1]{0:T(128)S(6)} %copy.12.refs_1_, f32[8,64,128]{2,1,0:T(8,128)S(1)} %get-tuple-element.42.refs_2_, ...), custom_call_target="tpu_custom_call" | custom-call | flops 7864320 | bytes 2621440 | tf_op jit(solution)/shard_map/forward_second/pallas_call | solution.py:376
  23.8 1.9 %adjoint_second.1 = (f32[8,64,128]{2,1,0:T(8,128)}, f32[128,128]{1,0:T(8,128)S(1)}, f32[128,128]{1,0:T(8,128)S(1)}, f32[128,128]{1,0:T(8,128)S(1)}, f32[128,128]{1,0:T(8,128)S(1)}) custom-call(f32[8,64,128]{2,1,0:T(8,128)S(1)} %get-tuple-element.38.refs_0_, f32[8,64,128]{2,1,0:T(8,128)S(1)} %get-tuple-element.39.refs_1_, ...), custom_call_target="tpu_custom_call" | custom-call | flops 9437184 | bytes 2621440 | tf_op jit(solution)/shard_map/adjoint_second/pallas_call | solution.py:376
  25.8 1.6 %collective-permute-start.8 = (f32[128,128]{1,0:T(8,128)S(1)}, f32[128,128]{1,0:T(8,128)S(1)}, u32[]{:S(2)}, u32[]{:S(2)}) collective-permute-start(f32[128,128]{1,0:T(8,128)S(1)} %get-tuple-element.49), channel_id=1, source_target_pairs={{0,4},{4,0},{8,12},{12,8},{1,5},{5,1},{9,13},{13,9},{2,6},{6,2},{1... | collective-permute-start | bytes 196616 | tf_op jit(solution)/shard_map/ppermute | solution.py:467
  27.3 2.6 %collective-permute-start.9 = (f32[128,128]{1,0:T(8,128)S(1)}, f32[128,128]{1,0:T(8,128)S(1)}, u32[]{:S(2)}, u32[]{:S(2)}) collective-permute-start(f32[128,128]{1,0:T(8,128)S(1)} %get-tuple-element.50), channel_id=1, source_target_pairs={{0,8},{4,12},{8,0},{12,4},{1,9},{5,13},{9,1},{13,5},{2,10},{6,14},... | collective-permute-start | bytes 196616 | tf_op jit(solution)/shard_map/ppermute | solution.py:467
  30.1 3.0 %collective-permute-done.9.refs_2_ = f32[128,128]{1,0:T(8,128)S(1)} collective-permute-done((f32[128,128]{1,0:T(8,128)S(1)}, f32[128,128]{1,0:T(8,128)S(1)}, u32[]{:S(2)}, u32[]{:S(2)}) %collective-permute-start.9) | collective-permute-done | bytes 65568 | tf_op jit(solution)/shard_map/ppermute | solution.py:467
  33.2 3.6 %collective-permute-done.10.refs_3_ = f32[128,128]{1,0:T(8,128)S(1)} collective-permute-done((f32[128,128]{1,0:T(8,128)S(1)}, f32[128,128]{1,0:T(8,128)S(1)}, u32[]{:S(2)}, u32[]{:S(2)}) %collective-permute-start.10) | collective-permute-done | bytes 65568 | tf_op jit(solution)/shard_map/ppermute | solution.py:467
  37.5 3.7 %collective-permute-start.13 = (f32[136,128]{1,0:T(8,128)S(1)}, f32[136,128]{1,0:T(8,128)S(1)}, u32[]{:S(2)}, u32[]{:S(2)}) collective-permute-start(f32[136,128]{1,0:T(8,128)S(1)} %total.1.refs_0_), channel_id=1, source_target_pairs={{0,12},{4,8},{8,4},{12,0},{1,13},{5,9},{9,5},{13,1},{2,14},{6,10},... | collective-permute-start | bytes 208904 | tf_op jit(solution)/shard_map/ppermute | solution.py:467
  41.3 1.5 %collective-permute-start.17 = (f32[1,64,128]{2,1,0:T(8,128)S(1)}, f32[1,64,128]{2,1,0:T(8,128)S(1)}, u32[]{:S(2)}, u32[]{:S(2)}) collective-permute-start(f32[1,64,128]{2,1,0:T(8,128)S(1)} %get-tuple-element.54), channel_id=1, source_target_pairs={{0,1},{2,3},{1,0},{3,2},{4,5},{6,7},{5,4},{7,6},{8,9},{10,11},{9,8... | collective-permute-start | bytes 98312 | tf_op jit(solution)/shard_map/ppermute | solution.py:408
  43.5 1.3 %collective-permute-done.13.refs_3_ = f32[136,128]{1,0:T(8,128)S(1)} collective-permute-done((f32[136,128]{1,0:T(8,128)S(1)}, f32[136,128]{1,0:T(8,128)S(1)}, u32[]{:S(2)}, u32[]{:S(2)}) %collective-permute-start.13) | collective-permute-done | bytes 69664 | tf_op jit(solution)/shard_map/ppermute | solution.py:467
  44.8 4.0 %collective-permute-start.14 = (f32[8,128]{1,0:T(8,128)S(1)}, f32[8,128]{1,0:T(8,128)S(1)}, u32[]{:S(2)}, u32[]{:S(2)}) collective-permute-start(f32[8,128]{1,0:T(8,128)S(1)} %top.1.refs_4_), channel_id=1, source_target_pairs={{0,1},{1,0},{2,3},{3,2},{4,5},{5,4},{6,7},{7,6},{8,9},{9,8},{10,11... | collective-permute-start | bytes 12296 | tf_op jit(solution)/shard_map/ppermute | solution.py:479
  48.8 1.2 %collective-permute-start.15 = (f32[8,128]{1,0:T(8,128)S(1)}, f32[8,128]{1,0:T(8,128)S(1)}, u32[]{:S(2)}, u32[]{:S(2)}) collective-permute-start(f32[8,128]{1,0:T(8,128)S(1)} %top.1.refs_4_), channel_id=1, source_target_pairs={{0,2},{1,3},{2,0},{3,1},{4,6},{5,7},{6,4},{7,5},{8,10},{9,11},{10,... | collective-permute-start | bytes 12296 | tf_op jit(solution)/shard_map/ppermute | solution.py:479
  50.2 2.2 %collective-permute-done.15.refs_6_ = f32[8,128]{1,0:T(8,128)S(1)} collective-permute-done((f32[8,128]{1,0:T(8,128)S(1)}, f32[8,128]{1,0:T(8,128)S(1)}, u32[]{:S(2)}, u32[]{:S(2)}) %collective-permute-start.15) | collective-permute-done | bytes 4128 | tf_op jit(solution)/shard_map/ppermute | solution.py:479
  52.4 0.7 %collective-permute-done.16.refs_7_ = f32[8,128]{1,0:T(8,128)S(1)} collective-permute-done((f32[8,128]{1,0:T(8,128)S(1)}, f32[8,128]{1,0:T(8,128)S(1)}, u32[]{:S(2)}, u32[]{:S(2)}) %collective-permute-start.16) | collective-permute-done | bytes 4128 | tf_op jit(solution)/shard_map/ppermute | solution.py:479
  53.0 1.2 %update.1 = (f32[8,64,128]{2,1,0:T(8,128)}, f32[8,64,128]{2,1,0:T(8,128)}) custom-call(f32[136,128]{1,0:T(8,128)S(1)} %total.1.refs_0_, f32[136,128]{1,0:T(8,128)S(1)} %collective-permute-done.11.refs_1_, f32[136,128]{1,0:T(8,128)S(1)} %collective-permute-done.12.refs_2_, f32[136,128]{1,0:T(8,128)S(1)} %collective-permute-done.13.refs_3_, ...), custom_call_target="tpu_custom_call" | custom-call | flops 1310720 | bytes 1572864 | tf_op jit(solution)/shard_map/update/pallas_call | solution.py:376
  (40 shorter events, 5.1 us)
Async XLA Ops:
  0.6 12.4 %copy-start.3 = (f32[1,8,64,128]{3,2,1,0:T(8,128)S(1)}, f32[1,8,64,128]{3,2,1,0:T(8,128)}, u32[]{:S(2)}) copy-start(f32[1,8,64,128]{3,2,1,0:T(8,128)} %param.10) | copy-start | bytes 786436
  0.6 12.4 %copy-start.4 = (f32[1,8,64,128]{3,2,1,0:T(8,128)S(1)}, f32[1,8,64,128]{3,2,1,0:T(8,128)}, u32[]{:S(2)}) copy-start(f32[1,8,64,128]{3,2,1,0:T(8,128)} %param.11) | copy-start | bytes 786436
  0.7 12.4 %copy-start = (f32[8,64,128]{2,1,0:T(8,128)S(1)}, f32[8,64,128]{2,1,0:T(8,128)}, u32[]{:S(2)}) copy-start(f32[8,64,128]{2,1,0:T(8,128)} %refs_8_.1) | copy-start | bytes 786436
  0.7 16.3 %copy-start.1 = (f32[1,8,64,128]{3,2,1,0:T(8,128)S(1)}, f32[1,8,64,128]{3,2,1,0:T(8,128)}, u32[]{:S(2)}) copy-start(f32[1,8,64,128]{3,2,1,0:T(8,128)} %param.12) | copy-start | bytes 786436
  0.7 16.3 %copy-start.2 = (f32[1,8,64,128]{3,2,1,0:T(8,128)S(1)}, f32[1,8,64,128]{3,2,1,0:T(8,128)}, u32[]{:S(2)}) copy-start(f32[1,8,64,128]{3,2,1,0:T(8,128)} %param.13) | copy-start | bytes 786436
  2.0 11.0 %collective-permute-start.2 = (f32[10,64,128]{2,1,0:T(8,128)S(1)}, f32[10,64,128]{2,1,0:T(8,128)S(1)}, u32[]{:S(2)}, u32[]{:S(2)}) collective-permute-start(f32[10,64,128]{2,1,0:T(8,128)S(1)} %get-tuple-element.33), channel_id=1, source_target_pairs={{0,1},{2,3},{1,0},{3,2},{4,5},{6,7},{5,4},{7,6},{8,9},{10,11},{9,8... | collective-permute-start | bytes 983048 | tf_op jit(solution)/shard_map/ppermute | solution.py:408
  2.6 10.5 %collective-permute-start.3 = (f32[10,64,128]{2,1,0:T(8,128)S(1)}, f32[10,64,128]{2,1,0:T(8,128)S(1)}, u32[]{:S(2)}, u32[]{:S(2)}) collective-permute-start(f32[10,64,128]{2,1,0:T(8,128)S(1)} %get-tuple-element.34), channel_id=1, source_target_pairs={{1,2},{2,1},{5,6},{6,5},{9,10},{10,9},{13,14},{14,13},{17,18},{18,... | collective-permute-start | bytes 983048 | tf_op jit(solution)/shard_map/ppermute | solution.py:407
  4.4 12.5 %collective-permute-start = (f32[7,64,128]{2,1,0:T(8,128)S(1)}, f32[7,64,128]{2,1,0:T(8,128)S(1)}, u32[]{:S(2)}, u32[]{:S(2)}) collective-permute-start(f32[7,64,128]{2,1,0:T(8,128)S(1)} %get-tuple-element.31), channel_id=1, source_target_pairs={{0,1},{2,3},{1,0},{3,2},{4,5},{6,7},{5,4},{7,6},{8,9},{10,11},{9,8... | collective-permute-start | bytes 688136 | tf_op jit(solution)/shard_map/ppermute | solution.py:408
  8.3 8.6 %collective-permute-start.1 = (f32[7,64,128]{2,1,0:T(8,128)S(1)}, f32[7,64,128]{2,1,0:T(8,128)S(1)}, u32[]{:S(2)}, u32[]{:S(2)}) collective-permute-start(f32[7,64,128]{2,1,0:T(8,128)S(1)} %get-tuple-element.32), channel_id=1, source_target_pairs={{1,2},{2,1},{5,6},{6,5},{9,10},{10,9},{13,14},{14,13},{17,18},{18,... | collective-permute-start | bytes 688136 | tf_op jit(solution)/shard_map/ppermute | solution.py:407
  14.9 7.1 %collective-permute-start.6 = (f32[7,64,128]{2,1,0:T(8,128)S(1)}, f32[7,64,128]{2,1,0:T(8,128)S(1)}, u32[]{:S(2)}, u32[]{:S(2)}) collective-permute-start(f32[7,64,128]{2,1,0:T(8,128)S(1)} %get-tuple-element.44), channel_id=1, source_target_pairs={{0,1},{2,3},{1,0},{3,2},{4,5},{6,7},{5,4},{7,6},{8,9},{10,11},{9,8... | collective-permute-start | bytes 688136 | tf_op jit(solution)/shard_map/ppermute | solution.py:408
  16.2 5.8 %collective-permute-start.7 = (f32[7,64,128]{2,1,0:T(8,128)S(1)}, f32[7,64,128]{2,1,0:T(8,128)S(1)}, u32[]{:S(2)}, u32[]{:S(2)}) collective-permute-start(f32[7,64,128]{2,1,0:T(8,128)S(1)} %get-tuple-element.45), channel_id=1, source_target_pairs={{1,2},{2,1},{5,6},{6,5},{9,10},{10,9},{13,14},{14,13},{17,18},{18,... | collective-permute-start | bytes 688136 | tf_op jit(solution)/shard_map/ppermute | solution.py:407
  18.3 5.5 %collective-permute-start.4 = (f32[7,64,128]{2,1,0:T(8,128)S(1)}, f32[7,64,128]{2,1,0:T(8,128)S(1)}, u32[]{:S(2)}, u32[]{:S(2)}) collective-permute-start(f32[7,64,128]{2,1,0:T(8,128)S(1)} %get-tuple-element.40), channel_id=1, source_target_pairs={{0,1},{2,3},{1,0},{3,2},{4,5},{6,7},{5,4},{7,6},{8,9},{10,11},{9,8... | collective-permute-start | bytes 688136 | tf_op jit(solution)/shard_map/ppermute | solution.py:408
  21.3 2.5 %collective-permute-start.5 = (f32[7,64,128]{2,1,0:T(8,128)S(1)}, f32[7,64,128]{2,1,0:T(8,128)S(1)}, u32[]{:S(2)}, u32[]{:S(2)}) collective-permute-start(f32[7,64,128]{2,1,0:T(8,128)S(1)} %get-tuple-element.41), channel_id=1, source_target_pairs={{1,2},{2,1},{5,6},{6,5},{9,10},{10,9},{13,14},{14,13},{17,18},{18,... | collective-permute-start | bytes 688136 | tf_op jit(solution)/shard_map/ppermute | solution.py:407
  25.8 4.4 %collective-permute-start.8 = (f32[128,128]{1,0:T(8,128)S(1)}, f32[128,128]{1,0:T(8,128)S(1)}, u32[]{:S(2)}, u32[]{:S(2)}) collective-permute-start(f32[128,128]{1,0:T(8,128)S(1)} %get-tuple-element.49), channel_id=1, source_target_pairs={{0,4},{4,0},{8,12},{12,8},{1,5},{5,1},{9,13},{13,9},{2,6},{6,2},{1... | collective-permute-start | bytes 196616 | tf_op jit(solution)/shard_map/ppermute | solution.py:467
  27.3 5.9 %collective-permute-start.9 = (f32[128,128]{1,0:T(8,128)S(1)}, f32[128,128]{1,0:T(8,128)S(1)}, u32[]{:S(2)}, u32[]{:S(2)}) collective-permute-start(f32[128,128]{1,0:T(8,128)S(1)} %get-tuple-element.50), channel_id=1, source_target_pairs={{0,8},{4,12},{8,0},{12,4},{1,9},{5,13},{9,1},{13,5},{2,10},{6,14},... | collective-permute-start | bytes 196616 | tf_op jit(solution)/shard_map/ppermute | solution.py:467
  29.9 6.9 %collective-permute-start.10 = (f32[128,128]{1,0:T(8,128)S(1)}, f32[128,128]{1,0:T(8,128)S(1)}, u32[]{:S(2)}, u32[]{:S(2)}) collective-permute-start(f32[128,128]{1,0:T(8,128)S(1)} %get-tuple-element.51), channel_id=1, source_target_pairs={{0,12},{4,8},{8,4},{12,0},{1,13},{5,9},{9,5},{13,1},{2,14},{6,10},... | collective-permute-start | bytes 196616 | tf_op jit(solution)/shard_map/ppermute | solution.py:467
  36.8 6.7 %collective-permute-start.11 = (f32[136,128]{1,0:T(8,128)S(1)}, f32[136,128]{1,0:T(8,128)S(1)}, u32[]{:S(2)}, u32[]{:S(2)}) collective-permute-start(f32[136,128]{1,0:T(8,128)S(1)} %total.1.refs_0_), channel_id=1, source_target_pairs={{0,4},{4,0},{8,12},{12,8},{1,5},{5,1},{9,13},{13,9},{2,6},{6,2},{1... | collective-permute-start | bytes 208904 | tf_op jit(solution)/shard_map/ppermute | solution.py:467
  36.9 6.6 %collective-permute-start.12 = (f32[136,128]{1,0:T(8,128)S(1)}, f32[136,128]{1,0:T(8,128)S(1)}, u32[]{:S(2)}, u32[]{:S(2)}) collective-permute-start(f32[136,128]{1,0:T(8,128)S(1)} %total.1.refs_0_), channel_id=1, source_target_pairs={{0,8},{4,12},{8,0},{12,4},{1,9},{5,13},{9,1},{13,5},{2,10},{6,14},... | collective-permute-start | bytes 208904 | tf_op jit(solution)/shard_map/ppermute | solution.py:467
  37.5 7.3 %collective-permute-start.13 = (f32[136,128]{1,0:T(8,128)S(1)}, f32[136,128]{1,0:T(8,128)S(1)}, u32[]{:S(2)}, u32[]{:S(2)}) collective-permute-start(f32[136,128]{1,0:T(8,128)S(1)} %total.1.refs_0_), channel_id=1, source_target_pairs={{0,12},{4,8},{8,4},{12,0},{1,13},{5,9},{9,5},{13,1},{2,14},{6,10},... | collective-permute-start | bytes 208904 | tf_op jit(solution)/shard_map/ppermute | solution.py:467
  41.3 9.0 %collective-permute-start.17 = (f32[1,64,128]{2,1,0:T(8,128)S(1)}, f32[1,64,128]{2,1,0:T(8,128)S(1)}, u32[]{:S(2)}, u32[]{:S(2)}) collective-permute-start(f32[1,64,128]{2,1,0:T(8,128)S(1)} %get-tuple-element.54), channel_id=1, source_target_pairs={{0,1},{2,3},{1,0},{3,2},{4,5},{6,7},{5,4},{7,6},{8,9},{10,11},{9,8... | collective-permute-start | bytes 98312 | tf_op jit(solution)/shard_map/ppermute | solution.py:408
  42.8 7.4 %collective-permute-start.18 = (f32[1,64,128]{2,1,0:T(8,128)S(1)}, f32[1,64,128]{2,1,0:T(8,128)S(1)}, u32[]{:S(2)}, u32[]{:S(2)}) collective-permute-start(f32[1,64,128]{2,1,0:T(8,128)S(1)} %get-tuple-element.55), channel_id=1, source_target_pairs={{1,2},{2,1},{5,6},{6,5},{9,10},{10,9},{13,14},{14,13},{17,18},{18,... | collective-permute-start | bytes 98312 | tf_op jit(solution)/shard_map/ppermute | solution.py:407
  44.8 5.4 %collective-permute-start.14 = (f32[8,128]{1,0:T(8,128)S(1)}, f32[8,128]{1,0:T(8,128)S(1)}, u32[]{:S(2)}, u32[]{:S(2)}) collective-permute-start(f32[8,128]{1,0:T(8,128)S(1)} %top.1.refs_4_), channel_id=1, source_target_pairs={{0,1},{1,0},{2,3},{3,2},{4,5},{5,4},{6,7},{7,6},{8,9},{9,8},{10,11... | collective-permute-start | bytes 12296 | tf_op jit(solution)/shard_map/ppermute | solution.py:479
  48.8 3.6 %collective-permute-start.15 = (f32[8,128]{1,0:T(8,128)S(1)}, f32[8,128]{1,0:T(8,128)S(1)}, u32[]{:S(2)}, u32[]{:S(2)}) collective-permute-start(f32[8,128]{1,0:T(8,128)S(1)} %top.1.refs_4_), channel_id=1, source_target_pairs={{0,2},{1,3},{2,0},{3,1},{4,6},{5,7},{6,4},{7,5},{8,10},{9,11},{10,... | collective-permute-start | bytes 12296 | tf_op jit(solution)/shard_map/ppermute | solution.py:479
  50.0 3.0 %collective-permute-start.16 = (f32[8,128]{1,0:T(8,128)S(1)}, f32[8,128]{1,0:T(8,128)S(1)}, u32[]{:S(2)}, u32[]{:S(2)}) collective-permute-start(f32[8,128]{1,0:T(8,128)S(1)} %top.1.refs_4_), channel_id=1, source_target_pairs={{0,3},{1,2},{2,1},{3,0},{4,7},{5,6},{6,5},{7,4},{8,11},{9,10},{10,... | collective-permute-start | bytes 12296 | tf_op jit(solution)/shard_map/ppermute | solution.py:479
  (3 other events, 13.7 us)

commit v4 on v3

v4 whole, which is shorter than its diff:
```python
import functools

import jax
import jax.numpy as jnp
from jax import lax
from jax.experimental import pallas as pl
from jax.experimental.pallas import tpu as pltpu
from jax.sharding import PartitionSpec as P

ITERS = 8
REACH = ITERS
GUARD = 8
LANES = 128
LIMIT = 16 * 2**20
VMEM = pltpu.VMEM
SMEM = pltpu.SMEM


def pairs(count, start):
    low = [(i, i + 1) for i in range(start, count - 1, 2)]
    return low + [(b, a) for a, b in low]


def partner_perms(count):
    if count & (count - 1) == 0:
        return {m: [(i, i ^ m) for i in range(count)] for m in range(1, count)}
    return {m: [(i, (i + m) % count) for i in range(count)] for m in range(1, count)}


def far_first(count):
    half = count // 2
    return [*range(half, count), *range(1, half)]


def send_slot(me, m, count):
    return me ^ m if count & (count - 1) == 0 else lax.rem(me + m, count)


def from_slot(me, m, count):
    return me ^ m if count & (count - 1) == 0 else lax.rem(me - m + count, count)


def spec(space):
    return pl.BlockSpec(memory_space=space)


def cost(flops, nbytes):
    return pl.CostEstimate(flops=int(flops), bytes_accessed=int(nbytes), transcendentals=0)


def is_even():
    return lax.rem(lax.axis_index("slab"), 2) == 0


def pack_kernel(depth, sizes, *refs):
    *fields, to_a, to_b, sem = refs

    def copies(up_a, up_b):
        out = []
        for j, (dst, up) in enumerate(((to_a, up_a), (to_b, up_b))):
            at = 0
            for i, (field, size) in enumerate(zip(fields, sizes)):
                out.append(
                    pltpu.make_async_copy(
                        field.at[pl.ds(depth - size if up else 0, size)],
                        dst.at[pl.ds(at, size)],
                        sem.at[j, i],
                    )
                )
                at += size
        return out

    even = is_even()

    @pl.when(even)
    def _():
        for c in copies(True, False):
            c.start()

    @pl.when(jnp.logical_not(even))
    def _():
        for c in copies(False, True):
            c.start()

    for c in copies(False, False):
        c.wait()


def inject_kernel(depth, width, rec_ref, misfit_ref, out_ref, left, right):
    rows = left.shape[0]
    base = (lax.axis_index("slab") * depth - REACH) * width
    index = rec_ref[...]
    row_of = index // LANES
    lane_of = index - row_of * LANES
    row_of = row_of - base
    group = 2 * width
    for first in range(0, rows, group):
        at = lax.broadcasted_iota(jnp.int32, (group, LANES), 0) + first
        hot = jnp.where(at == row_of, 1.0, 0.0).astype(jnp.bfloat16)
        for part in range(3):
            left[pl.ds(first, group), pl.ds(part * LANES, LANES)] = hot
    lane = lax.broadcasted_iota(jnp.int32, (LANES, LANES), 0)
    mine = lane == lane_of
    for k in range(ITERS):
        value = misfit_ref[pl.ds(k, 1), :]
        for part in range(3):
            piece = value.astype(jnp.bfloat16).astype(jnp.float32)
            value = value - piece
            right[pl.ds(k * LANES, LANES), pl.ds(part * LANES, LANES)] = jnp.where(
                mine, piece, 0.0
            ).astype(jnp.bfloat16)

    def pair(j, carry):
        cols = right[pl.ds(pl.multiple_of(j * 2 * LANES, 2 * LANES), 2 * LANES), :]
        both = lax.dot_general(
            left[...], cols, (((1,), (1,)), ((), ())), preferred_element_type=jnp.float32
        )
        out_ref[2 * j] = both[:, :LANES].reshape(out_ref.shape[1:])
        out_ref[2 * j + 1] = both[:, LANES:].reshape(out_ref.shape[1:])
        return carry

    lax.fori_loop(0, ITERS // 2, pair, 0)


def neighbours(src, p, r, first, last):
    c = src[p, pl.ds(r, 8), :]
    s = src[p + 1, pl.ds(r, 8), :] + src[p - 1, pl.ds(r, 8), :]
    s = s + src[p, pl.ds(r + 1, 8), :]
    s = s + src[p, pl.ds(r - 1, 8), :]
    s = s + jnp.where(last, 0.0, pltpu.roll(c, LANES - 1, 1))
    s = s + jnp.where(first, 0.0, pltpu.roll(c, 1, 1))
    return c, s


def edges():
    lane = lax.broadcasted_iota(jnp.int32, (8, LANES), 1)
    return lane == 0, lane == LANES - 1


def clear_guards(field):
    planes, rows, _ = field.shape
    zero = jnp.zeros((GUARD, LANES), jnp.float32)
    for p in range(planes):
        field[p, pl.ds(0, GUARD), :] = zero
        field[p, pl.ds(rows - GUARD, GUARD), :] = zero


def fill(depth, width, own, a_in, b_in, bufs):
    rows = [pl.ds(buf.shape[1] - width - GUARD if buf.shape[1] > width else 0, width) for buf in bufs]
    for src, buf, r in zip(own, bufs, rows):
        for p in range(depth):
            buf[REACH + p, r, :] = src[p]

    def put(low, high):
        for buf, r, (lo, at, size), (hi, _, _) in zip(bufs, rows, low, high):
            for p in range(size):
                buf[REACH - size + p, r, :] = lo[at + p]
                buf[REACH + depth + p, r, :] = hi[at + p]

    even = is_even()

    @pl.when(even)
    def _():
        put(b_in, a_in)

    @pl.when(jnp.logical_not(even))
    def _():
        put(a_in, b_in)


def blocks(depth, width, k):
    for p in range(k + 1, depth + 2 * REACH - 1 - k):
        for r in range(0, width, 8):
            yield p, r, REACH <= p < REACH + depth


def forward_kernel(
    depth, width, wavelet, src_index, now, later, model, ua_in, ub_in, ha_in, hb_in,
    u_out, base_out, lap_out, a_edge, b_edge, mod, weight,
    cur, old,
):
    n = REACH - 1
    clear_guards(cur)
    clear_guards(old)
    fill(
        depth, width, (now, later, model),
        ((ua_in, 0, REACH), (ha_in, 0, n), (ha_in, n, n)),
        ((ub_in, 0, REACH), (hb_in, 0, n), (hb_in, n, n)),
        (cur, old, mod),
    )
    for p in range(1, depth + 2 * REACH - 1):
        weight[p] = 2.0 - 6.0 * mod[p]
    first, last = edges()
    source = src_index[0]
    src_row = source // LANES
    src_lane = source - src_row * LANES
    src_row = src_row - (lax.axis_index("slab") * depth - REACH) * width
    bufs = (cur, old)
    for k in range(ITERS):
        s, d = bufs[k % 2], bufs[(k + 1) % 2]
        for p, r, own in blocks(depth, width, k):
            c, around = neighbours(s, p, GUARD + r, first, last)
            lap = around - 6.0 * c
            here = (p, pl.ds(GUARD + r, 8), slice(None))
            d[here] = 2.0 * c - d[here] + mod[p, pl.ds(r, 8), :] * lap
            if own:
                lap_out[k, p - REACH, pl.ds(r, 8), :] = lap

        @pl.when((src_row >= (k + 1) * width) & (src_row < (depth + 2 * REACH - 1 - k) * width))
        def _():
            plane = src_row // width
            here = (plane, pl.ds(GUARD + src_row - plane * width, 1), slice(None))
            at = lax.broadcasted_iota(jnp.int32, (1, LANES), 1) == src_lane
            d[here] = d[here] + jnp.where(at, wavelet[0, k], 0.0)

    u, u_later = bufs[ITERS % 2], bufs[(ITERS + 1) % 2]
    rows = pl.ds(GUARD, width)
    even = is_even()
    a_edge[...] = u[jnp.where(even, REACH + depth - 1, REACH), rows, :]
    slab = lax.axis_index("slab")
    alone = jnp.where(even, slab == 0, slab == lax.axis_size("slab") - 1)
    b_edge[...] = jnp.where(alone, 0.0, u[jnp.where(even, REACH, REACH + depth - 1), rows, :])
    for p in range(depth):
        c = u[REACH + p, rows, :]
        u_out[p] = c
        base_out[p] = 2.0 * c - u_later[REACH + p, rows, :]


def adjoint_kernel(
    depth, width, shots, now, later, a_in, b_in, mod, weight, laps, extra, a_out, *rest
):
    *pieces, image, cur, old = rest
    n = REACH - 1
    clear_guards(cur)
    clear_guards(old)
    fill(
        depth, width, (now, later),
        ((a_in, 0, REACH), (a_in, REACH, n)), ((b_in, 0, REACH), (b_in, REACH, n)),
        (cur, old),
    )
    first, last = edges()
    bufs = (cur, old)
    for k in range(ITERS):
        s, d = bufs[k % 2], bufs[(k + 1) % 2]
        for p, r, own in blocks(depth, width, k):
            c, around = neighbours(s, p, GUARD + r, first, last)
            here = (p, pl.ds(GUARD + r, 8), slice(None))
            rows = pl.ds(r, 8)
            new = weight[p, rows, :] * c - d[here] + mod[p, rows, :] * around
            d[here] = new + extra[k, p, rows, :]
            if own:
                q = p - REACH
                into = pl.ds(q * width + r, 8)
                add = c * laps[k, q, rows, :]
                image[into, :] = image[into, :] + add if k > 0 else add

    a = bufs[ITERS % 2]
    for p in range(depth):
        a_out[p] = a[REACH + p, pl.ds(GUARD, width), :]
    n = depth * width // shots
    me = lax.axis_index("shot")
    for m in range(shots):
        to = me if m == 0 else send_slot(me, m, shots)
        pieces[m][...] = image[pl.ds(pl.multiple_of(to * n, n), n), :]


def sum_kernel(*refs):
    *parts, out = refs
    n = parts[0].shape[0]
    top = jnp.zeros((8, LANES), jnp.float32)
    for r in range(0, n, 8):
        total = parts[0][pl.ds(r, 8), :]
        for part in parts[1:]:
            total = total + part[pl.ds(r, 8), :]
        out[pl.ds(r, 8), :] = total
        top = jnp.maximum(top, jnp.abs(total))
    out[pl.ds(n, 8), :] = top


def top_kernel(shots, riders, *refs):
    parts, planes, outs = refs[:shots], refs[shots : shots + riders], refs[shots + riders :]
    n = parts[0].shape[0] - 8
    top = parts[0][pl.ds(n, 8), :]
    for part in parts[1:]:
        top = jnp.maximum(top, part[pl.ds(n, 8), :])
    outs[0][...] = top
    for plane, out in zip(planes, outs[1:]):
        rows = plane.shape[0]
        out[pl.ds(0, rows), :] = plane[...]
        out[pl.ds(rows, 8), :] = top


def final_kernel(depth, width, shots, tops, *refs):
    n = depth * width // shots
    grads, refs = refs[:shots], refs[shots:]
    tops, refs = refs[:tops], refs[tops:]
    model, u, base, a_edge, b_edge, new_model, stepped, pad, grad = refs
    even = is_even()
    me = lax.axis_index("shot")
    rows = pl.ds(GUARD, width)
    clear_guards(pad)
    low, high = jnp.where(even, 0, depth + 1), jnp.where(even, depth + 1, 0)
    pad[low, rows, :] = b_edge[pl.ds(0, width), :]
    pad[high, rows, :] = a_edge[pl.ds(0, width), :]
    for p in range(depth):
        pad[p + 1, rows, :] = u[p]
    for m in range(shots):
        owner = me if m == 0 else from_slot(me, m, shots)
        grad[pl.ds(pl.multiple_of(owner * n, n), n), :] = grads[m][pl.ds(0, n), :]
    top = tops[0][...]
    for other in tops[1:]:
        top = jnp.maximum(top, other[pl.ds(other.shape[0] - 8, 8), :])
    peak = jnp.max(top)
    first, last = edges()
    for p in range(depth):
        for r in range(0, width, 8):
            g = grad[pl.ds(p * width + r, 8), :]
            new = jnp.clip(model[p, pl.ds(r, 8), :] - 0.1 * g / (peak + 1e-06), 0.05, 0.3)
            new_model[p, pl.ds(r, 8), :] = new
            c, around = neighbours(pad, p + 1, GUARD + r, first, last)
            stepped[p, pl.ds(r, 8), :] = base[p, pl.ds(r, 8), :] + new * (around - 6.0 * c)


def placed(x, space):
    if space is VMEM or space is pltpu.HBM:
        return pltpu.with_memory_space_constraint(x, space)
    return x


def call(kernel, outs, args, spaces, scratch, flops, nbytes):
    args = [placed(x, space) for x, space in zip(args, spaces)]
    return pl.pallas_call(
        kernel,
        out_shape=outs,
        in_specs=[spec(space) for space in spaces],
        out_specs=[spec(VMEM)] * len(outs),
        scratch_shapes=scratch,
        cost_estimate=cost(flops, nbytes),
        compiler_params=pltpu.CompilerParams(vmem_limit_bytes=LIMIT),
    )(*args)


def per_device(model, fwd_now, fwd_next, adj_now, adj_next, wavelet, misfit, src_index, rec_index):
    f32 = jnp.float32
    depth, width, length = model.shape
    assert length == LANES and fwd_now.shape[0] == 1 and width % 8 == 0 and depth == REACH
    u0, u1, a0, a1 = fwd_now[0], fwd_next[0], adj_now[0], adj_next[0]
    slabs, shots = lax.axis_size("slab"), lax.axis_size("shot")
    perm_a, perm_b = pairs(slabs, 0), pairs(slabs, 1)
    planes = depth + 2 * REACH
    cells = depth * width * LANES
    own = VMEM((depth, width, LANES), f32)
    wide = VMEM((planes, width, LANES), f32)
    field = VMEM((planes, width + 2 * GUARD, LANES), f32)
    edge = VMEM((width, LANES), f32)
    out = jax.ShapeDtypeStruct((depth, width, LANES), f32)
    n = REACH - 1

    def exchange(to_a, to_b):
        b = lax.ppermute(to_b, "slab", perm_b)
        return lax.ppermute(to_a, "slab", perm_a), b

    def packed(fields, sizes):
        total = sum(sizes)
        return call(
            functools.partial(pack_kernel, depth, sizes),
            [VMEM((total, width, LANES), f32)] * 2,
            fields, [pltpu.HBM] * len(fields), [pltpu.SemaphoreType.DMA((2, len(fields)))],
            0, 4 * 4 * total * width * LANES,
        )

    ua, ub = exchange(u0, u0)
    ha, hb = exchange(*packed((u1, model), (n, n)))
    ga, gb = exchange(*packed((a0, a1), (REACH, n)))
    (extra,) = call(
        functools.partial(inject_kernel, depth, width),
        [VMEM((ITERS, planes, width, LANES), f32)],
        (rec_index, misfit[0]), (VMEM, VMEM),
        [
            VMEM((planes * width, 3 * LANES), jnp.bfloat16),
            VMEM((ITERS * LANES, 3 * LANES), jnp.bfloat16),
        ],
        2 * planes * width * 3 * LANES * ITERS * LANES, 4 * ITERS * planes * width * LANES,
    )

    u, base, laps, a_edge, b_edge, mod, weight = call(
        functools.partial(forward_kernel, depth, width),
        [own, own, VMEM((ITERS, depth, width, LANES), f32), edge, edge, wide, wide],
        (wavelet, src_index, u0, u1, model, ua, ub, ha, hb), [SMEM] * 2 + [VMEM] * 7,
        [field] * 2, 15 * ITERS * 2 * cells, 80 * cells,
    )
    rows = depth * width // shots
    a, *pieces = call(
        functools.partial(adjoint_kernel, depth, width, shots),
        [out] + [VMEM((rows, LANES), f32)] * shots,
        (a0, a1, ga, gb, mod, weight, laps, extra), [VMEM] * 8,
        [VMEM((depth * width, LANES), f32), field, field],
        18 * ITERS * 2 * cells, 80 * cells,
    )

    perms = partner_perms(shots)
    order = far_first(shots)

    def with_others(own_one, pieces):
        got = {}
        for m in order:
            got[m] = lax.ppermute(pieces[m], "shot", perms[m])
        return [own_one] + [got[m] for m in range(1, shots)]

    parts = with_others(pieces[0], pieces)
    (grad,) = call(
        sum_kernel, [VMEM((rows + 8, LANES), f32)], parts, [VMEM] * shots, [],
        shots * rows * LANES, 4 * shots * rows * LANES,
    )
    grads = with_others(grad, [grad] * shots)

    sides = {1: a_edge, 3: b_edge} if slabs == 4 else {}
    top, *ridden = call(
        functools.partial(top_kernel, shots, len(sides)),
        [VMEM((8, LANES), f32)] + [VMEM((width + 8, LANES), f32)] * len(sides),
        (*grads, *sides.values()), [VMEM] * (shots + len(sides)), [], 0, 4096 * shots,
    )
    riding = dict(zip(sides, ridden))
    got = {
        m: lax.ppermute(riding.get(m, top), "slab", q) for m, q in partner_perms(slabs).items()
    }
    if sides:
        a_edge, b_edge = got[1], got[3]
    else:
        a_edge, b_edge = exchange(a_edge, b_edge)
    tops = [top, *got.values()]

    new_model, stepped = call(
        functools.partial(final_kernel, depth, width, shots, len(tops)),
        [out, out],
        (*grads, *tops, model, u, base, a_edge, b_edge), [VMEM] * (shots + len(tops) + 5),
        [VMEM((depth + 2, width + 2 * GUARD, LANES), f32), VMEM((depth * width, LANES), f32)],
        20 * cells, 4 * 6 * cells,
    )
    return new_model, stepped[None], a[None]


def solution(mesh):
    in_specs = (
        P(("groups", "slab"), None, None),
        P(("groups", "shot"), "slab", None, None),
        P(("groups", "shot"), "slab", None, None),
        P(("groups", "shot"), "slab", None, None),
        P(("groups", "shot"), "slab", None, None),
        P(("groups", "shot"), None),
        P(("groups", "shot"), None, None),
        P(("groups", "shot")),
        P(("groups", "shot"), None),
    )
    out_specs = (
        P(("groups", "slab"), None, None),
        P(("groups", "shot"), "slab", None, None),
        P(("groups", "shot"), "slab", None, None),
    )
    return jax.shard_map(
        per_device, mesh=mesh, in_specs=in_specs, out_specs=out_specs, check_vma=False
    )
```

time: 54.6 us -> 52.4 us (0.960)
  starting transfers between devices: 27.9 us -> 22 us
  waiting for transfers between devices: 10.8 us -> 13.7 us
  Pallas kernels: 12.6 us -> 13.6 us
    ppermute x9, starting transfers between devices: 14.2 us -> 11 us  [the longest x6 8.84 us: with_others(): got[m] = lax.ppermute(pieces[m], 'shot', perms[m])]
    ppermute x9, waiting for transfers between devices: 10.8 us -> 13.7 us  [the longest x6 11.2 us: with_others(): got[m] = lax.ppermute(pieces[m], 'shot', perms[m])]
    ppermute x5 -> x3, starting transfers between devices: 10.4 us -> 8.74 us  [exchange(): return (lax.ppermute(to_a, 'slab', perm_a), b)]
    ppermute x5 -> x3, starting transfers between devices: 3.31 us -> 2.17 us  [exchange(): b = lax.ppermute(to_b, 'slab', perm_b)]
    pallas_call x10 -> x8, Pallas kernels: 12.6 us -> 13.6 us  [call(): pl.pallas_call(kernel, out_shape=outs, in_specs=[spec(space) for space in...]
  transfers between devices with their start and end apart: 19 -> 15, of which waited for: 5 -> 5; matrix products, arithmetic and copies ran while one was open for 0% -> 0% of each run, Pallas kernels for 15% -> 17%
where the time goes in v4:
time: 52.4 us; the launch traced here: 52.1 us
  starting transfers between devices  22 us (42%)
  waiting for transfers between devices  13.7 us (26%)
  Pallas kernels  13.6 us (26%)
  between operations  1.5 us (3%)
  local copies, waits for them, and re-layouts  1.37 us (3%)
    pallas_call x8, Pallas kernels, call(): pl.pallas_call(kernel, out_shape=outs, in_specs=[spec(space) for space in...  13.6 us
    ppermute x6, waiting for transfers between devices, with_others(): got[m] = lax.ppermute(pieces[m], 'shot', perms[m])  11.2 us
    ppermute x6, starting transfers between devices, with_others(): got[m] = lax.ppermute(pieces[m], 'shot', perms[m])  8.84 us
    ppermute x3, starting transfers between devices, exchange(): return (lax.ppermute(to_a, 'slab', perm_a), b)  8.74 us
    ppermute x3, waiting for transfers between devices, per_device(): lax.ppermute(riding.get(m, top), 'slab', q)  2.47 us
    ppermute x3, starting transfers between devices, per_device(): lax.ppermute(riding.get(m, top), 'slab', q)  2.21 us
    ppermute x3, starting transfers between devices, exchange(): b = lax.ppermute(to_b, 'slab', perm_b)  2.17 us
    unnamed x16, local copies, waits for them, and re-layouts  1.37 us
  transfers between devices with their start and end apart: 15, of which 5 were waited for; matrix products, arithmetic and copies ran while one was open for 0% of the time, Pallas kernels for 17%

profile of v4, /device:TPU:0, one launch (start us, length us, event | category | flops | bytes accessed | tf_op | source)
XLA Modules:
  0.0 52.1 jit_solution(5874730159438138953)
XLA Ops:
  0.7 0.8 %collective-permute-start.3 = (f32[8,64,128]{2,1,0:T(8,128)}, f32[8,64,128]{2,1,0:T(8,128)S(1)}, u32[]{:S(2)}, u32[]{:S(2)}) collective-permute-start(f32[8,64,128]{2,1,0:T(8,128)} %bitcast.13), channel_id=1, source_target_pairs={{1,2},{2,1},{5,6},{6,5},{9,10},{10,9},{13,14},{14,13},{17,18},{18,... | collective-permute-start | bytes 786440 | tf_op jit(solution)/shard_map/ppermute | solution.py:360
  1.5 1.3 %shard_map.112 = (f32[15,64,128]{2,1,0:T(8,128)S(1)}, f32[15,64,128]{2,1,0:T(8,128)S(1)}) custom-call(f32[8,64,128]{2,1,0:T(8,128)} %bitcast.7, f32[8,64,128]{2,1,0:T(8,128)} %bitcast.9), custom_call_target="tpu_custom_call" | custom-call | bytes 1966080 | tf_op jit(solution)/shard_map/pallas_call | solution.py:332
  2.8 4.4 %collective-permute-start = (f32[15,64,128]{2,1,0:T(8,128)S(1)}, f32[15,64,128]{2,1,0:T(8,128)S(1)}, u32[]{:S(2)}, u32[]{:S(2)}) collective-permute-start(f32[15,64,128]{2,1,0:T(8,128)S(1)} %get-tuple-element.24), channel_id=1, source_target_pairs={{0,1},{2,3},{1,0},{3,2},{4,5},{6,7},{5,4},{7,6},{8,9},{10,11},{9,8... | collective-permute-start | bytes 1474568 | tf_op jit(solution)/shard_map/ppermute | solution.py:361
  7.1 0.7 %collective-permute-start.1 = (f32[15,64,128]{2,1,0:T(8,128)S(1)}, f32[15,64,128]{2,1,0:T(8,128)S(1)}, u32[]{:S(2)}, u32[]{:S(2)}) collective-permute-start(f32[15,64,128]{2,1,0:T(8,128)S(1)} %get-tuple-element.25), channel_id=1, source_target_pairs={{1,2},{2,1},{5,6},{6,5},{9,10},{10,9},{13,14},{14,13},{17,18},{18,... | collective-permute-start | bytes 1474568 | tf_op jit(solution)/shard_map/ppermute | solution.py:360
  7.8 1.3 %shard_map.113 = (f32[14,64,128]{2,1,0:T(8,128)S(1)}, f32[14,64,128]{2,1,0:T(8,128)S(1)}) custom-call(f32[8,64,128]{2,1,0:T(8,128)} %bitcast.11, f32[8,64,128]{2,1,0:T(8,128)} %refs_8_.1), custom_call_target="tpu_custom_call" | custom-call | bytes 1835008 | tf_op jit(solution)/shard_map/pallas_call | solution.py:332
  9.2 1.3 %collective-permute-start.4 = (f32[14,64,128]{2,1,0:T(8,128)S(1)}, f32[14,64,128]{2,1,0:T(8,128)S(1)}, u32[]{:S(2)}, u32[]{:S(2)}) collective-permute-start(f32[14,64,128]{2,1,0:T(8,128)S(1)} %get-tuple-element.26), channel_id=1, source_target_pairs={{0,1},{2,3},{1,0},{3,2},{4,5},{6,7},{5,4},{7,6},{8,9},{10,11},{9,8... | collective-permute-start | bytes 1376264 | tf_op jit(solution)/shard_map/ppermute | solution.py:361
  10.5 0.7 %collective-permute-start.5 = (f32[14,64,128]{2,1,0:T(8,128)S(1)}, f32[14,64,128]{2,1,0:T(8,128)S(1)}, u32[]{:S(2)}, u32[]{:S(2)}) collective-permute-start(f32[14,64,128]{2,1,0:T(8,128)S(1)} %get-tuple-element.27), channel_id=1, source_target_pairs={{1,2},{2,1},{5,6},{6,5},{9,10},{10,9},{13,14},{14,13},{17,18},{18,... | collective-permute-start | bytes 1376264 | tf_op jit(solution)/shard_map/ppermute | solution.py:360
  11.2 3.0 %collective-permute-start.2 = (f32[8,64,128]{2,1,0:T(8,128)}, f32[8,64,128]{2,1,0:T(8,128)S(1)}, u32[]{:S(2)}, u32[]{:S(2)}) collective-permute-start(f32[8,64,128]{2,1,0:T(8,128)} %bitcast.14), channel_id=1, source_target_pairs={{0,1},{2,3},{1,0},{3,2},{4,5},{6,7},{5,4},{7,6},{8,9},{10,11},{9,8... | collective-permute-start | bytes 786440 | tf_op jit(solution)/shard_map/ppermute | solution.py:361
  14.9 0.7 %copy-done.5 = f32[1,8,128]{2,1,0:T(8,128)S(1)} copy-done((f32[1,8,128]{2,1,0:T(8,128)S(1)}, f32[1,8,128]{2,1,0:T(8,128)}, u32[]{:S(2)}) %copy-start.5) | copy-done | bytes 4120
  16.2 2.7 %shard_map.115.extra = f32[8,24,64,128]{3,2,1,0:T(8,128)S(1)} custom-call(s32[1,128]{1,0:T(1,128)S(1)} %copy-done.6, f32[8,128]{1,0:T(8,128)S(1)} %bitcast.16), custom_call_target="tpu_custom_call" | custom-call | flops 1207959552 | bytes 6291456 | tf_op jit(solution)/shard_map/pallas_call | solution.py:332
  19.0 3.6 %shard_map.114 = (f32[8,64,128]{2,1,0:T(8,128)S(1)}, f32[8,64,128]{2,1,0:T(8,128)S(1)}, f32[8,8,64,128]{3,2,1,0:T(8,128)S(1)}, f32[64,128]{1,0:T(8,128)S(1)}, f3...) custom-call(f32[1,8]{1,0:T(1,128)S(1)} %copy-done.7, s32[1]{0:T(128)S(6)} %copy.12.src_index, ...), custom_call_target="tpu_custom_call" | custom-call | flops 15728640 | bytes 5242880 | tf_op jit(solution)/shard_map/pallas_call | solution.py:332
  22.6 3.7 %shard_map.116 = (f32[8,64,128]{2,1,0:T(8,128)}, f32[128,128]{1,0:T(8,128)S(1)}, f32[128,128]{1,0:T(8,128)S(1)}, f32[128,128]{1,0:T(8,128)S(1)}, f32[128,128]{1,0:T(8,128)S(1)}) custom-call(f32[8,64,128]{2,1,0:T(8,128)S(1)} %bitcast.8, f32[8,64,128]{2,1,0:T(8,128)S(1)} %bitcast.10, f32[15,64,128]{2,1,0:T(8,128)S(1)} %collective-permute-done.a_in, ...), custom_call_target="tpu_custom_call" | custom-call | flops 18874368 | bytes 5242880 | tf_op jit(solution)/shard_map/pallas_call | solution.py:332
  26.3 1.6 %collective-permute-start.6 = (f32[128,128]{1,0:T(8,128)S(1)}, f32[128,128]{1,0:T(8,128)S(1)}, u32[]{:S(2)}, u32[]{:S(2)}) collective-permute-start(f32[128,128]{1,0:T(8,128)S(1)} %get-tuple-element.32), channel_id=1, source_target_pairs={{0,4},{4,0},{8,12},{12,8},{1,5},{5,1},{9,13},{13,9},{2,6},{6,2},{1... | collective-permute-start | bytes 196616 | tf_op jit(solution)/shard_map/ppermute | solution.py:407
  27.9 2.6 %collective-permute-start.7 = (f32[128,128]{1,0:T(8,128)S(1)}, f32[128,128]{1,0:T(8,128)S(1)}, u32[]{:S(2)}, u32[]{:S(2)}) collective-permute-start(f32[128,128]{1,0:T(8,128)S(1)} %get-tuple-element.33), channel_id=1, source_target_pairs={{0,8},{4,12},{8,0},{12,4},{1,9},{5,13},{9,1},{13,5},{2,10},{6,14},... | collective-permute-start | bytes 196616 | tf_op jit(solution)/shard_map/ppermute | solution.py:407
  30.7 3.1 %collective-permute-done.7.refs_2_ = f32[128,128]{1,0:T(8,128)S(1)} collective-permute-done((f32[128,128]{1,0:T(8,128)S(1)}, f32[128,128]{1,0:T(8,128)S(1)}, u32[]{:S(2)}, u32[]{:S(2)}) %collective-permute-start.7) | collective-permute-done | bytes 65568 | tf_op jit(solution)/shard_map/ppermute | solution.py:407
  33.7 2.8 %collective-permute-done.8.refs_3_ = f32[128,128]{1,0:T(8,128)S(1)} collective-permute-done((f32[128,128]{1,0:T(8,128)S(1)}, f32[128,128]{1,0:T(8,128)S(1)}, u32[]{:S(2)}, u32[]{:S(2)}) %collective-permute-start.8) | collective-permute-done | bytes 65568 | tf_op jit(solution)/shard_map/ppermute | solution.py:407
  36.6 1.3 %collective-permute-start.11 = (f32[136,128]{1,0:T(8,128)S(1)}, f32[136,128]{1,0:T(8,128)S(1)}, u32[]{:S(2)}, u32[]{:S(2)}) collective-permute-start(f32[136,128]{1,0:T(8,128)S(1)} %shard_map.117.refs_0_), channel_id=1, source_target_pairs={{0,12},{4,8},{8,4},{12,0},{1,13},{5,9},{9,5},{13,1},{2,14},{6,10},... | collective-permute-start | bytes 208904 | tf_op jit(solution)/shard_map/ppermute | solution.py:407
  37.8 3.2 %collective-permute-start.9 = (f32[136,128]{1,0:T(8,128)S(1)}, f32[136,128]{1,0:T(8,128)S(1)}, u32[]{:S(2)}, u32[]{:S(2)}) collective-permute-start(f32[136,128]{1,0:T(8,128)S(1)} %shard_map.117.refs_0_), channel_id=1, source_target_pairs={{0,4},{4,0},{8,12},{12,8},{1,5},{5,1},{9,13},{13,9},{2,6},{6,2},{1... | collective-permute-start | bytes 208904 | tf_op jit(solution)/shard_map/ppermute | solution.py:407
  41.0 2.0 %collective-permute-done.11.refs_3_ = f32[136,128]{1,0:T(8,128)S(1)} collective-permute-done((f32[136,128]{1,0:T(8,128)S(1)}, f32[136,128]{1,0:T(8,128)S(1)}, u32[]{:S(2)}, u32[]{:S(2)}) %collective-permute-start.11) | collective-permute-done | bytes 69664 | tf_op jit(solution)/shard_map/ppermute | solution.py:407
  43.0 3.4 %collective-permute-done.10.refs_2_ = f32[136,128]{1,0:T(8,128)S(1)} collective-permute-done((f32[136,128]{1,0:T(8,128)S(1)}, f32[136,128]{1,0:T(8,128)S(1)}, u32[]{:S(2)}, u32[]{:S(2)}) %collective-permute-start.10) | collective-permute-done | bytes 69664 | tf_op jit(solution)/shard_map/ppermute | solution.py:407
  46.6 0.9 %collective-permute-start.14 = (f32[72,128]{1,0:T(8,128)S(1)}, f32[72,128]{1,0:T(8,128)S(1)}, u32[]{:S(2)}, u32[]{:S(2)}) collective-permute-start(f32[72,128]{1,0:T(8,128)S(1)} %get-tuple-element.39), channel_id=1, source_target_pairs={{0,3},{1,2},{2,1},{3,0},{4,7},{5,6},{6,5},{7,4},{8,11},{9,10},{10,... | collective-permute-start | bytes 110600 | tf_op jit(solution)/shard_map/ppermute | solution.py:425
  47.5 1.1 %collective-permute-start.13 = (f32[8,128]{1,0:T(8,128)S(1)}, f32[8,128]{1,0:T(8,128)S(1)}, u32[]{:S(2)}, u32[]{:S(2)}) collective-permute-start(f32[8,128]{1,0:T(8,128)S(1)} %get-tuple-element.37.refs_4_), channel_id=1, source_target_pairs={{0,2},{1,3},{2,0},{3,1},{4,6},{5,7},{6,4},{7,5},{8,10},{9,11},{10,... | collective-permute-start | bytes 12296 | tf_op jit(solution)/shard_map/ppermute | solution.py:425
  48.6 2.5 %collective-permute-done.13.refs_6_ = f32[8,128]{1,0:T(8,128)S(1)} collective-permute-done((f32[8,128]{1,0:T(8,128)S(1)}, f32[8,128]{1,0:T(8,128)S(1)}, u32[]{:S(2)}, u32[]{:S(2)}) %collective-permute-start.13) | collective-permute-done | bytes 4128 | tf_op jit(solution)/shard_map/ppermute | solution.py:425
  51.1 1.0 %shard_map.119 = (f32[8,64,128]{2,1,0:T(8,128)}, f32[8,64,128]{2,1,0:T(8,128)}) custom-call(f32[136,128]{1,0:T(8,128)S(1)} %shard_map.117.refs_0_, f32[136,128]{1,0:T(8,128)S(1)} %collective-permute-done.9.refs_1_, f32[136,128]{1,0:T(8,128)S(1)} %collective-permute-done.10.refs_2_, f32[136,128]{1,0:T(8,128)S(1)} %collective-permute-done.11.refs_3_, ...), custom_call_target="tpu_custom_call" | custom-call | flops 1310720 | bytes 1572864 | tf_op jit(solution)/shard_map/pallas_call | solution.py:332
  (30 shorter events, 1.2 us)
Async XLA Ops:
  0.6 18.3 %copy-start.4 = (f32[1,8,64,128]{3,2,1,0:T(8,128)S(1)}, f32[1,8,64,128]{3,2,1,0:T(8,128)}, u32[]{:S(2)}) copy-start(f32[1,8,64,128]{3,2,1,0:T(8,128)} %param.10) | copy-start | bytes 786436
  0.6 21.9 %copy-start.2 = (f32[1,8,64,128]{3,2,1,0:T(8,128)S(1)}, f32[1,8,64,128]{3,2,1,0:T(8,128)}, u32[]{:S(2)}) copy-start(f32[1,8,64,128]{3,2,1,0:T(8,128)} %param.13) | copy-start | bytes 786436
  0.7 21.9 %copy-start.1 = (f32[1,8,64,128]{3,2,1,0:T(8,128)S(1)}, f32[1,8,64,128]{3,2,1,0:T(8,128)}, u32[]{:S(2)}) copy-start(f32[1,8,64,128]{3,2,1,0:T(8,128)} %param.12) | copy-start | bytes 786436
  0.7 18.3 %copy-start = (f32[8,64,128]{2,1,0:T(8,128)S(1)}, f32[8,64,128]{2,1,0:T(8,128)}, u32[]{:S(2)}) copy-start(f32[8,64,128]{2,1,0:T(8,128)} %refs_8_.1) | copy-start | bytes 786436
  0.7 18.3 %copy-start.3 = (f32[1,8,64,128]{3,2,1,0:T(8,128)S(1)}, f32[1,8,64,128]{3,2,1,0:T(8,128)}, u32[]{:S(2)}) copy-start(f32[1,8,64,128]{3,2,1,0:T(8,128)} %param.11) | copy-start | bytes 786436
  0.7 10.5 %collective-permute-start.3 = (f32[8,64,128]{2,1,0:T(8,128)}, f32[8,64,128]{2,1,0:T(8,128)S(1)}, u32[]{:S(2)}, u32[]{:S(2)}) collective-permute-start(f32[8,64,128]{2,1,0:T(8,128)} %bitcast.13), channel_id=1, source_target_pairs={{1,2},{2,1},{5,6},{6,5},{9,10},{10,9},{13,14},{14,13},{17,18},{18,... | collective-permute-start | bytes 786440 | tf_op jit(solution)/shard_map/ppermute | solution.py:360
  2.8 19.8 %collective-permute-start = (f32[15,64,128]{2,1,0:T(8,128)S(1)}, f32[15,64,128]{2,1,0:T(8,128)S(1)}, u32[]{:S(2)}, u32[]{:S(2)}) collective-permute-start(f32[15,64,128]{2,1,0:T(8,128)S(1)} %get-tuple-element.24), channel_id=1, source_target_pairs={{0,1},{2,3},{1,0},{3,2},{4,5},{6,7},{5,4},{7,6},{8,9},{10,11},{9,8... | collective-permute-start | bytes 1474568 | tf_op jit(solution)/shard_map/ppermute | solution.py:361
  7.1 15.4 %collective-permute-start.1 = (f32[15,64,128]{2,1,0:T(8,128)S(1)}, f32[15,64,128]{2,1,0:T(8,128)S(1)}, u32[]{:S(2)}, u32[]{:S(2)}) collective-permute-start(f32[15,64,128]{2,1,0:T(8,128)S(1)} %get-tuple-element.25), channel_id=1, source_target_pairs={{1,2},{2,1},{5,6},{6,5},{9,10},{10,9},{13,14},{14,13},{17,18},{18,... | collective-permute-start | bytes 1474568 | tf_op jit(solution)/shard_map/ppermute | solution.py:360
  9.2 9.8 %collective-permute-start.4 = (f32[14,64,128]{2,1,0:T(8,128)S(1)}, f32[14,64,128]{2,1,0:T(8,128)S(1)}, u32[]{:S(2)}, u32[]{:S(2)}) collective-permute-start(f32[14,64,128]{2,1,0:T(8,128)S(1)} %get-tuple-element.26), channel_id=1, source_target_pairs={{0,1},{2,3},{1,0},{3,2},{4,5},{6,7},{5,4},{7,6},{8,9},{10,11},{9,8... | collective-permute-start | bytes 1376264 | tf_op jit(solution)/shard_map/ppermute | solution.py:361
  10.5 8.4 %collective-permute-start.5 = (f32[14,64,128]{2,1,0:T(8,128)S(1)}, f32[14,64,128]{2,1,0:T(8,128)S(1)}, u32[]{:S(2)}, u32[]{:S(2)}) collective-permute-start(f32[14,64,128]{2,1,0:T(8,128)S(1)} %get-tuple-element.27), channel_id=1, source_target_pairs={{1,2},{2,1},{5,6},{6,5},{9,10},{10,9},{13,14},{14,13},{17,18},{18,... | collective-permute-start | bytes 1376264 | tf_op jit(solution)/shard_map/ppermute | solution.py:360
  11.2 7.7 %collective-permute-start.2 = (f32[8,64,128]{2,1,0:T(8,128)}, f32[8,64,128]{2,1,0:T(8,128)S(1)}, u32[]{:S(2)}, u32[]{:S(2)}) collective-permute-start(f32[8,64,128]{2,1,0:T(8,128)} %bitcast.14), channel_id=1, source_target_pairs={{0,1},{2,3},{1,0},{3,2},{4,5},{6,7},{5,4},{7,6},{8,9},{10,11},{9,8... | collective-permute-start | bytes 786440 | tf_op jit(solution)/shard_map/ppermute | solution.py:361
  14.9 0.7 %copy-start.5 = (f32[1,8,128]{2,1,0:T(8,128)S(1)}, f32[1,8,128]{2,1,0:T(8,128)}, u32[]{:S(2)}) copy-start(f32[1,8,128]{2,1,0:T(8,128)} %param.15) | copy-start | bytes 12292
  15.6 0.7 %copy-start.6 = (s32[1,128]{1,0:T(1,128)S(1)}, s32[1,128]{1,0:T(1,128)}, u32[]{:S(2)}) copy-start(s32[1,128]{1,0:T(1,128)} %rec_ref.1) | copy-start | bytes 1540
  16.2 2.7 %copy-start.7 = (f32[1,8]{1,0:T(1,128)S(1)}, f32[1,8]{1,0:T(1,128)}, u32[]{:S(2)}) copy-start(f32[1,8]{1,0:T(1,128)} %wavelet.1) | copy-start | bytes 100
  26.3 4.4 %collective-permute-start.6 = (f32[128,128]{1,0:T(8,128)S(1)}, f32[128,128]{1,0:T(8,128)S(1)}, u32[]{:S(2)}, u32[]{:S(2)}) collective-permute-start(f32[128,128]{1,0:T(8,128)S(1)} %get-tuple-element.32), channel_id=1, source_target_pairs={{0,4},{4,0},{8,12},{12,8},{1,5},{5,1},{9,13},{13,9},{2,6},{6,2},{1... | collective-permute-start | bytes 196616 | tf_op jit(solution)/shard_map/ppermute | solution.py:407
  27.9 5.9 %collective-permute-start.7 = (f32[128,128]{1,0:T(8,128)S(1)}, f32[128,128]{1,0:T(8,128)S(1)}, u32[]{:S(2)}, u32[]{:S(2)}) collective-permute-start(f32[128,128]{1,0:T(8,128)S(1)} %get-tuple-element.33), channel_id=1, source_target_pairs={{0,8},{4,12},{8,0},{12,4},{1,9},{5,13},{9,1},{13,5},{2,10},{6,14},... | collective-permute-start | bytes 196616 | tf_op jit(solution)/shard_map/ppermute | solution.py:407
  30.5 6.1 %collective-permute-start.8 = (f32[128,128]{1,0:T(8,128)S(1)}, f32[128,128]{1,0:T(8,128)S(1)}, u32[]{:S(2)}, u32[]{:S(2)}) collective-permute-start(f32[128,128]{1,0:T(8,128)S(1)} %get-tuple-element.34), channel_id=1, source_target_pairs={{0,12},{4,8},{8,4},{12,0},{1,13},{5,9},{9,5},{13,1},{2,14},{6,10},... | collective-permute-start | bytes 196616 | tf_op jit(solution)/shard_map/ppermute | solution.py:407
  36.6 6.4 %collective-permute-start.11 = (f32[136,128]{1,0:T(8,128)S(1)}, f32[136,128]{1,0:T(8,128)S(1)}, u32[]{:S(2)}, u32[]{:S(2)}) collective-permute-start(f32[136,128]{1,0:T(8,128)S(1)} %shard_map.117.refs_0_), channel_id=1, source_target_pairs={{0,12},{4,8},{8,4},{12,0},{1,13},{5,9},{9,5},{13,1},{2,14},{6,10},... | collective-permute-start | bytes 208904 | tf_op jit(solution)/shard_map/ppermute | solution.py:407
  37.8 8.6 %collective-permute-start.10 = (f32[136,128]{1,0:T(8,128)S(1)}, f32[136,128]{1,0:T(8,128)S(1)}, u32[]{:S(2)}, u32[]{:S(2)}) collective-permute-start(f32[136,128]{1,0:T(8,128)S(1)} %shard_map.117.refs_0_), channel_id=1, source_target_pairs={{0,8},{4,12},{8,0},{12,4},{1,9},{5,13},{9,1},{13,5},{2,10},{6,14},... | collective-permute-start | bytes 208904 | tf_op jit(solution)/shard_map/ppermute | solution.py:407
  37.8 8.6 %collective-permute-start.9 = (f32[136,128]{1,0:T(8,128)S(1)}, f32[136,128]{1,0:T(8,128)S(1)}, u32[]{:S(2)}, u32[]{:S(2)}) collective-permute-start(f32[136,128]{1,0:T(8,128)S(1)} %shard_map.117.refs_0_), channel_id=1, source_target_pairs={{0,4},{4,0},{8,12},{12,8},{1,5},{5,1},{9,13},{13,9},{2,6},{6,2},{1... | collective-permute-start | bytes 208904 | tf_op jit(solution)/shard_map/ppermute | solution.py:407
  46.4 4.7 %collective-permute-start.12 = (f32[72,128]{1,0:T(8,128)S(1)}, f32[72,128]{1,0:T(8,128)S(1)}, u32[]{:S(2)}, u32[]{:S(2)}) collective-permute-start(f32[72,128]{1,0:T(8,128)S(1)} %get-tuple-element.38), channel_id=1, source_target_pairs={{0,1},{1,0},{2,3},{3,2},{4,5},{5,4},{6,7},{7,6},{8,9},{9,8},{10,11... | collective-permute-start | bytes 110600 | tf_op jit(solution)/shard_map/ppermute | solution.py:425
  46.6 4.5 %collective-permute-start.14 = (f32[72,128]{1,0:T(8,128)S(1)}, f32[72,128]{1,0:T(8,128)S(1)}, u32[]{:S(2)}, u32[]{:S(2)}) collective-permute-start(f32[72,128]{1,0:T(8,128)S(1)} %get-tuple-element.39), channel_id=1, source_target_pairs={{0,3},{1,2},{2,1},{3,0},{4,7},{5,6},{6,5},{7,4},{8,11},{9,10},{10,... | collective-permute-start | bytes 110600 | tf_op jit(solution)/shard_map/ppermute | solution.py:425
  47.5 3.6 %collective-permute-start.13 = (f32[8,128]{1,0:T(8,128)S(1)}, f32[8,128]{1,0:T(8,128)S(1)}, u32[]{:S(2)}, u32[]{:S(2)}) collective-permute-start(f32[8,128]{1,0:T(8,128)S(1)} %get-tuple-element.37.refs_4_), channel_id=1, source_target_pairs={{0,2},{1,3},{2,0},{3,1},{4,6},{5,7},{6,4},{7,5},{8,10},{9,11},{10,... | collective-permute-start | bytes 12296 | tf_op jit(solution)/shard_map/ppermute | solution.py:425

commit v5 on v4

v5 whole, which is shorter than its diff:
```python
import functools

import jax
import jax.numpy as jnp
from jax import lax
from jax.experimental import pallas as pl
from jax.experimental.pallas import tpu as pltpu
from jax.sharding import PartitionSpec as P

ITERS = 8
REACH = ITERS
GUARD = 8
LANES = 128
LIMIT = 16 * 2**20
VMEM = pltpu.VMEM
SMEM = pltpu.SMEM


def pairs(count, start):
    low = [(i, i + 1) for i in range(start, count - 1, 2)]
    return low + [(b, a) for a, b in low]


def partner_perms(count):
    if count & (count - 1) == 0:
        return {m: [(i, i ^ m) for i in range(count)] for m in range(1, count)}
    return {m: [(i, (i + m) % count) for i in range(count)] for m in range(1, count)}


def far_first(count):
    half = count // 2
    return [*range(half, count), *range(1, half)]


def send_slot(me, m, count):
    return me ^ m if count & (count - 1) == 0 else lax.rem(me + m, count)


def from_slot(me, m, count):
    return me ^ m if count & (count - 1) == 0 else lax.rem(me - m + count, count)


def spec(space):
    return pl.BlockSpec(memory_space=space)


def cost(flops, nbytes):
    return pl.CostEstimate(flops=int(flops), bytes_accessed=int(nbytes), transcendentals=0)


def is_even():
    return lax.rem(lax.axis_index("slab"), 2) == 0


def pack_kernel(depth, sizes, *refs):
    count = (len(refs) - 4) // 2
    args, (to_a, to_b), whole, (sem, own_sem) = (
        refs[:count], refs[count : count + 2], refs[count + 2 : -2], refs[-2:],
    )

    def copies(up_a, up_b):
        out = []
        for j, (dst, up) in enumerate(((to_a, up_a), (to_b, up_b))):
            at = 0
            for i, (field, size) in enumerate(zip(args, sizes)):
                out.append(
                    pltpu.make_async_copy(
                        field.at[pl.ds(depth - size if up else 0, size)],
                        dst.at[pl.ds(at, size)],
                        sem.at[j, i],
                    )
                )
                at += size
        return out

    even = is_even()

    @pl.when(even)
    def _():
        for c in copies(True, False):
            c.start()

    @pl.when(jnp.logical_not(even))
    def _():
        for c in copies(False, True):
            c.start()

    own = [
        pltpu.make_async_copy(src, dst, own_sem.at[i]) for i, (src, dst) in enumerate(zip(args, whole))
    ]
    for c in own:
        c.start()
    for c in copies(False, False) + own:
        c.wait()


def hot_rows(base, rec_ref, left):
    index = rec_ref[...]
    row_of = index // LANES
    lane_of = index - row_of * LANES
    row_of = row_of - base
    group = 128
    for first in range(0, left.shape[0], group):
        at = lax.broadcasted_iota(jnp.int32, (group, LANES), 0) + first
        hot = jnp.where(at == row_of, 1.0, 0.0).astype(jnp.bfloat16)
        for part in range(3):
            left[pl.ds(first, group), pl.ds(part * LANES, LANES)] = hot
    return lane_of


def residuals(left, first, size, lane_of, value):
    mine = lax.broadcasted_iota(jnp.int32, (LANES, LANES), 0) == lane_of
    parts = []
    for _ in range(3):
        piece = value.astype(jnp.bfloat16).astype(jnp.float32)
        value = value - piece
        parts.append(jnp.where(mine, piece, 0.0).astype(jnp.bfloat16))
    return lax.dot_general(
        left[pl.ds(first, size), :], jnp.concatenate(parts, axis=1),
        (((1,), (1,)), ((), ())), preferred_element_type=jnp.float32,
    )


def around(src, p, width, first, last):
    starts = range(GUARD, GUARD + width, 8)
    here = [src[p, pl.ds(r, 8), :] for r in starts]
    after = [pltpu.roll(c, LANES - 1, 1) for c in here]
    before = [pltpu.roll(c, 1, 1) for c in here]
    out = []
    for r, c, x, y in zip(starts, here, after, before):
        s = src[p + 1, pl.ds(r, 8), :] + src[p - 1, pl.ds(r, 8), :]
        s = s + src[p, pl.ds(r + 1, 8), :]
        s = s + src[p, pl.ds(r - 1, 8), :]
        s = s + jnp.where(last, 0.0, x)
        s = s + jnp.where(first, 0.0, y)
        out.append((r - GUARD, c, s))
    return out


def edges():
    lane = lax.broadcasted_iota(jnp.int32, (8, LANES), 1)
    return lane == 0, lane == LANES - 1


def clear_guards(field):
    planes, rows, _ = field.shape
    zero = jnp.zeros((GUARD, LANES), jnp.float32)
    for p in range(planes):
        field[p, pl.ds(0, GUARD), :] = zero
        field[p, pl.ds(rows - GUARD, GUARD), :] = zero


def fill(depth, width, reach, own, a_in, b_in, bufs):
    rows = [pl.ds(GUARD if buf.shape[1] > width else 0, width) for buf in bufs]
    for src, buf, r in zip(own, bufs, rows):
        for p in range(depth):
            buf[reach + p, r, :] = src[p]

    def put(low, high):
        for buf, r, (lo, at, size), (hi, _, _) in zip(bufs, rows, low, high):
            for p in range(size):
                buf[reach - size + p, r, :] = lo[at + p]
                buf[reach + depth + p, r, :] = hi[at + p]

    even = is_even()

    @pl.when(even)
    def _():
        put(b_in, a_in)

    @pl.when(jnp.logical_not(even))
    def _():
        put(a_in, b_in)


def forward_kernel(
    depth, width, wavelet, src_index, rec_index, misfit, now, later, model, ua_in, ub_in, ha_in, hb_in,
    u_out, later_out, lap_out, a_edge, b_edge, mod, weight, extra,
    amplitude, sem, left, cur, old,
):
    n = REACH - 1
    slab = lax.axis_index("slab")
    fetch = pltpu.make_async_copy(wavelet, amplitude, sem)
    fetch.start()
    clear_guards(cur)
    clear_guards(old)
    fill(
        depth, width, REACH, (now, later, model),
        ((ua_in, 0, REACH), (ha_in, 0, n), (ha_in, n, n)),
        ((ub_in, 0, REACH), (hb_in, 0, n), (hb_in, n, n)),
        (cur, old, mod),
    )
    lane_of = hot_rows((slab * depth - n) * width, rec_index, left)
    fetch.wait()
    for p in range(1, depth + 2 * REACH - 1):
        weight[p] = 2.0 - 6.0 * mod[p]
    first, last = edges()
    source = src_index[0]
    src_row = source // LANES
    src_lane = source - src_row * LANES
    src_row = src_row - (slab * depth - REACH) * width
    bufs = (cur, old)
    for k in range(ITERS):
        s, d = bufs[k % 2], bufs[(k + 1) % 2]
        low, high = (k + 1, depth + 2 * n - 1 - k) if k < n else (n, n + depth)
        extra[k, pl.ds(low * width, (high - low) * width), :] = residuals(
            left, low * width, (high - low) * width, lane_of, misfit[pl.ds(k, 1), :]
        )
        for p in range(k + 1, depth + 2 * REACH - 1 - k):
            for r, c, total in around(s, p, width, first, last):
                lap = total - 6.0 * c
                here = (p, pl.ds(GUARD + r, 8), slice(None))
                d[here] = 2.0 * c - d[here] + mod[p, pl.ds(r, 8), :] * lap
                if REACH <= p < REACH + depth:
                    lap_out[k, p - REACH, pl.ds(r, 8), :] = lap

        @pl.when((src_row >= (k + 1) * width) & (src_row < (depth + 2 * REACH - 1 - k) * width))
        def _():
            plane = src_row // width
            here = (plane, pl.ds(GUARD + src_row - plane * width, 1), slice(None))
            at = lax.broadcasted_iota(jnp.int32, (1, LANES), 1) == src_lane
            d[here] = d[here] + jnp.where(at, amplitude[0, k], 0.0)

    u, u_later = bufs[ITERS % 2], bufs[(ITERS + 1) % 2]
    rows = pl.ds(GUARD, width)
    even = is_even()
    a_edge[...] = u[jnp.where(even, REACH + depth - 1, REACH), rows, :]
    b_edge[...] = u[jnp.where(even, REACH, REACH + depth - 1), rows, :]
    for p in range(depth):
        u_out[p] = u[REACH + p, rows, :]
        later_out[p] = u_later[REACH + p, rows, :]


def adjoint_kernel(
    depth, width, shots, now, later, a_in, b_in, mod, weight, laps, extra, ua_edge, ub_edge,
    a_out, later_out, a_edge, b_edge, *rest
):
    *pieces, image, cur, old = rest
    n = REACH - 1
    clear_guards(cur)
    clear_guards(old)
    fill(
        depth, width, n, (now, later),
        ((a_in, 0, n), (a_in, n, n - 1)), ((b_in, 0, n), (b_in, n, n - 1)),
        (cur, old),
    )
    first, last = edges()
    bufs = (cur, old)

    def imaged(k, p, r, c):
        into = pl.ds((p - n) * width + r, 8)
        add = c * laps[k, p - n, pl.ds(r, 8), :]
        image[into, :] = image[into, :] + add if k > 0 else add

    for k in range(n):
        s, d = bufs[k % 2], bufs[(k + 1) % 2]
        for p in range(k + 1, depth + 2 * n - 1 - k):
            for r, c, total in around(s, p, width, first, last):
                here = (p, pl.ds(GUARD + r, 8), slice(None))
                rows = pl.ds(r, 8)
                new = weight[p + 1, rows, :] * c - d[here] + mod[p + 1, rows, :] * total
                d[here] = new + extra[k, pl.ds(p * width + r, 8), :]
                if n <= p < n + depth:
                    imaged(k, p, r, c)

    a, a_later = bufs[n % 2], bufs[(n + 1) % 2]
    for p in range(n, n + depth):
        for r in range(0, width, 8):
            imaged(n, p, r, a[p, pl.ds(GUARD + r, 8), :])
    size = depth * width // shots
    me = lax.axis_index("shot")
    for m in range(shots):
        to = me if m == 0 else send_slot(me, m, shots)
        pieces[m][...] = image[pl.ds(pl.multiple_of(to * size, size), size), :]
    rows = pl.ds(GUARD, width)
    for p in range(depth):
        a_out[p] = a[n + p, rows, :]
        later_out[p] = a_later[n + p, rows, :]
    even = is_even()
    a_edge[0] = ua_edge[...]
    b_edge[0] = ub_edge[...]
    a_edge[1] = a[jnp.where(even, n + depth - 1, n), rows, :]
    b_edge[1] = a[jnp.where(even, n, n + depth - 1), rows, :]


def last_kernel(
    depth, width, u, u_later, a, a_later, a_in, b_in, mod, weight, extra,
    base_out, lap_out, adjoint_out,
    upad, apad,
):
    n = REACH - 1
    clear_guards(upad)
    clear_guards(apad)
    fill(
        depth, width, 1, (u, a), ((a_in, 0, 1), (a_in, 1, 1)), ((b_in, 0, 1), (b_in, 1, 1)),
        (upad, apad),
    )
    first, last = edges()
    for p in range(depth):
        for r, c, total in around(upad, p + 1, width, first, last):
            rows = pl.ds(r, 8)
            lap_out[p, rows, :] = total - 6.0 * c
            base_out[p, rows, :] = 2.0 * c - u_later[p, rows, :]
        for r, c, total in around(apad, p + 1, width, first, last):
            rows = pl.ds(r, 8)
            q = REACH + p
            new = weight[q, rows, :] * c - a_later[p, rows, :] + mod[q, rows, :] * total
            adjoint_out[p, rows, :] = new + extra[n, pl.ds((n + p) * width + r, 8), :]


def sum_kernel(*refs):
    *parts, out = refs
    n = parts[0].shape[0]
    top = jnp.zeros((8, LANES), jnp.float32)
    for r in range(0, n, 8):
        total = parts[0][pl.ds(r, 8), :]
        for part in parts[1:]:
            total = total + part[pl.ds(r, 8), :]
        out[pl.ds(r, 8), :] = total
        top = jnp.maximum(top, jnp.abs(total))
    out[pl.ds(n, 8), :] = top


def top_kernel(*refs):
    *parts, out = refs
    n = parts[0].shape[0] - 8
    top = parts[0][pl.ds(n, 8), :]
    for part in parts[1:]:
        top = jnp.maximum(top, part[pl.ds(n, 8), :])
    out[...] = top


def update_kernel(depth, width, shots, *refs):
    grads, refs = refs[:shots], refs[shots:]
    *tops, model, base, laps, new_model, stepped, grad = refs
    n = depth * width // shots
    me = lax.axis_index("shot")
    for m in range(shots):
        owner = me if m == 0 else from_slot(me, m, shots)
        grad[pl.ds(pl.multiple_of(owner * n, n), n), :] = grads[m][pl.ds(0, n), :]
    top = tops[0][...]
    for other in tops[1:]:
        top = jnp.maximum(top, other[...])
    peak = jnp.max(top)
    for p in range(depth):
        for r in range(0, width, 8):
            g = grad[pl.ds(p * width + r, 8), :]
            rows = pl.ds(r, 8)
            new = jnp.clip(model[p, rows, :] - 0.1 * g / (peak + 1e-06), 0.05, 0.3)
            new_model[p, rows, :] = new
            stepped[p, rows, :] = base[p, rows, :] + new * laps[p, rows, :]


def placed(x, space):
    if space is VMEM or space is pltpu.HBM:
        return pltpu.with_memory_space_constraint(x, space)
    return x


def call(kernel, outs, args, spaces, scratch, flops, nbytes):
    args = [placed(x, space) for x, space in zip(args, spaces)]
    return pl.pallas_call(
        kernel,
        out_shape=outs,
        in_specs=[spec(space) for space in spaces],
        out_specs=[spec(VMEM)] * len(outs),
        scratch_shapes=scratch,
        cost_estimate=cost(flops, nbytes),
        compiler_params=pltpu.CompilerParams(vmem_limit_bytes=LIMIT),
    )(*args)


def per_device(model, fwd_now, fwd_next, adj_now, adj_next, wavelet, misfit, src_index, rec_index):
    f32 = jnp.float32
    depth, width, length = model.shape
    assert length == LANES and fwd_now.shape[0] == 1 and width % 8 == 0 and depth == REACH
    u0, u1, a0, a1 = fwd_now[0], fwd_next[0], adj_now[0], adj_next[0]
    slabs, shots = lax.axis_size("slab"), lax.axis_size("shot")
    perm_a, perm_b = pairs(slabs, 0), pairs(slabs, 1)
    planes = depth + 2 * REACH
    cells = depth * width * LANES
    own = VMEM((depth, width, LANES), f32)
    wide = VMEM((planes, width, LANES), f32)
    field = VMEM((planes, width + 2 * GUARD, LANES), f32)
    edge = VMEM((width, LANES), f32)
    out = jax.ShapeDtypeStruct((depth, width, LANES), f32)
    n = REACH - 1

    def exchange(to_a, to_b):
        b = lax.ppermute(to_b, "slab", perm_b)
        return lax.ppermute(to_a, "slab", perm_a), b

    def packed(args, sizes):
        total = sum(sizes)
        to_a, to_b, *whole = call(
            functools.partial(pack_kernel, depth, sizes),
            [VMEM((total, width, LANES), f32)] * 2 + [VMEM(x.shape, x.dtype) for x in args],
            args, [pltpu.HBM] * len(args),
            [pltpu.SemaphoreType.DMA((2, len(sizes))), pltpu.SemaphoreType.DMA((len(args),))],
            0, 4 * 4 * total * width * LANES,
        )
        return (to_a, to_b), whole

    ua, ub = exchange(u0, u0)
    to, (u1, model, u0) = packed((u1, model, u0), (n, n))
    ha, hb = exchange(*to)
    to, (a0, a1, rec_index, misfit) = packed((a0, a1, rec_index, misfit[0]), (n, n - 1))
    ga, gb = exchange(*to)
    near = depth + 2 * n
    u, u_later, laps, ua_edge, ub_edge, mod, weight, extra = call(
        functools.partial(forward_kernel, depth, width),
        [
            own, own, VMEM((ITERS, depth, width, LANES), f32), edge, edge, wide, wide,
            VMEM((ITERS, near * width, LANES), f32),
        ],
        (wavelet, src_index, rec_index, misfit, u0, u1, model, ua, ub, ha, hb),
        [pltpu.HBM, SMEM] + [VMEM] * 9,
        [
            SMEM(wavelet.shape, f32), pltpu.SemaphoreType.DMA,
            VMEM((near * width, 3 * LANES), jnp.bfloat16), field, field,
        ],
        15 * ITERS * 2 * cells, 80 * cells,
    )
    rows = depth * width // shots
    both = VMEM((2, width, LANES), f32)
    field = VMEM((near, width + 2 * GUARD, LANES), f32)
    a, a_later, a_edge, b_edge, *pieces = call(
        functools.partial(adjoint_kernel, depth, width, shots),
        [own, own, both, both] + [VMEM((rows, LANES), f32)] * shots,
        (a0, a1, ga, gb, mod, weight, laps, extra, ua_edge, ub_edge), [VMEM] * 10,
        [VMEM((depth * width, LANES), f32), field, field],
        18 * ITERS * 2 * cells, 80 * cells,
    )

    def with_others(own_one, pieces, axis):
        got, perms = {}, partner_perms(lax.axis_size(axis))
        for m in far_first(len(perms) + 1):
            got[m] = lax.ppermute(pieces[m], axis, perms[m])
        return [own_one] + [got[m] for m in sorted(got)]

    parts = with_others(pieces[0], pieces, "shot")
    a_edge, b_edge = exchange(a_edge, b_edge)
    (grad,) = call(
        sum_kernel, [VMEM((rows + 8, LANES), f32)], parts, [VMEM] * shots, [],
        shots * rows * LANES, 4 * shots * rows * LANES,
    )
    grads = with_others(grad, [grad] * shots, "shot")
    pad = VMEM((depth + 2, width + 2 * GUARD, LANES), f32)
    base, lap, a = call(
        functools.partial(last_kernel, depth, width), [own, own, out],
        (u, u_later, a, a_later, a_edge, b_edge, mod, weight, extra), [VMEM] * 9,
        [pad, pad], 30 * cells, 32 * cells,
    )
    (top,) = call(top_kernel, [VMEM((8, LANES), f32)], grads, [VMEM] * shots, [], 0, 4096 * shots)
    tops = with_others(top, [top] * slabs, "slab")
    new_model, stepped = call(
        functools.partial(update_kernel, depth, width, shots), [out, out],
        (*grads, *tops, model, base, lap), [VMEM] * (shots + slabs + 3),
        [VMEM((depth * width, LANES), f32)], 10 * cells, 4 * 6 * cells,
    )
    return new_model, stepped[None], a[None]


def solution(mesh):
    in_specs = (
        P(("groups", "slab"), None, None),
        P(("groups", "shot"), "slab", None, None),
        P(("groups", "shot"), "slab", None, None),
        P(("groups", "shot"), "slab", None, None),
        P(("groups", "shot"), "slab", None, None),
        P(("groups", "shot"), None),
        P(("groups", "shot"), None, None),
        P(("groups", "shot")),
        P(("groups", "shot"), None),
    )
    out_specs = (
        P(("groups", "slab"), None, None),
        P(("groups", "shot"), "slab", None, None),
        P(("groups", "shot"), "slab", None, None),
    )
    return jax.shard_map(per_device, mesh=mesh, in_specs=in_specs, out_specs=out_specs, check_vma=False)
```

time: 52.4 us -> 47.6 us (0.908)
  Pallas kernels: 13.6 us -> 11.6 us
  waiting for transfers between devices: 13.7 us -> 12.1 us
  local copies, waits for them, and re-layouts: 1.37 us -> 0 us
    ppermute x9, waiting for transfers between devices: 13.7 us -> 11.4 us  [with_others(): got[m] = lax.ppermute(pieces[m], axis, perms[m])]
    pallas_call x8, Pallas kernels: 13.6 us -> 11.6 us  [call(): pl.pallas_call(kernel, out_shape=outs, in_specs=[spec(space) for space in...]
    unnamed x16 -> x0, local copies, waits for them, and re-layouts: 1.37 us -> none
    ppermute x3 -> x4, waiting for transfers between devices: 0.01 us -> 0.73 us  [exchange(): return (lax.ppermute(to_a, 'slab', perm_a), b)]
    ppermute x3 -> x4, starting transfers between devices: 2.17 us -> 2.68 us  [exchange(): b = lax.ppermute(to_b, 'slab', perm_b)]
    ppermute x3 -> x4, starting transfers between devices: 8.74 us -> 8.71 us  [exchange(): return (lax.ppermute(to_a, 'slab', perm_a), b)]
  transfers between devices with their start and end apart: 15 -> 17, of which waited for: 5 -> 7; matrix products, arithmetic and copies ran while one was open for 0% -> 0% of each run, Pallas kernels for 17% -> 17%
where the time goes in v5:
time: 47.6 us; the launch traced here: 47.3 us
  starting transfers between devices  22.2 us (47%)
  waiting for transfers between devices  12.1 us (25%)
  Pallas kernels  11.6 us (24%)
  between operations  1.39 us (3%)
    pallas_call x8, Pallas kernels, call(): pl.pallas_call(kernel, out_shape=outs, in_specs=[spec(space) for space in...  11.6 us
    ppermute x9, waiting for transfers between devices, with_others(): got[m] = lax.ppermute(pieces[m], axis, perms[m])  11.4 us
    ppermute x9, starting transfers between devices, with_others(): got[m] = lax.ppermute(pieces[m], axis, perms[m])  10.8 us
    ppermute x4, starting transfers between devices, exchange(): return (lax.ppermute(to_a, 'slab', perm_a), b)  8.71 us
    ppermute x4, starting transfers between devices, exchange(): b = lax.ppermute(to_b, 'slab', perm_b)  2.68 us
  transfers between devices with their start and end apart: 17, of which 7 were waited for; matrix products, arithmetic and copies ran while one was open for 0% of the time, Pallas kernels for 17%

profile of v5, /device:TPU:0, one launch (start us, length us, event | category | flops | bytes accessed | tf_op | source)
XLA Modules:
  0.0 47.3 jit_solution(7176572348620977927)
XLA Ops:
  0.6 0.7 %collective-permute-start.3 = (f32[8,64,128]{2,1,0:T(8,128)}, f32[8,64,128]{2,1,0:T(8,128)S(1)}, u32[]{:S(2)}, u32[]{:S(2)}) collective-permute-start(f32[8,64,128]{2,1,0:T(8,128)} %bitcast.8), channel_id=1, source_target_pairs={{1,2},{2,1},{5,6},{6,5},{9,10},{10,9},{13,14},{14,13},{17,18},{18,... | collective-permute-start | bytes 786440 | tf_op jit(solution)/shard_map/ppermute | solution.py:390
  1.3 1.5 %shard_map.113 = (f32[14,64,128]{2,1,0:T(8,128)S(1)}, f32[14,64,128]{2,1,0:T(8,128)S(1)}, f32[8,64,128]{2,1,0:T(8,128)S(1)}, f32[8,64,128]{2,1,0:T(8,128)S(1)}, f32[8,64,128]{2,1,0:T(8,128)S(1)}) custom-call(f32[8,64,128]{2,1,0:T(8,128)} %bitcast.7, f32[8,64,128]{2,1,0:T(8,128)} %refs_1_.1, f32[8,64,128]{2,1,0:T(8,128)} %bitcast.9), custom_call_target="tpu_custom_call" | custom-call | bytes 1835008 | tf_op jit(solution)/shard_map/pallas_call | solution.py:362
  2.8 4.3 %collective-permute-start.4 = (f32[14,64,128]{2,1,0:T(8,128)S(1)}, f32[14,64,128]{2,1,0:T(8,128)S(1)}, u32[]{:S(2)}, u32[]{:S(2)}) collective-permute-start(f32[14,64,128]{2,1,0:T(8,128)S(1)} %get-tuple-element.44), channel_id=1, source_target_pairs={{0,1},{2,3},{1,0},{3,2},{4,5},{6,7},{5,4},{7,6},{8,9},{10,11},{9,8... | collective-permute-start | bytes 1376264 | tf_op jit(solution)/shard_map/ppermute | solution.py:391
  7.2 0.7 %collective-permute-start.5 = (f32[14,64,128]{2,1,0:T(8,128)S(1)}, f32[14,64,128]{2,1,0:T(8,128)S(1)}, u32[]{:S(2)}, u32[]{:S(2)}) collective-permute-start(f32[14,64,128]{2,1,0:T(8,128)S(1)} %get-tuple-element.45), channel_id=1, source_target_pairs={{1,2},{2,1},{5,6},{6,5},{9,10},{10,9},{13,14},{14,13},{17,18},{18,... | collective-permute-start | bytes 1376264 | tf_op jit(solution)/shard_map/ppermute | solution.py:390
  7.8 1.5 %shard_map.112 = (f32[13,64,128]{2,1,0:T(8,128)S(1)}, f32[13,64,128]{2,1,0:T(8,128)S(1)}, f32[8,64,128]{2,1,0:T(8,128)S(1)}, f32[8,64,128]{2,1,0:T(8,128)S(1)}, ...) custom-call(f32[8,64,128]{2,1,0:T(8,128)} %bitcast.11, f32[8,64,128]{2,1,0:T(8,128)} %bitcast.12, s32[1,128]{1,0:T(1,128)} %refs_2_.1, ...), custom_call_target="tpu_custom_call" | custom-call | bytes 1703936 | tf_op jit(solution)/shard_map/pallas_call | solution.py:362
  9.3 1.4 %collective-permute-start = (f32[13,64,128]{2,1,0:T(8,128)S(1)}, f32[13,64,128]{2,1,0:T(8,128)S(1)}, u32[]{:S(2)}, u32[]{:S(2)}) collective-permute-start(f32[13,64,128]{2,1,0:T(8,128)S(1)} %get-tuple-element.37), channel_id=1, source_target_pairs={{0,1},{2,3},{1,0},{3,2},{4,5},{6,7},{5,4},{7,6},{8,9},{10,11},{9,8... | collective-permute-start | bytes 1277960 | tf_op jit(solution)/shard_map/ppermute | solution.py:391
  10.7 0.7 %collective-permute-start.1 = (f32[13,64,128]{2,1,0:T(8,128)S(1)}, f32[13,64,128]{2,1,0:T(8,128)S(1)}, u32[]{:S(2)}, u32[]{:S(2)}) collective-permute-start(f32[13,64,128]{2,1,0:T(8,128)S(1)} %get-tuple-element.38), channel_id=1, source_target_pairs={{1,2},{2,1},{5,6},{6,5},{9,10},{10,9},{13,14},{14,13},{17,18},{18,... | collective-permute-start | bytes 1277960 | tf_op jit(solution)/shard_map/ppermute | solution.py:390
  11.4 3.0 %collective-permute-start.2 = (f32[8,64,128]{2,1,0:T(8,128)}, f32[8,64,128]{2,1,0:T(8,128)S(1)}, u32[]{:S(2)}, u32[]{:S(2)}) collective-permute-start(f32[8,64,128]{2,1,0:T(8,128)} %bitcast.10), channel_id=1, source_target_pairs={{0,1},{2,3},{1,0},{3,2},{4,5},{6,7},{5,4},{7,6},{8,9},{10,11},{9,8... | collective-permute-start | bytes 786440 | tf_op jit(solution)/shard_map/ppermute | solution.py:391
  15.0 0.7 %collective-permute-done.2.ua_in = f32[8,64,128]{2,1,0:T(8,128)S(1)} collective-permute-done((f32[8,64,128]{2,1,0:T(8,128)}, f32[8,64,128]{2,1,0:T(8,128)S(1)}, u32[]{:S(2)}, u32[]{:S(2)}) %collective-permute-start.2) | collective-permute-done | bytes 262176 | tf_op jit(solution)/shard_map/ppermute | solution.py:391
  15.8 4.2 %shard_map.114 = (f32[8,64,128]{2,1,0:T(8,128)S(1)}, f32[8,64,128]{2,1,0:T(8,128)S(1)}, f32[8,8,64,128]{3,2,1,0:T(8,128)S(1)}, f32[64,128]{1,0:T(8,128)S(1)}, f3...) custom-call(f32[1,8]{1,0:T(1,128)} %wavelet.1, ...), custom_call_target="tpu_custom_call" | custom-call | flops 15728640 | bytes 5242880 | tf_op jit(solution)/shard_map/pallas_call | solution.py:362
  19.9 2.3 %shard_map.115 = (f32[8,64,128]{2,1,0:T(8,128)S(1)}, f32[8,64,128]{2,1,0:T(8,128)S(1)}, f32[2,64,128]{2,1,0:T(8,128)S(1)}, f32[2,64,128]{2,1,0:T(8,128)S(1)}, f3...) custom-call(f32[8,64,128]{2,1,0:T(8,128)S(1)} %get-tuple-element.35.now, ...), custom_call_target="tpu_custom_call" | custom-call | flops 18874368 | bytes 5242880 | tf_op jit(solution)/shard_map/pallas_call | solution.py:362
  22.3 1.6 %collective-permute-start.6 = (f32[128,128]{1,0:T(8,128)S(1)}, f32[128,128]{1,0:T(8,128)S(1)}, u32[]{:S(2)}, u32[]{:S(2)}) collective-permute-start(f32[128,128]{1,0:T(8,128)S(1)} %get-tuple-element.53), channel_id=1, source_target_pairs={{0,4},{4,0},{8,12},{12,8},{1,5},{5,1},{9,13},{13,9},{2,6},{6,2},{1... | collective-permute-start | bytes 196616 | tf_op jit(solution)/shard_map/ppermute | solution.py:438
  23.9 2.6 %collective-permute-start.7 = (f32[128,128]{1,0:T(8,128)S(1)}, f32[128,128]{1,0:T(8,128)S(1)}, u32[]{:S(2)}, u32[]{:S(2)}) collective-permute-start(f32[128,128]{1,0:T(8,128)S(1)} %get-tuple-element.54), channel_id=1, source_target_pairs={{0,8},{4,12},{8,0},{12,4},{1,9},{5,13},{9,1},{13,5},{2,10},{6,14},... | collective-permute-start | bytes 196616 | tf_op jit(solution)/shard_map/ppermute | solution.py:438
  26.7 4.1 %collective-permute-done.7.refs_2_ = f32[128,128]{1,0:T(8,128)S(1)} collective-permute-done((f32[128,128]{1,0:T(8,128)S(1)}, f32[128,128]{1,0:T(8,128)S(1)}, u32[]{:S(2)}, u32[]{:S(2)}) %collective-permute-start.7) | collective-permute-done | bytes 65568 | tf_op jit(solution)/shard_map/ppermute | solution.py:438
  30.9 2.5 %collective-permute-done.8.refs_3_ = f32[128,128]{1,0:T(8,128)S(1)} collective-permute-done((f32[128,128]{1,0:T(8,128)S(1)}, f32[128,128]{1,0:T(8,128)S(1)}, u32[]{:S(2)}, u32[]{:S(2)}) %collective-permute-start.8) | collective-permute-done | bytes 65568 | tf_op jit(solution)/shard_map/ppermute | solution.py:438
  33.4 1.2 %collective-permute-start.11 = (f32[136,128]{1,0:T(8,128)S(1)}, f32[136,128]{1,0:T(8,128)S(1)}, u32[]{:S(2)}, u32[]{:S(2)}) collective-permute-start(f32[136,128]{1,0:T(8,128)S(1)} %shard_map.116.refs_0_), channel_id=1, source_target_pairs={{0,12},{4,8},{8,4},{12,0},{1,13},{5,9},{9,5},{13,1},{2,14},{6,10},... | collective-permute-start | bytes 208904 | tf_op jit(solution)/shard_map/ppermute | solution.py:438
  34.5 1.2 %collective-permute-start.10 = (f32[136,128]{1,0:T(8,128)S(1)}, f32[136,128]{1,0:T(8,128)S(1)}, u32[]{:S(2)}, u32[]{:S(2)}) collective-permute-start(f32[136,128]{1,0:T(8,128)S(1)} %shard_map.116.refs_0_), channel_id=1, source_target_pairs={{0,8},{4,12},{8,0},{12,4},{1,9},{5,13},{9,1},{13,5},{2,10},{6,14},... | collective-permute-start | bytes 208904 | tf_op jit(solution)/shard_map/ppermute | solution.py:438
  35.8 2.0 %collective-permute-start.9 = (f32[136,128]{1,0:T(8,128)S(1)}, f32[136,128]{1,0:T(8,128)S(1)}, u32[]{:S(2)}, u32[]{:S(2)}) collective-permute-start(f32[136,128]{1,0:T(8,128)S(1)} %shard_map.116.refs_0_), channel_id=1, source_target_pairs={{0,4},{4,0},{8,12},{12,8},{1,5},{5,1},{9,13},{13,9},{2,6},{6,2},{1... | collective-permute-start | bytes 208904 | tf_op jit(solution)/shard_map/ppermute | solution.py:438
  37.8 0.7 %collective-permute-start.16 = (f32[2,64,128]{2,1,0:T(8,128)S(1)}, f32[2,64,128]{2,1,0:T(8,128)S(1)}, u32[]{:S(2)}, u32[]{:S(2)}) collective-permute-start(f32[2,64,128]{2,1,0:T(8,128)S(1)} %get-tuple-element.61), channel_id=1, source_target_pairs={{1,2},{2,1},{5,6},{6,5},{9,10},{10,9},{13,14},{14,13},{17,18},{18,... | collective-permute-start | bytes 196616 | tf_op jit(solution)/shard_map/ppermute | solution.py:390
  38.5 1.8 %collective-permute-done.11.refs_3_ = f32[136,128]{1,0:T(8,128)S(1)} collective-permute-done((f32[136,128]{1,0:T(8,128)S(1)}, f32[136,128]{1,0:T(8,128)S(1)}, u32[]{:S(2)}, u32[]{:S(2)}) %collective-permute-start.11) | collective-permute-done | bytes 69664 | tf_op jit(solution)/shard_map/ppermute | solution.py:438
  40.3 2.3 %collective-permute-done.10.refs_2_ = f32[136,128]{1,0:T(8,128)S(1)} collective-permute-done((f32[136,128]{1,0:T(8,128)S(1)}, f32[136,128]{1,0:T(8,128)S(1)}, u32[]{:S(2)}, u32[]{:S(2)}) %collective-permute-start.10) | collective-permute-done | bytes 69664 | tf_op jit(solution)/shard_map/ppermute | solution.py:438
  42.6 1.6 %collective-permute-start.13 = (f32[8,128]{1,0:T(8,128)S(1)}, f32[8,128]{1,0:T(8,128)S(1)}, u32[]{:S(2)}, u32[]{:S(2)}) collective-permute-start(f32[8,128]{1,0:T(8,128)S(1)} %shard_map.117.refs_4_), channel_id=1, source_target_pairs={{0,2},{1,3},{2,0},{3,1},{4,6},{5,7},{6,4},{7,5},{8,10},{9,11},{10,... | collective-permute-start | bytes 12296 | tf_op jit(solution)/shard_map/ppermute | solution.py:438
  44.5 1.1 %shard_map.118 = (f32[8,64,128]{2,1,0:T(8,128)S(1)}, f32[8,64,128]{2,1,0:T(8,128)S(1)}, f32[8,64,128]{2,1,0:T(8,128)}) custom-call(f32[8,64,128]{2,1,0:T(8,128)S(1)} %get-tuple-element.56.u, f32[8,64,128]{2,1,0:T(8,128)S(1)} %get-tuple-element.57.u_later, f32[8,64,128]{2,1,0:T(8,128)S(1)} %get-tuple-element.58.a, ...), custom_call_target="tpu_custom_call" | custom-call | flops 1966080 | bytes 2097152 | tf_op jit(solution)/shard_map/pallas_call | solution.py:362
  46.3 1.0 %shard_map.119 = (f32[8,64,128]{2,1,0:T(8,128)}, f32[8,64,128]{2,1,0:T(8,128)}) custom-call(f32[136,128]{1,0:T(8,128)S(1)} %shard_map.116.refs_0_, f32[136,128]{1,0:T(8,128)S(1)} %collective-permute-done.9.refs_1_, f32[136,128]{1,0:T(8,128)S(1)} %collective-permute-done.10.refs_2_, f32[136,128]{1,0:T(8,128)S(1)} %collective-permute-done.11.refs_3_, ...), custom_call_target="tpu_custom_call" | custom-call | flops 655360 | bytes 1572864 | tf_op jit(solution)/shard_map/pallas_call | solution.py:362
  (18 shorter events, 1.3 us)
Async XLA Ops:
  0.6 10.7 %collective-permute-start.3 = (f32[8,64,128]{2,1,0:T(8,128)}, f32[8,64,128]{2,1,0:T(8,128)S(1)}, u32[]{:S(2)}, u32[]{:S(2)}) collective-permute-start(f32[8,64,128]{2,1,0:T(8,128)} %bitcast.8), channel_id=1, source_target_pairs={{1,2},{2,1},{5,6},{6,5},{9,10},{10,9},{13,14},{14,13},{17,18},{18,... | collective-permute-start | bytes 786440 | tf_op jit(solution)/shard_map/ppermute | solution.py:390
  2.8 12.9 %collective-permute-start.4 = (f32[14,64,128]{2,1,0:T(8,128)S(1)}, f32[14,64,128]{2,1,0:T(8,128)S(1)}, u32[]{:S(2)}, u32[]{:S(2)}) collective-permute-start(f32[14,64,128]{2,1,0:T(8,128)S(1)} %get-tuple-element.44), channel_id=1, source_target_pairs={{0,1},{2,3},{1,0},{3,2},{4,5},{6,7},{5,4},{7,6},{8,9},{10,11},{9,8... | collective-permute-start | bytes 1376264 | tf_op jit(solution)/shard_map/ppermute | solution.py:391
  7.2 8.6 %collective-permute-start.5 = (f32[14,64,128]{2,1,0:T(8,128)S(1)}, f32[14,64,128]{2,1,0:T(8,128)S(1)}, u32[]{:S(2)}, u32[]{:S(2)}) collective-permute-start(f32[14,64,128]{2,1,0:T(8,128)S(1)} %get-tuple-element.45), channel_id=1, source_target_pairs={{1,2},{2,1},{5,6},{6,5},{9,10},{10,9},{13,14},{14,13},{17,18},{18,... | collective-permute-start | bytes 1376264 | tf_op jit(solution)/shard_map/ppermute | solution.py:390
  9.3 10.6 %collective-permute-start = (f32[13,64,128]{2,1,0:T(8,128)S(1)}, f32[13,64,128]{2,1,0:T(8,128)S(1)}, u32[]{:S(2)}, u32[]{:S(2)}) collective-permute-start(f32[13,64,128]{2,1,0:T(8,128)S(1)} %get-tuple-element.37), channel_id=1, source_target_pairs={{0,1},{2,3},{1,0},{3,2},{4,5},{6,7},{5,4},{7,6},{8,9},{10,11},{9,8... | collective-permute-start | bytes 1277960 | tf_op jit(solution)/shard_map/ppermute | solution.py:391
  10.7 9.3 %collective-permute-start.1 = (f32[13,64,128]{2,1,0:T(8,128)S(1)}, f32[13,64,128]{2,1,0:T(8,128)S(1)}, u32[]{:S(2)}, u32[]{:S(2)}) collective-permute-start(f32[13,64,128]{2,1,0:T(8,128)S(1)} %get-tuple-element.38), channel_id=1, source_target_pairs={{1,2},{2,1},{5,6},{6,5},{9,10},{10,9},{13,14},{14,13},{17,18},{18,... | collective-permute-start | bytes 1277960 | tf_op jit(solution)/shard_map/ppermute | solution.py:390
  11.4 4.4 %collective-permute-start.2 = (f32[8,64,128]{2,1,0:T(8,128)}, f32[8,64,128]{2,1,0:T(8,128)S(1)}, u32[]{:S(2)}, u32[]{:S(2)}) collective-permute-start(f32[8,64,128]{2,1,0:T(8,128)} %bitcast.10), channel_id=1, source_target_pairs={{0,1},{2,3},{1,0},{3,2},{4,5},{6,7},{5,4},{7,6},{8,9},{10,11},{9,8... | collective-permute-start | bytes 786440 | tf_op jit(solution)/shard_map/ppermute | solution.py:391
  22.3 4.5 %collective-permute-start.6 = (f32[128,128]{1,0:T(8,128)S(1)}, f32[128,128]{1,0:T(8,128)S(1)}, u32[]{:S(2)}, u32[]{:S(2)}) collective-permute-start(f32[128,128]{1,0:T(8,128)S(1)} %get-tuple-element.53), channel_id=1, source_target_pairs={{0,4},{4,0},{8,12},{12,8},{1,5},{5,1},{9,13},{13,9},{2,6},{6,2},{1... | collective-permute-start | bytes 196616 | tf_op jit(solution)/shard_map/ppermute | solution.py:438
  23.9 6.9 %collective-permute-start.7 = (f32[128,128]{1,0:T(8,128)S(1)}, f32[128,128]{1,0:T(8,128)S(1)}, u32[]{:S(2)}, u32[]{:S(2)}) collective-permute-start(f32[128,128]{1,0:T(8,128)S(1)} %get-tuple-element.54), channel_id=1, source_target_pairs={{0,8},{4,12},{8,0},{12,4},{1,9},{5,13},{9,1},{13,5},{2,10},{6,14},... | collective-permute-start | bytes 196616 | tf_op jit(solution)/shard_map/ppermute | solution.py:438
  26.5 6.8 %collective-permute-start.8 = (f32[128,128]{1,0:T(8,128)S(1)}, f32[128,128]{1,0:T(8,128)S(1)}, u32[]{:S(2)}, u32[]{:S(2)}) collective-permute-start(f32[128,128]{1,0:T(8,128)S(1)} %get-tuple-element.55), channel_id=1, source_target_pairs={{0,12},{4,8},{8,4},{12,0},{1,13},{5,9},{9,5},{13,1},{2,14},{6,10},... | collective-permute-start | bytes 196616 | tf_op jit(solution)/shard_map/ppermute | solution.py:438
  33.4 6.9 %collective-permute-start.11 = (f32[136,128]{1,0:T(8,128)S(1)}, f32[136,128]{1,0:T(8,128)S(1)}, u32[]{:S(2)}, u32[]{:S(2)}) collective-permute-start(f32[136,128]{1,0:T(8,128)S(1)} %shard_map.116.refs_0_), channel_id=1, source_target_pairs={{0,12},{4,8},{8,4},{12,0},{1,13},{5,9},{9,5},{13,1},{2,14},{6,10},... | collective-permute-start | bytes 208904 | tf_op jit(solution)/shard_map/ppermute | solution.py:438
  34.5 8.0 %collective-permute-start.10 = (f32[136,128]{1,0:T(8,128)S(1)}, f32[136,128]{1,0:T(8,128)S(1)}, u32[]{:S(2)}, u32[]{:S(2)}) collective-permute-start(f32[136,128]{1,0:T(8,128)S(1)} %shard_map.116.refs_0_), channel_id=1, source_target_pairs={{0,8},{4,12},{8,0},{12,4},{1,9},{5,13},{9,1},{13,5},{2,10},{6,14},... | collective-permute-start | bytes 208904 | tf_op jit(solution)/shard_map/ppermute | solution.py:438
  35.8 6.8 %collective-permute-start.9 = (f32[136,128]{1,0:T(8,128)S(1)}, f32[136,128]{1,0:T(8,128)S(1)}, u32[]{:S(2)}, u32[]{:S(2)}) collective-permute-start(f32[136,128]{1,0:T(8,128)S(1)} %shard_map.116.refs_0_), channel_id=1, source_target_pairs={{0,4},{4,0},{8,12},{12,8},{1,5},{5,1},{9,13},{13,9},{2,6},{6,2},{1... | collective-permute-start | bytes 208904 | tf_op jit(solution)/shard_map/ppermute | solution.py:438
  37.8 6.7 %collective-permute-start.15 = (f32[2,64,128]{2,1,0:T(8,128)S(1)}, f32[2,64,128]{2,1,0:T(8,128)S(1)}, u32[]{:S(2)}, u32[]{:S(2)}) collective-permute-start(f32[2,64,128]{2,1,0:T(8,128)S(1)} %get-tuple-element.60), channel_id=1, source_target_pairs={{0,1},{2,3},{1,0},{3,2},{4,5},{6,7},{5,4},{7,6},{8,9},{10,11},{9,8... | collective-permute-start | bytes 196616 | tf_op jit(solution)/shard_map/ppermute | solution.py:391
  37.8 6.7 %collective-permute-start.16 = (f32[2,64,128]{2,1,0:T(8,128)S(1)}, f32[2,64,128]{2,1,0:T(8,128)S(1)}, u32[]{:S(2)}, u32[]{:S(2)}) collective-permute-start(f32[2,64,128]{2,1,0:T(8,128)S(1)} %get-tuple-element.61), channel_id=1, source_target_pairs={{1,2},{2,1},{5,6},{6,5},{9,10},{10,9},{13,14},{14,13},{17,18},{18,... | collective-permute-start | bytes 196616 | tf_op jit(solution)/shard_map/ppermute | solution.py:390
  42.6 3.1 %collective-permute-start.14 = (f32[8,128]{1,0:T(8,128)S(1)}, f32[8,128]{1,0:T(8,128)S(1)}, u32[]{:S(2)}, u32[]{:S(2)}) collective-permute-start(f32[8,128]{1,0:T(8,128)S(1)} %shard_map.117.refs_4_), channel_id=1, source_target_pairs={{0,3},{1,2},{2,1},{3,0},{4,7},{5,6},{6,5},{7,4},{8,11},{9,10},{10,... | collective-permute-start | bytes 12296 | tf_op jit(solution)/shard_map/ppermute | solution.py:438
  42.6 3.7 %collective-permute-start.13 = (f32[8,128]{1,0:T(8,128)S(1)}, f32[8,128]{1,0:T(8,128)S(1)}, u32[]{:S(2)}, u32[]{:S(2)}) collective-permute-start(f32[8,128]{1,0:T(8,128)S(1)} %shard_map.117.refs_4_), channel_id=1, source_target_pairs={{0,2},{1,3},{2,0},{3,1},{4,6},{5,7},{6,4},{7,5},{8,10},{9,11},{10,... | collective-permute-start | bytes 12296 | tf_op jit(solution)/shard_map/ppermute | solution.py:438
  44.3 2.0 %collective-permute-start.12 = (f32[8,128]{1,0:T(8,128)S(1)}, f32[8,128]{1,0:T(8,128)S(1)}, u32[]{:S(2)}, u32[]{:S(2)}) collective-permute-start(f32[8,128]{1,0:T(8,128)S(1)} %shard_map.117.refs_4_), channel_id=1, source_target_pairs={{0,1},{1,0},{2,3},{3,2},{4,5},{5,4},{6,7},{7,6},{8,9},{9,8},{10,11... | collective-permute-start | bytes 12296 | tf_op jit(solution)/shard_map/ppermute | solution.py:438

commit v6 on v5

--- a/solution.py
+++ b/solution.py
@@ -309,38 +309,38 @@
 
 
 def sum_kernel(*refs):
-    *parts, out = refs
-    n = parts[0].shape[0]
+    *parts, out, top_out = refs
     top = jnp.zeros((8, LANES), jnp.float32)
-    for r in range(0, n, 8):
+    for r in range(0, out.shape[0], 8):
         total = parts[0][pl.ds(r, 8), :]
         for part in parts[1:]:
             total = total + part[pl.ds(r, 8), :]
         out[pl.ds(r, 8), :] = total
         top = jnp.maximum(top, jnp.abs(total))
+    top_out[...] = top
+
+
+def top_kernel(grad, *refs):
+    *parts, out = refs
+    n = grad.shape[0]
+    out[pl.ds(0, n), :] = grad[...]
+    top = parts[0][...]
+    for part in parts[1:]:
+        top = jnp.maximum(top, part[...])
     out[pl.ds(n, 8), :] = top
-
-
-def top_kernel(*refs):
-    *parts, out = refs
-    n = parts[0].shape[0] - 8
-    top = parts[0][pl.ds(n, 8), :]
-    for part in parts[1:]:
-        top = jnp.maximum(top, part[pl.ds(n, 8), :])
-    out[...] = top
 
 
 def update_kernel(depth, width, shots, *refs):
     grads, refs = refs[:shots], refs[shots:]
-    *tops, model, base, laps, new_model, stepped, grad = refs
+    model, base, laps, new_model, stepped, grad = refs
     n = depth * width // shots
     me = lax.axis_index("shot")
     for m in range(shots):
         owner = me if m == 0 else from_slot(me, m, shots)
         grad[pl.ds(pl.multiple_of(owner * n, n), n), :] = grads[m][pl.ds(0, n), :]
-    top = tops[0][...]
-    for other in tops[1:]:
-        top = jnp.maximum(top, other[...])
+    top = grads[0][pl.ds(n, 8), :]
+    for other in grads[1:]:
+        top = jnp.maximum(top, other[pl.ds(n, 8), :])
     peak = jnp.max(top)
     for p in range(depth):
         for r in range(0, width, 8):
@@ -440,9 +440,15 @@
 
     parts = with_others(pieces[0], pieces, "shot")
     a_edge, b_edge = exchange(a_edge, b_edge)
+    tile = VMEM((8, LANES), f32)
+    grad, top = call(
+        sum_kernel, [VMEM((rows, LANES), f32), tile], parts, [VMEM] * shots, [],
+        shots * rows * LANES, 4 * shots * rows * LANES,
+    )
+    tops = with_others(top, [top] * slabs, "slab")
     (grad,) = call(
-        sum_kernel, [VMEM((rows + 8, LANES), f32)], parts, [VMEM] * shots, [],
-        shots * rows * LANES, 4 * shots * rows * LANES,
+        top_kernel, [VMEM((rows + 8, LANES), f32)], [grad, *tops], [VMEM] * (slabs + 1), [],
+        0, 4096 * shots,
     )
     grads = with_others(grad, [grad] * shots, "shot")
     pad = VMEM((depth + 2, width + 2 * GUARD, LANES), f32)
@@ -451,11 +457,9 @@
         (u, u_later, a, a_later, a_edge, b_edge, mod, weight, extra), [VMEM] * 9,
         [pad, pad], 30 * cells, 32 * cells,
     )
-    (top,) = call(top_kernel, [VMEM((8, LANES), f32)], grads, [VMEM] * shots, [], 0, 4096 * shots)
-    tops = with_others(top, [top] * slabs, "slab")
     new_model, stepped = call(
         functools.partial(update_kernel, depth, width, shots), [out, out],
-        (*grads, *tops, model, base, lap), [VMEM] * (shots + slabs + 3),
+        (*grads, model, base, lap), [VMEM] * (shots + 3),
         [VMEM((depth * width, LANES), f32)], 10 * cells, 4 * 6 * cells,
     )
     return new_model, stepped[None], a[None]

time: 47.6 us -> 49.5 us (1.040)
  the two profiles are of different devices: /device:TPU:0 before, /device:TPU:1 now
where the time goes in v6:
time: 49.5 us; the launch traced here: 49.3 us
  starting transfers between devices  24.1 us (49%)
  waiting for transfers between devices  12.2 us (25%)
  Pallas kernels  11.5 us (23%)
  between operations  1.41 us (3%)
    ppermute x4, starting transfers between devices, exchange(): b = lax.ppermute(to_b, 'slab', perm_b)  13.2 us
    pallas_call x8, Pallas kernels, call(): pl.pallas_call(kernel, out_shape=outs, in_specs=[spec(space) for space in...  11.5 us
    ppermute x9, starting transfers between devices, with_others(): got[m] = lax.ppermute(pieces[m], axis, perms[m])  9.5 us
    ppermute x9, waiting for transfers between devices, with_others(): got[m] = lax.ppermute(pieces[m], axis, perms[m])  7.47 us
    ppermute x4, waiting for transfers between devices, exchange(): b = lax.ppermute(to_b, 'slab', perm_b)  3.66 us
    ppermute x4, starting transfers between devices, exchange(): return (lax.ppermute(to_a, 'slab', perm_a), b)  1.45 us
    ppermute x4, waiting for transfers between devices, exchange(): return (lax.ppermute(to_a, 'slab', perm_a), b)  1.09 us
  transfers between devices with their start and end apart: 17, of which 8 were waited for; matrix products, arithmetic and copies ran while one was open for 0% of the time, Pallas kernels for 17%

profile of v6, /device:TPU:1, one launch (start us, length us, event | category | flops | bytes accessed | tf_op | source)
XLA Modules:
  0.0 49.3 jit_solution(11915254194977984494)
XLA Ops:
  0.6 4.5 %collective-permute-start.3 = (f32[8,64,128]{2,1,0:T(8,128)}, f32[8,64,128]{2,1,0:T(8,128)S(1)}, u32[]{:S(2)}, u32[]{:S(2)}) collective-permute-start(f32[8,64,128]{2,1,0:T(8,128)} %bitcast.8), channel_id=1, source_target_pairs={{1,2},{2,1},{5,6},{6,5},{9,10},{10,9},{13,14},{14,13},{17,18},{18,... | collective-permute-start | bytes 786440 | tf_op jit(solution)/shard_map/ppermute | solution.py:390
  5.1 1.5 %shard_map.113 = (f32[14,64,128]{2,1,0:T(8,128)S(1)}, f32[14,64,128]{2,1,0:T(8,128)S(1)}, f32[8,64,128]{2,1,0:T(8,128)S(1)}, f32[8,64,128]{2,1,0:T(8,128)S(1)}, f32[8,64,128]{2,1,0:T(8,128)S(1)}) custom-call(f32[8,64,128]{2,1,0:T(8,128)} %bitcast.7, f32[8,64,128]{2,1,0:T(8,128)} %refs_1_.1, f32[8,64,128]{2,1,0:T(8,128)} %bitcast.9), custom_call_target="tpu_custom_call" | custom-call | bytes 1835008 | tf_op jit(solution)/shard_map/pallas_call | solution.py:362
  6.7 2.0 %collective-permute-start.5 = (f32[14,64,128]{2,1,0:T(8,128)S(1)}, f32[14,64,128]{2,1,0:T(8,128)S(1)}, u32[]{:S(2)}, u32[]{:S(2)}) collective-permute-start(f32[14,64,128]{2,1,0:T(8,128)S(1)} %get-tuple-element.47), channel_id=1, source_target_pairs={{1,2},{2,1},{5,6},{6,5},{9,10},{10,9},{13,14},{14,13},{17,18},{18,... | collective-permute-start | bytes 1376264 | tf_op jit(solution)/shard_map/ppermute | solution.py:390
  8.7 1.5 %shard_map.112 = (f32[13,64,128]{2,1,0:T(8,128)S(1)}, f32[13,64,128]{2,1,0:T(8,128)S(1)}, f32[8,64,128]{2,1,0:T(8,128)S(1)}, f32[8,64,128]{2,1,0:T(8,128)S(1)}, ...) custom-call(f32[8,64,128]{2,1,0:T(8,128)} %bitcast.11, f32[8,64,128]{2,1,0:T(8,128)} %bitcast.12, s32[1,128]{1,0:T(1,128)} %refs_2_.1, ...), custom_call_target="tpu_custom_call" | custom-call | bytes 1703936 | tf_op jit(solution)/shard_map/pallas_call | solution.py:362
  10.2 3.6 %collective-permute-start.1 = (f32[13,64,128]{2,1,0:T(8,128)S(1)}, f32[13,64,128]{2,1,0:T(8,128)S(1)}, u32[]{:S(2)}, u32[]{:S(2)}) collective-permute-start(f32[13,64,128]{2,1,0:T(8,128)S(1)} %get-tuple-element.40), channel_id=1, source_target_pairs={{1,2},{2,1},{5,6},{6,5},{9,10},{10,9},{13,14},{14,13},{17,18},{18,... | collective-permute-start | bytes 1277960 | tf_op jit(solution)/shard_map/ppermute | solution.py:390
  14.5 1.1 %collective-permute-done.2.ua_in = f32[8,64,128]{2,1,0:T(8,128)S(1)} collective-permute-done((f32[8,64,128]{2,1,0:T(8,128)}, f32[8,64,128]{2,1,0:T(8,128)S(1)}, u32[]{:S(2)}, u32[]{:S(2)}) %collective-permute-start.2) | collective-permute-done | bytes 262176 | tf_op jit(solution)/shard_map/ppermute | solution.py:391
  15.6 0.8 %collective-permute-done.5.hb_in = f32[14,64,128]{2,1,0:T(8,128)S(1)} collective-permute-done((f32[14,64,128]{2,1,0:T(8,128)S(1)}, f32[14,64,128]{2,1,0:T(8,128)S(1)}, u32[]{:S(2)}, u32[]{:S(2)}) %collective-permute-start.5) | collective-permute-done | bytes 458784 | tf_op jit(solution)/shard_map/ppermute | solution.py:390
  16.5 4.2 %shard_map.114 = (f32[8,64,128]{2,1,0:T(8,128)S(1)}, f32[8,64,128]{2,1,0:T(8,128)S(1)}, f32[8,8,64,128]{3,2,1,0:T(8,128)S(1)}, f32[64,128]{1,0:T(8,128)S(1)}, f3...) custom-call(f32[1,8]{1,0:T(1,128)} %wavelet.1, ...), custom_call_target="tpu_custom_call" | custom-call | flops 15728640 | bytes 5242880 | tf_op jit(solution)/shard_map/pallas_call | solution.py:362
  21.0 2.3 %shard_map.115 = (f32[8,64,128]{2,1,0:T(8,128)S(1)}, f32[8,64,128]{2,1,0:T(8,128)S(1)}, f32[2,64,128]{2,1,0:T(8,128)S(1)}, f32[2,64,128]{2,1,0:T(8,128)S(1)}, f3...) custom-call(f32[8,64,128]{2,1,0:T(8,128)S(1)} %get-tuple-element.37.now, ...), custom_call_target="tpu_custom_call" | custom-call | flops 18874368 | bytes 5242880 | tf_op jit(solution)/shard_map/pallas_call | solution.py:362
  23.4 1.4 %collective-permute-start.6 = (f32[128,128]{1,0:T(8,128)S(1)}, f32[128,128]{1,0:T(8,128)S(1)}, u32[]{:S(2)}, u32[]{:S(2)}) collective-permute-start(f32[128,128]{1,0:T(8,128)S(1)} %get-tuple-element.55), channel_id=1, source_target_pairs={{0,4},{4,0},{8,12},{12,8},{1,5},{5,1},{9,13},{13,9},{2,6},{6,2},{1... | collective-permute-start | bytes 196616 | tf_op jit(solution)/shard_map/ppermute | solution.py:438
  24.7 2.3 %collective-permute-start.7 = (f32[128,128]{1,0:T(8,128)S(1)}, f32[128,128]{1,0:T(8,128)S(1)}, u32[]{:S(2)}, u32[]{:S(2)}) collective-permute-start(f32[128,128]{1,0:T(8,128)S(1)} %get-tuple-element.56), channel_id=1, source_target_pairs={{0,8},{4,12},{8,0},{12,4},{1,9},{5,13},{9,1},{13,5},{2,10},{6,14},... | collective-permute-start | bytes 196616 | tf_op jit(solution)/shard_map/ppermute | solution.py:438
  27.0 3.8 %collective-permute-done.7.refs_2_ = f32[128,128]{1,0:T(8,128)S(1)} collective-permute-done((f32[128,128]{1,0:T(8,128)S(1)}, f32[128,128]{1,0:T(8,128)S(1)}, u32[]{:S(2)}, u32[]{:S(2)}) %collective-permute-start.7) | collective-permute-done | bytes 65568 | tf_op jit(solution)/shard_map/ppermute | solution.py:438
  30.8 2.1 %collective-permute-done.8.refs_3_ = f32[128,128]{1,0:T(8,128)S(1)} collective-permute-done((f32[128,128]{1,0:T(8,128)S(1)}, f32[128,128]{1,0:T(8,128)S(1)}, u32[]{:S(2)}, u32[]{:S(2)}) %collective-permute-start.8) | collective-permute-done | bytes 65568 | tf_op jit(solution)/shard_map/ppermute | solution.py:438
  32.9 1.1 %collective-permute-start.11 = (f32[8,128]{1,0:T(8,128)S(1)}, f32[8,128]{1,0:T(8,128)S(1)}, u32[]{:S(2)}, u32[]{:S(2)}) collective-permute-start(f32[8,128]{1,0:T(8,128)S(1)} %get-tuple-element.59.refs_0_), channel_id=1, source_target_pairs={{0,3},{1,2},{2,1},{3,0},{4,7},{5,6},{6,5},{7,4},{8,11},{9,10},{10,... | collective-permute-start | bytes 12296 | tf_op jit(solution)/shard_map/ppermute | solution.py:438
  34.0 0.7 %collective-permute-start.10 = (f32[8,128]{1,0:T(8,128)S(1)}, f32[8,128]{1,0:T(8,128)S(1)}, u32[]{:S(2)}, u32[]{:S(2)}) collective-permute-start(f32[8,128]{1,0:T(8,128)S(1)} %get-tuple-element.59.refs_0_), channel_id=1, source_target_pairs={{0,2},{1,3},{2,0},{3,1},{4,6},{5,7},{6,4},{7,5},{8,10},{9,11},{10,... | collective-permute-start | bytes 12296 | tf_op jit(solution)/shard_map/ppermute | solution.py:438
  35.1 0.9 %collective-permute-done.11.refs_3_ = f32[8,128]{1,0:T(8,128)S(1)} collective-permute-done((f32[8,128]{1,0:T(8,128)S(1)}, f32[8,128]{1,0:T(8,128)S(1)}, u32[]{:S(2)}, u32[]{:S(2)}) %collective-permute-start.11) | collective-permute-done | bytes 4128 | tf_op jit(solution)/shard_map/ppermute | solution.py:438
  36.1 0.7 %collective-permute-done.10.refs_2_ = f32[8,128]{1,0:T(8,128)S(1)} collective-permute-done((f32[8,128]{1,0:T(8,128)S(1)}, f32[8,128]{1,0:T(8,128)S(1)}, u32[]{:S(2)}, u32[]{:S(2)}) %collective-permute-start.10) | collective-permute-done | bytes 4128 | tf_op jit(solution)/shard_map/ppermute | solution.py:438
  36.7 0.9 %collective-permute-start.14 = (f32[136,128]{1,0:T(8,128)S(1)}, f32[136,128]{1,0:T(8,128)S(1)}, u32[]{:S(2)}, u32[]{:S(2)}) collective-permute-start(f32[136,128]{1,0:T(8,128)S(1)} %shard_map.117.refs_0_), channel_id=1, source_target_pairs={{0,12},{4,8},{8,4},{12,0},{1,13},{5,9},{9,5},{13,1},{2,14},{6,10},... | collective-permute-start | bytes 208904 | tf_op jit(solution)/shard_map/ppermute | solution.py:438
  38.0 2.4 %collective-permute-start.12 = (f32[136,128]{1,0:T(8,128)S(1)}, f32[136,128]{1,0:T(8,128)S(1)}, u32[]{:S(2)}, u32[]{:S(2)}) collective-permute-start(f32[136,128]{1,0:T(8,128)S(1)} %shard_map.117.refs_0_), channel_id=1, source_target_pairs={{0,4},{4,0},{8,12},{12,8},{1,5},{5,1},{9,13},{13,9},{2,6},{6,2},{1... | collective-permute-start | bytes 208904 | tf_op jit(solution)/shard_map/ppermute | solution.py:438
  40.4 1.2 %collective-permute-start.15 = (f32[2,64,128]{2,1,0:T(8,128)S(1)}, f32[2,64,128]{2,1,0:T(8,128)S(1)}, u32[]{:S(2)}, u32[]{:S(2)}) collective-permute-start(f32[2,64,128]{2,1,0:T(8,128)S(1)} %get-tuple-element.64), channel_id=1, source_target_pairs={{0,1},{2,3},{1,0},{3,2},{4,5},{6,7},{5,4},{7,6},{8,9},{10,11},{9,8... | collective-permute-start | bytes 196616 | tf_op jit(solution)/shard_map/ppermute | solution.py:391
  41.6 3.1 %collective-permute-start.16 = (f32[2,64,128]{2,1,0:T(8,128)S(1)}, f32[2,64,128]{2,1,0:T(8,128)S(1)}, u32[]{:S(2)}, u32[]{:S(2)}) collective-permute-start(f32[2,64,128]{2,1,0:T(8,128)S(1)} %get-tuple-element.65), channel_id=1, source_target_pairs={{1,2},{2,1},{5,6},{6,5},{9,10},{10,9},{13,14},{14,13},{17,18},{18,... | collective-permute-start | bytes 196616 | tf_op jit(solution)/shard_map/ppermute | solution.py:390
  44.7 2.4 %collective-permute-done.16.b_in = f32[2,64,128]{2,1,0:T(8,128)S(1)} collective-permute-done((f32[2,64,128]{2,1,0:T(8,128)S(1)}, f32[2,64,128]{2,1,0:T(8,128)S(1)}, u32[]{:S(2)}, u32[]{:S(2)}) %collective-permute-start.16) | collective-permute-done | bytes 65568 | tf_op jit(solution)/shard_map/ppermute | solution.py:390
  47.2 1.1 %shard_map.118 = (f32[8,64,128]{2,1,0:T(8,128)S(1)}, f32[8,64,128]{2,1,0:T(8,128)S(1)}, f32[8,64,128]{2,1,0:T(8,128)}) custom-call(f32[8,64,128]{2,1,0:T(8,128)S(1)} %get-tuple-element.60.u, f32[8,64,128]{2,1,0:T(8,128)S(1)} %get-tuple-element.61.u_later, f32[8,64,128]{2,1,0:T(8,128)S(1)} %get-tuple-element.62.a, ...), custom_call_target="tpu_custom_call" | custom-call | flops 1966080 | bytes 2097152 | tf_op jit(solution)/shard_map/pallas_call | solution.py:362
  48.3 1.0 %shard_map.119 = (f32[8,64,128]{2,1,0:T(8,128)}, f32[8,64,128]{2,1,0:T(8,128)}) custom-call(f32[136,128]{1,0:T(8,128)S(1)} %shard_map.117.refs_0_, f32[136,128]{1,0:T(8,128)S(1)} %collective-permute-done.12.refs_1_, f32[136,128]{1,0:T(8,128)S(1)} %collective-permute-done.13.refs_2_, f32[136,128]{1,0:T(8,128)S(1)} %collective-permute-done.14.refs_3_, ...), custom_call_target="tpu_custom_call" | custom-call | flops 655360 | bytes 1572864 | tf_op jit(solution)/shard_map/pallas_call | solution.py:362
  (18 shorter events, 1.3 us)
Async XLA Ops:
  0.6 13.2 %collective-permute-start.3 = (f32[8,64,128]{2,1,0:T(8,128)}, f32[8,64,128]{2,1,0:T(8,128)S(1)}, u32[]{:S(2)}, u32[]{:S(2)}) collective-permute-start(f32[8,64,128]{2,1,0:T(8,128)} %bitcast.8), channel_id=1, source_target_pairs={{1,2},{2,1},{5,6},{6,5},{9,10},{10,9},{13,14},{14,13},{17,18},{18,... | collective-permute-start | bytes 786440 | tf_op jit(solution)/shard_map/ppermute | solution.py:390
  6.6 9.0 %collective-permute-start.4 = (f32[14,64,128]{2,1,0:T(8,128)S(1)}, f32[14,64,128]{2,1,0:T(8,128)S(1)}, u32[]{:S(2)}, u32[]{:S(2)}) collective-permute-start(f32[14,64,128]{2,1,0:T(8,128)S(1)} %get-tuple-element.46), channel_id=1, source_target_pairs={{0,1},{2,3},{1,0},{3,2},{4,5},{6,7},{5,4},{7,6},{8,9},{10,11},{9,8... | collective-permute-start | bytes 1376264 | tf_op jit(solution)/shard_map/ppermute | solution.py:391
  6.7 9.8 %collective-permute-start.5 = (f32[14,64,128]{2,1,0:T(8,128)S(1)}, f32[14,64,128]{2,1,0:T(8,128)S(1)}, u32[]{:S(2)}, u32[]{:S(2)}) collective-permute-start(f32[14,64,128]{2,1,0:T(8,128)S(1)} %get-tuple-element.47), channel_id=1, source_target_pairs={{1,2},{2,1},{5,6},{6,5},{9,10},{10,9},{13,14},{14,13},{17,18},{18,... | collective-permute-start | bytes 1376264 | tf_op jit(solution)/shard_map/ppermute | solution.py:390
  10.1 10.6 %collective-permute-start = (f32[13,64,128]{2,1,0:T(8,128)S(1)}, f32[13,64,128]{2,1,0:T(8,128)S(1)}, u32[]{:S(2)}, u32[]{:S(2)}) collective-permute-start(f32[13,64,128]{2,1,0:T(8,128)S(1)} %get-tuple-element.39), channel_id=1, source_target_pairs={{0,1},{2,3},{1,0},{3,2},{4,5},{6,7},{5,4},{7,6},{8,9},{10,11},{9,8... | collective-permute-start | bytes 1277960 | tf_op jit(solution)/shard_map/ppermute | solution.py:391
  10.2 10.9 %collective-permute-start.1 = (f32[13,64,128]{2,1,0:T(8,128)S(1)}, f32[13,64,128]{2,1,0:T(8,128)S(1)}, u32[]{:S(2)}, u32[]{:S(2)}) collective-permute-start(f32[13,64,128]{2,1,0:T(8,128)S(1)} %get-tuple-element.40), channel_id=1, source_target_pairs={{1,2},{2,1},{5,6},{6,5},{9,10},{10,9},{13,14},{14,13},{17,18},{18,... | collective-permute-start | bytes 1277960 | tf_op jit(solution)/shard_map/ppermute | solution.py:390
  13.8 1.8 %collective-permute-start.2 = (f32[8,64,128]{2,1,0:T(8,128)}, f32[8,64,128]{2,1,0:T(8,128)S(1)}, u32[]{:S(2)}, u32[]{:S(2)}) collective-permute-start(f32[8,64,128]{2,1,0:T(8,128)} %bitcast.10), channel_id=1, source_target_pairs={{0,1},{2,3},{1,0},{3,2},{4,5},{6,7},{5,4},{7,6},{8,9},{10,11},{9,8... | collective-permute-start | bytes 786440 | tf_op jit(solution)/shard_map/ppermute | solution.py:391
  23.4 3.7 %collective-permute-start.6 = (f32[128,128]{1,0:T(8,128)S(1)}, f32[128,128]{1,0:T(8,128)S(1)}, u32[]{:S(2)}, u32[]{:S(2)}) collective-permute-start(f32[128,128]{1,0:T(8,128)S(1)} %get-tuple-element.55), channel_id=1, source_target_pairs={{0,4},{4,0},{8,12},{12,8},{1,5},{5,1},{9,13},{13,9},{2,6},{6,2},{1... | collective-permute-start | bytes 196616 | tf_op jit(solution)/shard_map/ppermute | solution.py:438
  24.7 6.1 %collective-permute-start.7 = (f32[128,128]{1,0:T(8,128)S(1)}, f32[128,128]{1,0:T(8,128)S(1)}, u32[]{:S(2)}, u32[]{:S(2)}) collective-permute-start(f32[128,128]{1,0:T(8,128)S(1)} %get-tuple-element.56), channel_id=1, source_target_pairs={{0,8},{4,12},{8,0},{12,4},{1,9},{5,13},{9,1},{13,5},{2,10},{6,14},... | collective-permute-start | bytes 196616 | tf_op jit(solution)/shard_map/ppermute | solution.py:438
  27.0 5.9 %collective-permute-start.8 = (f32[128,128]{1,0:T(8,128)S(1)}, f32[128,128]{1,0:T(8,128)S(1)}, u32[]{:S(2)}, u32[]{:S(2)}) collective-permute-start(f32[128,128]{1,0:T(8,128)S(1)} %get-tuple-element.57), channel_id=1, source_target_pairs={{0,12},{4,8},{8,4},{12,0},{1,13},{5,9},{9,5},{13,1},{2,14},{6,10},... | collective-permute-start | bytes 196616 | tf_op jit(solution)/shard_map/ppermute | solution.py:438
  32.9 3.2 %collective-permute-start.11 = (f32[8,128]{1,0:T(8,128)S(1)}, f32[8,128]{1,0:T(8,128)S(1)}, u32[]{:S(2)}, u32[]{:S(2)}) collective-permute-start(f32[8,128]{1,0:T(8,128)S(1)} %get-tuple-element.59.refs_0_), channel_id=1, source_target_pairs={{0,3},{1,2},{2,1},{3,0},{4,7},{5,6},{6,5},{7,4},{8,11},{9,10},{10,... | collective-permute-start | bytes 12296 | tf_op jit(solution)/shard_map/ppermute | solution.py:438
  34.0 2.7 %collective-permute-start.10 = (f32[8,128]{1,0:T(8,128)S(1)}, f32[8,128]{1,0:T(8,128)S(1)}, u32[]{:S(2)}, u32[]{:S(2)}) collective-permute-start(f32[8,128]{1,0:T(8,128)S(1)} %get-tuple-element.59.refs_0_), channel_id=1, source_target_pairs={{0,2},{1,3},{2,0},{3,1},{4,6},{5,7},{6,4},{7,5},{8,10},{9,11},{10,... | collective-permute-start | bytes 12296 | tf_op jit(solution)/shard_map/ppermute | solution.py:438
  34.8 1.9 %collective-permute-start.9 = (f32[8,128]{1,0:T(8,128)S(1)}, f32[8,128]{1,0:T(8,128)S(1)}, u32[]{:S(2)}, u32[]{:S(2)}) collective-permute-start(f32[8,128]{1,0:T(8,128)S(1)} %get-tuple-element.59.refs_0_), channel_id=1, source_target_pairs={{0,1},{1,0},{2,3},{3,2},{4,5},{5,4},{6,7},{7,6},{8,9},{9,8},{10,11... | collective-permute-start | bytes 12296 | tf_op jit(solution)/shard_map/ppermute | solution.py:438
  36.7 11.5 %collective-permute-start.14 = (f32[136,128]{1,0:T(8,128)S(1)}, f32[136,128]{1,0:T(8,128)S(1)}, u32[]{:S(2)}, u32[]{:S(2)}) collective-permute-start(f32[136,128]{1,0:T(8,128)S(1)} %shard_map.117.refs_0_), channel_id=1, source_target_pairs={{0,12},{4,8},{8,4},{12,0},{1,13},{5,9},{9,5},{13,1},{2,14},{6,10},... | collective-permute-start | bytes 208904 | tf_op jit(solution)/shard_map/ppermute | solution.py:438
  37.7 10.6 %collective-permute-start.13 = (f32[136,128]{1,0:T(8,128)S(1)}, f32[136,128]{1,0:T(8,128)S(1)}, u32[]{:S(2)}, u32[]{:S(2)}) collective-permute-start(f32[136,128]{1,0:T(8,128)S(1)} %shard_map.117.refs_0_), channel_id=1, source_target_pairs={{0,8},{4,12},{8,0},{12,4},{1,9},{5,13},{9,1},{13,5},{2,10},{6,14},... | collective-permute-start | bytes 208904 | tf_op jit(solution)/shard_map/ppermute | solution.py:438
  38.0 10.3 %collective-permute-start.12 = (f32[136,128]{1,0:T(8,128)S(1)}, f32[136,128]{1,0:T(8,128)S(1)}, u32[]{:S(2)}, u32[]{:S(2)}) collective-permute-start(f32[136,128]{1,0:T(8,128)S(1)} %shard_map.117.refs_0_), channel_id=1, source_target_pairs={{0,4},{4,0},{8,12},{12,8},{1,5},{5,1},{9,13},{13,9},{2,6},{6,2},{1... | collective-permute-start | bytes 208904 | tf_op jit(solution)/shard_map/ppermute | solution.py:438
  40.4 4.4 %collective-permute-start.15 = (f32[2,64,128]{2,1,0:T(8,128)S(1)}, f32[2,64,128]{2,1,0:T(8,128)S(1)}, u32[]{:S(2)}, u32[]{:S(2)}) collective-permute-start(f32[2,64,128]{2,1,0:T(8,128)S(1)} %get-tuple-element.64), channel_id=1, source_target_pairs={{0,1},{2,3},{1,0},{3,2},{4,5},{6,7},{5,4},{7,6},{8,9},{10,11},{9,8... | collective-permute-start | bytes 196616 | tf_op jit(solution)/shard_map/ppermute | solution.py:391
  41.6 5.6 %collective-permute-start.16 = (f32[2,64,128]{2,1,0:T(8,128)S(1)}, f32[2,64,128]{2,1,0:T(8,128)S(1)}, u32[]{:S(2)}, u32[]{:S(2)}) collective-permute-start(f32[2,64,128]{2,1,0:T(8,128)S(1)} %get-tuple-element.65), channel_id=1, source_target_pairs={{1,2},{2,1},{5,6},{6,5},{9,10},{10,9},{13,14},{14,13},{17,18},{18,... | collective-permute-start | bytes 196616 | tf_op jit(solution)/shard_map/ppermute | solution.py:390

commit v7 on v6

--- a/solution.py
+++ b/solution.py
@@ -6,6 +6,7 @@
 from jax.experimental import pallas as pl
 from jax.experimental.pallas import tpu as pltpu
 from jax.sharding import PartitionSpec as P
+
 
 ITERS = 8
 REACH = ITERS
@@ -432,9 +433,9 @@
         18 * ITERS * 2 * cells, 80 * cells,
     )
 
-    def with_others(own_one, pieces, axis):
+    def with_others(own_one, pieces, axis, order=far_first):
         got, perms = {}, partner_perms(lax.axis_size(axis))
-        for m in far_first(len(perms) + 1):
+        for m in order(len(perms) + 1):
             got[m] = lax.ppermute(pieces[m], axis, perms[m])
         return [own_one] + [got[m] for m in sorted(got)]
 
@@ -445,7 +446,7 @@
         sum_kernel, [VMEM((rows, LANES), f32), tile], parts, [VMEM] * shots, [],
         shots * rows * LANES, 4 * shots * rows * LANES,
     )
-    tops = with_others(top, [top] * slabs, "slab")
+    tops = with_others(top, [top] * slabs, "slab", lambda count: range(count - 1, 0, -1))
     (grad,) = call(
         top_kernel, [VMEM((rows + 8, LANES), f32)], [grad, *tops], [VMEM] * (slabs + 1), [],
         0, 4096 * shots,

time: 49.5 us -> 49.5 us (level)
  no operation moved by 1% of the time
where the time goes in v7:
time: 49.5 us; the launch traced here: 49.3 us
  starting transfers between devices  24.1 us (49%)
  waiting for transfers between devices  12.2 us (25%)
  Pallas kernels  11.5 us (23%)
  between operations  1.41 us (3%)
    ppermute x4, starting transfers between devices, exchange(): b = lax.ppermute(to_b, 'slab', perm_b)  13.2 us
    pallas_call x8, Pallas kernels, call(): pl.pallas_call(kernel, out_shape=outs, in_specs=[spec(space) for space in...  11.5 us
    ppermute x9, starting transfers between devices, with_others(): got[m] = lax.ppermute(pieces[m], axis, perms[m])  9.5 us
    ppermute x9, waiting for transfers between devices, with_others(): got[m] = lax.ppermute(pieces[m], axis, perms[m])  7.47 us
    ppermute x4, waiting for transfers between devices, exchange(): b = lax.ppermute(to_b, 'slab', perm_b)  3.66 us
    ppermute x4, starting transfers between devices, exchange(): return (lax.ppermute(to_a, 'slab', perm_a), b)  1.45 us
    ppermute x4, waiting for transfers between devices, exchange(): return (lax.ppermute(to_a, 'slab', perm_a), b)  1.09 us
  transfers between devices with their start and end apart: 17, of which 8 were waited for; matrix products, arithmetic and copies ran while one was open for 0% of the time, Pallas kernels for 17%

profile of v7, /device:TPU:1, one launch (start us, length us, event | category | flops | bytes accessed | tf_op | source)
XLA Modules:
  0.0 49.3 jit_solution(11915254194977984494)
XLA Ops:
  0.6 4.5 %collective-permute-start.3 = (f32[8,64,128]{2,1,0:T(8,128)}, f32[8,64,128]{2,1,0:T(8,128)S(1)}, u32[]{:S(2)}, u32[]{:S(2)}) collective-permute-start(f32[8,64,128]{2,1,0:T(8,128)} %bitcast.8), channel_id=1, source_target_pairs={{1,2},{2,1},{5,6},{6,5},{9,10},{10,9},{13,14},{14,13},{17,18},{18,... | collective-permute-start | bytes 786440 | tf_op jit(solution)/shard_map/ppermute | solution.py:391
  5.1 1.5 %shard_map.113 = (f32[14,64,128]{2,1,0:T(8,128)S(1)}, f32[14,64,128]{2,1,0:T(8,128)S(1)}, f32[8,64,128]{2,1,0:T(8,128)S(1)}, f32[8,64,128]{2,1,0:T(8,128)S(1)}, f32[8,64,128]{2,1,0:T(8,128)S(1)}) custom-call(f32[8,64,128]{2,1,0:T(8,128)} %bitcast.7, f32[8,64,128]{2,1,0:T(8,128)} %refs_1_.1, f32[8,64,128]{2,1,0:T(8,128)} %bitcast.9), custom_call_target="tpu_custom_call" | custom-call | bytes 1835008 | tf_op jit(solution)/shard_map/pallas_call | solution.py:363
  6.7 2.0 %collective-permute-start.5 = (f32[14,64,128]{2,1,0:T(8,128)S(1)}, f32[14,64,128]{2,1,0:T(8,128)S(1)}, u32[]{:S(2)}, u32[]{:S(2)}) collective-permute-start(f32[14,64,128]{2,1,0:T(8,128)S(1)} %get-tuple-element.47), channel_id=1, source_target_pairs={{1,2},{2,1},{5,6},{6,5},{9,10},{10,9},{13,14},{14,13},{17,18},{18,... | collective-permute-start | bytes 1376264 | tf_op jit(solution)/shard_map/ppermute | solution.py:391
  8.7 1.5 %shard_map.112 = (f32[13,64,128]{2,1,0:T(8,128)S(1)}, f32[13,64,128]{2,1,0:T(8,128)S(1)}, f32[8,64,128]{2,1,0:T(8,128)S(1)}, f32[8,64,128]{2,1,0:T(8,128)S(1)}, ...) custom-call(f32[8,64,128]{2,1,0:T(8,128)} %bitcast.11, f32[8,64,128]{2,1,0:T(8,128)} %bitcast.12, s32[1,128]{1,0:T(1,128)} %refs_2_.1, ...), custom_call_target="tpu_custom_call" | custom-call | bytes 1703936 | tf_op jit(solution)/shard_map/pallas_call | solution.py:363
  10.2 3.6 %collective-permute-start.1 = (f32[13,64,128]{2,1,0:T(8,128)S(1)}, f32[13,64,128]{2,1,0:T(8,128)S(1)}, u32[]{:S(2)}, u32[]{:S(2)}) collective-permute-start(f32[13,64,128]{2,1,0:T(8,128)S(1)} %get-tuple-element.40), channel_id=1, source_target_pairs={{1,2},{2,1},{5,6},{6,5},{9,10},{10,9},{13,14},{14,13},{17,18},{18,... | collective-permute-start | bytes 1277960 | tf_op jit(solution)/shard_map/ppermute | solution.py:391
  14.5 1.1 %collective-permute-done.2.ua_in = f32[8,64,128]{2,1,0:T(8,128)S(1)} collective-permute-done((f32[8,64,128]{2,1,0:T(8,128)}, f32[8,64,128]{2,1,0:T(8,128)S(1)}, u32[]{:S(2)}, u32[]{:S(2)}) %collective-permute-start.2) | collective-permute-done | bytes 262176 | tf_op jit(solution)/shard_map/ppermute | solution.py:392
  15.6 0.8 %collective-permute-done.5.hb_in = f32[14,64,128]{2,1,0:T(8,128)S(1)} collective-permute-done((f32[14,64,128]{2,1,0:T(8,128)S(1)}, f32[14,64,128]{2,1,0:T(8,128)S(1)}, u32[]{:S(2)}, u32[]{:S(2)}) %collective-permute-start.5) | collective-permute-done | bytes 458784 | tf_op jit(solution)/shard_map/ppermute | solution.py:391
  16.5 4.2 %shard_map.114 = (f32[8,64,128]{2,1,0:T(8,128)S(1)}, f32[8,64,128]{2,1,0:T(8,128)S(1)}, f32[8,8,64,128]{3,2,1,0:T(8,128)S(1)}, f32[64,128]{1,0:T(8,128)S(1)}, f3...) custom-call(f32[1,8]{1,0:T(1,128)} %wavelet.1, ...), custom_call_target="tpu_custom_call" | custom-call | flops 15728640 | bytes 5242880 | tf_op jit(solution)/shard_map/pallas_call | solution.py:363
  21.0 2.3 %shard_map.115 = (f32[8,64,128]{2,1,0:T(8,128)S(1)}, f32[8,64,128]{2,1,0:T(8,128)S(1)}, f32[2,64,128]{2,1,0:T(8,128)S(1)}, f32[2,64,128]{2,1,0:T(8,128)S(1)}, f3...) custom-call(f32[8,64,128]{2,1,0:T(8,128)S(1)} %get-tuple-element.37.now, ...), custom_call_target="tpu_custom_call" | custom-call | flops 18874368 | bytes 5242880 | tf_op jit(solution)/shard_map/pallas_call | solution.py:363
  23.4 1.4 %collective-permute-start.6 = (f32[128,128]{1,0:T(8,128)S(1)}, f32[128,128]{1,0:T(8,128)S(1)}, u32[]{:S(2)}, u32[]{:S(2)}) collective-permute-start(f32[128,128]{1,0:T(8,128)S(1)} %get-tuple-element.55), channel_id=1, source_target_pairs={{0,4},{4,0},{8,12},{12,8},{1,5},{5,1},{9,13},{13,9},{2,6},{6,2},{1... | collective-permute-start | bytes 196616 | tf_op jit(solution)/shard_map/ppermute | solution.py:439
  24.7 2.3 %collective-permute-start.7 = (f32[128,128]{1,0:T(8,128)S(1)}, f32[128,128]{1,0:T(8,128)S(1)}, u32[]{:S(2)}, u32[]{:S(2)}) collective-permute-start(f32[128,128]{1,0:T(8,128)S(1)} %get-tuple-element.56), channel_id=1, source_target_pairs={{0,8},{4,12},{8,0},{12,4},{1,9},{5,13},{9,1},{13,5},{2,10},{6,14},... | collective-permute-start | bytes 196616 | tf_op jit(solution)/shard_map/ppermute | solution.py:439
  27.0 3.8 %collective-permute-done.7.refs_2_ = f32[128,128]{1,0:T(8,128)S(1)} collective-permute-done((f32[128,128]{1,0:T(8,128)S(1)}, f32[128,128]{1,0:T(8,128)S(1)}, u32[]{:S(2)}, u32[]{:S(2)}) %collective-permute-start.7) | collective-permute-done | bytes 65568 | tf_op jit(solution)/shard_map/ppermute | solution.py:439
  30.8 2.1 %collective-permute-done.8.refs_3_ = f32[128,128]{1,0:T(8,128)S(1)} collective-permute-done((f32[128,128]{1,0:T(8,128)S(1)}, f32[128,128]{1,0:T(8,128)S(1)}, u32[]{:S(2)}, u32[]{:S(2)}) %collective-permute-start.8) | collective-permute-done | bytes 65568 | tf_op jit(solution)/shard_map/ppermute | solution.py:439
  32.9 1.1 %collective-permute-start.11 = (f32[8,128]{1,0:T(8,128)S(1)}, f32[8,128]{1,0:T(8,128)S(1)}, u32[]{:S(2)}, u32[]{:S(2)}) collective-permute-start(f32[8,128]{1,0:T(8,128)S(1)} %get-tuple-element.59.refs_0_), channel_id=1, source_target_pairs={{0,3},{1,2},{2,1},{3,0},{4,7},{5,6},{6,5},{7,4},{8,11},{9,10},{10,... | collective-permute-start | bytes 12296 | tf_op jit(solution)/shard_map/ppermute | solution.py:439
  34.0 0.7 %collective-permute-start.10 = (f32[8,128]{1,0:T(8,128)S(1)}, f32[8,128]{1,0:T(8,128)S(1)}, u32[]{:S(2)}, u32[]{:S(2)}) collective-permute-start(f32[8,128]{1,0:T(8,128)S(1)} %get-tuple-element.59.refs_0_), channel_id=1, source_target_pairs={{0,2},{1,3},{2,0},{3,1},{4,6},{5,7},{6,4},{7,5},{8,10},{9,11},{10,... | collective-permute-start | bytes 12296 | tf_op jit(solution)/shard_map/ppermute | solution.py:439
  35.1 0.9 %collective-permute-done.11.refs_3_ = f32[8,128]{1,0:T(8,128)S(1)} collective-permute-done((f32[8,128]{1,0:T(8,128)S(1)}, f32[8,128]{1,0:T(8,128)S(1)}, u32[]{:S(2)}, u32[]{:S(2)}) %collective-permute-start.11) | collective-permute-done | bytes 4128 | tf_op jit(solution)/shard_map/ppermute | solution.py:439
  36.1 0.7 %collective-permute-done.10.refs_2_ = f32[8,128]{1,0:T(8,128)S(1)} collective-permute-done((f32[8,128]{1,0:T(8,128)S(1)}, f32[8,128]{1,0:T(8,128)S(1)}, u32[]{:S(2)}, u32[]{:S(2)}) %collective-permute-start.10) | collective-permute-done | bytes 4128 | tf_op jit(solution)/shard_map/ppermute | solution.py:439
  36.7 0.9 %collective-permute-start.14 = (f32[136,128]{1,0:T(8,128)S(1)}, f32[136,128]{1,0:T(8,128)S(1)}, u32[]{:S(2)}, u32[]{:S(2)}) collective-permute-start(f32[136,128]{1,0:T(8,128)S(1)} %shard_map.117.refs_0_), channel_id=1, source_target_pairs={{0,12},{4,8},{8,4},{12,0},{1,13},{5,9},{9,5},{13,1},{2,14},{6,10},... | collective-permute-start | bytes 208904 | tf_op jit(solution)/shard_map/ppermute | solution.py:439
  38.0 2.4 %collective-permute-start.12 = (f32[136,128]{1,0:T(8,128)S(1)}, f32[136,128]{1,0:T(8,128)S(1)}, u32[]{:S(2)}, u32[]{:S(2)}) collective-permute-start(f32[136,128]{1,0:T(8,128)S(1)} %shard_map.117.refs_0_), channel_id=1, source_target_pairs={{0,4},{4,0},{8,12},{12,8},{1,5},{5,1},{9,13},{13,9},{2,6},{6,2},{1... | collective-permute-start | bytes 208904 | tf_op jit(solution)/shard_map/ppermute | solution.py:439
  40.4 1.2 %collective-permute-start.15 = (f32[2,64,128]{2,1,0:T(8,128)S(1)}, f32[2,64,128]{2,1,0:T(8,128)S(1)}, u32[]{:S(2)}, u32[]{:S(2)}) collective-permute-start(f32[2,64,128]{2,1,0:T(8,128)S(1)} %get-tuple-element.64), channel_id=1, source_target_pairs={{0,1},{2,3},{1,0},{3,2},{4,5},{6,7},{5,4},{7,6},{8,9},{10,11},{9,8... | collective-permute-start | bytes 196616 | tf_op jit(solution)/shard_map/ppermute | solution.py:392
  41.6 3.1 %collective-permute-start.16 = (f32[2,64,128]{2,1,0:T(8,128)S(1)}, f32[2,64,128]{2,1,0:T(8,128)S(1)}, u32[]{:S(2)}, u32[]{:S(2)}) collective-permute-start(f32[2,64,128]{2,1,0:T(8,128)S(1)} %get-tuple-element.65), channel_id=1, source_target_pairs={{1,2},{2,1},{5,6},{6,5},{9,10},{10,9},{13,14},{14,13},{17,18},{18,... | collective-permute-start | bytes 196616 | tf_op jit(solution)/shard_map/ppermute | solution.py:391
  44.7 2.4 %collective-permute-done.16.b_in = f32[2,64,128]{2,1,0:T(8,128)S(1)} collective-permute-done((f32[2,64,128]{2,1,0:T(8,128)S(1)}, f32[2,64,128]{2,1,0:T(8,128)S(1)}, u32[]{:S(2)}, u32[]{:S(2)}) %collective-permute-start.16) | collective-permute-done | bytes 65568 | tf_op jit(solution)/shard_map/ppermute | solution.py:391
  47.2 1.1 %shard_map.118 = (f32[8,64,128]{2,1,0:T(8,128)S(1)}, f32[8,64,128]{2,1,0:T(8,128)S(1)}, f32[8,64,128]{2,1,0:T(8,128)}) custom-call(f32[8,64,128]{2,1,0:T(8,128)S(1)} %get-tuple-element.60.u, f32[8,64,128]{2,1,0:T(8,128)S(1)} %get-tuple-element.61.u_later, f32[8,64,128]{2,1,0:T(8,128)S(1)} %get-tuple-element.62.a, ...), custom_call_target="tpu_custom_call" | custom-call | flops 1966080 | bytes 2097152 | tf_op jit(solution)/shard_map/pallas_call | solution.py:363
  48.3 1.0 %shard_map.119 = (f32[8,64,128]{2,1,0:T(8,128)}, f32[8,64,128]{2,1,0:T(8,128)}) custom-call(f32[136,128]{1,0:T(8,128)S(1)} %shard_map.117.refs_0_, f32[136,128]{1,0:T(8,128)S(1)} %collective-permute-done.12.refs_1_, f32[136,128]{1,0:T(8,128)S(1)} %collective-permute-done.13.refs_2_, f32[136,128]{1,0:T(8,128)S(1)} %collective-permute-done.14.refs_3_, ...), custom_call_target="tpu_custom_call" | custom-call | flops 655360 | bytes 1572864 | tf_op jit(solution)/shard_map/pallas_call | solution.py:363
  (18 shorter events, 1.3 us)
Async XLA Ops:
  0.6 13.2 %collective-permute-start.3 = (f32[8,64,128]{2,1,0:T(8,128)}, f32[8,64,128]{2,1,0:T(8,128)S(1)}, u32[]{:S(2)}, u32[]{:S(2)}) collective-permute-start(f32[8,64,128]{2,1,0:T(8,128)} %bitcast.8), channel_id=1, source_target_pairs={{1,2},{2,1},{5,6},{6,5},{9,10},{10,9},{13,14},{14,13},{17,18},{18,... | collective-permute-start | bytes 786440 | tf_op jit(solution)/shard_map/ppermute | solution.py:391
  6.6 9.0 %collective-permute-start.4 = (f32[14,64,128]{2,1,0:T(8,128)S(1)}, f32[14,64,128]{2,1,0:T(8,128)S(1)}, u32[]{:S(2)}, u32[]{:S(2)}) collective-permute-start(f32[14,64,128]{2,1,0:T(8,128)S(1)} %get-tuple-element.46), channel_id=1, source_target_pairs={{0,1},{2,3},{1,0},{3,2},{4,5},{6,7},{5,4},{7,6},{8,9},{10,11},{9,8... | collective-permute-start | bytes 1376264 | tf_op jit(solution)/shard_map/ppermute | solution.py:392
  6.7 9.8 %collective-permute-start.5 = (f32[14,64,128]{2,1,0:T(8,128)S(1)}, f32[14,64,128]{2,1,0:T(8,128)S(1)}, u32[]{:S(2)}, u32[]{:S(2)}) collective-permute-start(f32[14,64,128]{2,1,0:T(8,128)S(1)} %get-tuple-element.47), channel_id=1, source_target_pairs={{1,2},{2,1},{5,6},{6,5},{9,10},{10,9},{13,14},{14,13},{17,18},{18,... | collective-permute-start | bytes 1376264 | tf_op jit(solution)/shard_map/ppermute | solution.py:391
  10.1 10.6 %collective-permute-start = (f32[13,64,128]{2,1,0:T(8,128)S(1)}, f32[13,64,128]{2,1,0:T(8,128)S(1)}, u32[]{:S(2)}, u32[]{:S(2)}) collective-permute-start(f32[13,64,128]{2,1,0:T(8,128)S(1)} %get-tuple-element.39), channel_id=1, source_target_pairs={{0,1},{2,3},{1,0},{3,2},{4,5},{6,7},{5,4},{7,6},{8,9},{10,11},{9,8... | collective-permute-start | bytes 1277960 | tf_op jit(solution)/shard_map/ppermute | solution.py:392
  10.2 10.9 %collective-permute-start.1 = (f32[13,64,128]{2,1,0:T(8,128)S(1)}, f32[13,64,128]{2,1,0:T(8,128)S(1)}, u32[]{:S(2)}, u32[]{:S(2)}) collective-permute-start(f32[13,64,128]{2,1,0:T(8,128)S(1)} %get-tuple-element.40), channel_id=1, source_target_pairs={{1,2},{2,1},{5,6},{6,5},{9,10},{10,9},{13,14},{14,13},{17,18},{18,... | collective-permute-start | bytes 1277960 | tf_op jit(solution)/shard_map/ppermute | solution.py:391
  13.8 1.8 %collective-permute-start.2 = (f32[8,64,128]{2,1,0:T(8,128)}, f32[8,64,128]{2,1,0:T(8,128)S(1)}, u32[]{:S(2)}, u32[]{:S(2)}) collective-permute-start(f32[8,64,128]{2,1,0:T(8,128)} %bitcast.10), channel_id=1, source_target_pairs={{0,1},{2,3},{1,0},{3,2},{4,5},{6,7},{5,4},{7,6},{8,9},{10,11},{9,8... | collective-permute-start | bytes 786440 | tf_op jit(solution)/shard_map/ppermute | solution.py:392
  23.4 3.7 %collective-permute-start.6 = (f32[128,128]{1,0:T(8,128)S(1)}, f32[128,128]{1,0:T(8,128)S(1)}, u32[]{:S(2)}, u32[]{:S(2)}) collective-permute-start(f32[128,128]{1,0:T(8,128)S(1)} %get-tuple-element.55), channel_id=1, source_target_pairs={{0,4},{4,0},{8,12},{12,8},{1,5},{5,1},{9,13},{13,9},{2,6},{6,2},{1... | collective-permute-start | bytes 196616 | tf_op jit(solution)/shard_map/ppermute | solution.py:439
  24.7 6.1 %collective-permute-start.7 = (f32[128,128]{1,0:T(8,128)S(1)}, f32[128,128]{1,0:T(8,128)S(1)}, u32[]{:S(2)}, u32[]{:S(2)}) collective-permute-start(f32[128,128]{1,0:T(8,128)S(1)} %get-tuple-element.56), channel_id=1, source_target_pairs={{0,8},{4,12},{8,0},{12,4},{1,9},{5,13},{9,1},{13,5},{2,10},{6,14},... | collective-permute-start | bytes 196616 | tf_op jit(solution)/shard_map/ppermute | solution.py:439
  27.0 5.9 %collective-permute-start.8 = (f32[128,128]{1,0:T(8,128)S(1)}, f32[128,128]{1,0:T(8,128)S(1)}, u32[]{:S(2)}, u32[]{:S(2)}) collective-permute-start(f32[128,128]{1,0:T(8,128)S(1)} %get-tuple-element.57), channel_id=1, source_target_pairs={{0,12},{4,8},{8,4},{12,0},{1,13},{5,9},{9,5},{13,1},{2,14},{6,10},... | collective-permute-start | bytes 196616 | tf_op jit(solution)/shard_map/ppermute | solution.py:439
  32.9 3.2 %collective-permute-start.11 = (f32[8,128]{1,0:T(8,128)S(1)}, f32[8,128]{1,0:T(8,128)S(1)}, u32[]{:S(2)}, u32[]{:S(2)}) collective-permute-start(f32[8,128]{1,0:T(8,128)S(1)} %get-tuple-element.59.refs_0_), channel_id=1, source_target_pairs={{0,3},{1,2},{2,1},{3,0},{4,7},{5,6},{6,5},{7,4},{8,11},{9,10},{10,... | collective-permute-start | bytes 12296 | tf_op jit(solution)/shard_map/ppermute | solution.py:439
  34.0 2.7 %collective-permute-start.10 = (f32[8,128]{1,0:T(8,128)S(1)}, f32[8,128]{1,0:T(8,128)S(1)}, u32[]{:S(2)}, u32[]{:S(2)}) collective-permute-start(f32[8,128]{1,0:T(8,128)S(1)} %get-tuple-element.59.refs_0_), channel_id=1, source_target_pairs={{0,2},{1,3},{2,0},{3,1},{4,6},{5,7},{6,4},{7,5},{8,10},{9,11},{10,... | collective-permute-start | bytes 12296 | tf_op jit(solution)/shard_map/ppermute | solution.py:439
  34.8 1.9 %collective-permute-start.9 = (f32[8,128]{1,0:T(8,128)S(1)}, f32[8,128]{1,0:T(8,128)S(1)}, u32[]{:S(2)}, u32[]{:S(2)}) collective-permute-start(f32[8,128]{1,0:T(8,128)S(1)} %get-tuple-element.59.refs_0_), channel_id=1, source_target_pairs={{0,1},{1,0},{2,3},{3,2},{4,5},{5,4},{6,7},{7,6},{8,9},{9,8},{10,11... | collective-permute-start | bytes 12296 | tf_op jit(solution)/shard_map/ppermute | solution.py:439
  36.7 11.5 %collective-permute-start.14 = (f32[136,128]{1,0:T(8,128)S(1)}, f32[136,128]{1,0:T(8,128)S(1)}, u32[]{:S(2)}, u32[]{:S(2)}) collective-permute-start(f32[136,128]{1,0:T(8,128)S(1)} %shard_map.117.refs_0_), channel_id=1, source_target_pairs={{0,12},{4,8},{8,4},{12,0},{1,13},{5,9},{9,5},{13,1},{2,14},{6,10},... | collective-permute-start | bytes 208904 | tf_op jit(solution)/shard_map/ppermute | solution.py:439
  37.7 10.6 %collective-permute-start.13 = (f32[136,128]{1,0:T(8,128)S(1)}, f32[136,128]{1,0:T(8,128)S(1)}, u32[]{:S(2)}, u32[]{:S(2)}) collective-permute-start(f32[136,128]{1,0:T(8,128)S(1)} %shard_map.117.refs_0_), channel_id=1, source_target_pairs={{0,8},{4,12},{8,0},{12,4},{1,9},{5,13},{9,1},{13,5},{2,10},{6,14},... | collective-permute-start | bytes 208904 | tf_op jit(solution)/shard_map/ppermute | solution.py:439
  38.0 10.3 %collective-permute-start.12 = (f32[136,128]{1,0:T(8,128)S(1)}, f32[136,128]{1,0:T(8,128)S(1)}, u32[]{:S(2)}, u32[]{:S(2)}) collective-permute-start(f32[136,128]{1,0:T(8,128)S(1)} %shard_map.117.refs_0_), channel_id=1, source_target_pairs={{0,4},{4,0},{8,12},{12,8},{1,5},{5,1},{9,13},{13,9},{2,6},{6,2},{1... | collective-permute-start | bytes 208904 | tf_op jit(solution)/shard_map/ppermute | solution.py:439
  40.4 4.4 %collective-permute-start.15 = (f32[2,64,128]{2,1,0:T(8,128)S(1)}, f32[2,64,128]{2,1,0:T(8,128)S(1)}, u32[]{:S(2)}, u32[]{:S(2)}) collective-permute-start(f32[2,64,128]{2,1,0:T(8,128)S(1)} %get-tuple-element.64), channel_id=1, source_target_pairs={{0,1},{2,3},{1,0},{3,2},{4,5},{6,7},{5,4},{7,6},{8,9},{10,11},{9,8... | collective-permute-start | bytes 196616 | tf_op jit(solution)/shard_map/ppermute | solution.py:392
  41.6 5.6 %collective-permute-start.16 = (f32[2,64,128]{2,1,0:T(8,128)S(1)}, f32[2,64,128]{2,1,0:T(8,128)S(1)}, u32[]{:S(2)}, u32[]{:S(2)}) collective-permute-start(f32[2,64,128]{2,1,0:T(8,128)S(1)} %get-tuple-element.65), channel_id=1, source_target_pairs={{1,2},{2,1},{5,6},{6,5},{9,10},{10,9},{13,14},{14,13},{17,18},{18,... | collective-permute-start | bytes 196616 | tf_op jit(solution)/shard_map/ppermute | solution.py:391

commit v8 on v7

--- a/solution.py
+++ b/solution.py
@@ -15,6 +15,7 @@
 LIMIT = 16 * 2**20
 VMEM = pltpu.VMEM
 SMEM = pltpu.SMEM
+HBM = pl.ANY
 
 
 def pairs(count, start):
@@ -333,7 +334,8 @@
 
 def update_kernel(depth, width, shots, *refs):
     grads, refs = refs[:shots], refs[shots:]
-    model, base, laps, new_model, stepped, grad = refs
+    model, base, laps, model_out, stepped_out, grad, new_model, stepped, sem = refs
+    sent = []
     n = depth * width // shots
     me = lax.axis_index("shot")
     for m in range(shots):
@@ -350,6 +352,11 @@
             new = jnp.clip(model[p, rows, :] - 0.1 * g / (peak + 1e-06), 0.05, 0.3)
             new_model[p, rows, :] = new
             stepped[p, rows, :] = base[p, rows, :] + new * laps[p, rows, :]
+        for i, (src, dst) in enumerate(((new_model, model_out), (stepped, stepped_out))):
+            sent.append(pltpu.make_async_copy(src.at[p], dst.at[p], sem.at[i, p]))
+            sent[-1].start()
+    for copy in sent:
+        copy.wait()
 
 
 def placed(x, space):
@@ -358,13 +365,13 @@
     return x
 
 
-def call(kernel, outs, args, spaces, scratch, flops, nbytes):
+def call(kernel, outs, args, spaces, scratch, flops, nbytes, out_space=VMEM):
     args = [placed(x, space) for x, space in zip(args, spaces)]
     return pl.pallas_call(
         kernel,
         out_shape=outs,
         in_specs=[spec(space) for space in spaces],
-        out_specs=[spec(VMEM)] * len(outs),
+        out_specs=[spec(out_space)] * len(outs),
         scratch_shapes=scratch,
         cost_estimate=cost(flops, nbytes),
         compiler_params=pltpu.CompilerParams(vmem_limit_bytes=LIMIT),
@@ -461,7 +468,8 @@
     new_model, stepped = call(
         functools.partial(update_kernel, depth, width, shots), [out, out],
         (*grads, model, base, lap), [VMEM] * (shots + 3),
-        [VMEM((depth * width, LANES), f32)], 10 * cells, 4 * 6 * cells,
+        [VMEM((depth * width, LANES), f32), own, own, pltpu.SemaphoreType.DMA((2, depth))],
+        10 * cells, 4 * 6 * cells, HBM,
     )
     return new_model, stepped[None], a[None]
 

time: 49.5 us -> 49.6 us (level)
  no operation moved by 1% of the time
where the time goes in v8:
time: 49.6 us; the launch traced here: 49.3 us
  starting transfers between devices  24.1 us (49%)
  waiting for transfers between devices  12.2 us (25%)
  Pallas kernels  11.6 us (23%)
  between operations  1.41 us (3%)
    ppermute x4, starting transfers between devices, exchange(): b = lax.ppermute(to_b, 'slab', perm_b)  13.2 us
    pallas_call x8, Pallas kernels, call(): pl.pallas_call(kernel, out_shape=outs, in_specs=[spec(space) for space in...  11.6 us
    ppermute x9, starting transfers between devices, with_others(): got[m] = lax.ppermute(pieces[m], axis, perms[m])  9.5 us
    ppermute x9, waiting for transfers between devices, with_others(): got[m] = lax.ppermute(pieces[m], axis, perms[m])  7.47 us
    ppermute x4, waiting for transfers between devices, exchange(): b = lax.ppermute(to_b, 'slab', perm_b)  3.66 us
    ppermute x4, starting transfers between devices, exchange(): return (lax.ppermute(to_a, 'slab', perm_a), b)  1.45 us
    ppermute x4, waiting for transfers between devices, exchange(): return (lax.ppermute(to_a, 'slab', perm_a), b)  1.09 us
  transfers between devices with their start and end apart: 17, of which 8 were waited for; matrix products, arithmetic and copies ran while one was open for 0% of the time, Pallas kernels for 17%

profile of v8, /device:TPU:1, one launch (start us, length us, event | category | flops | bytes accessed | tf_op | source)
XLA Modules:
  0.0 49.3 jit_solution(4688711089650391404)
XLA Ops:
  0.6 4.5 %collective-permute-start.3 = (f32[8,64,128]{2,1,0:T(8,128)}, f32[8,64,128]{2,1,0:T(8,128)S(1)}, u32[]{:S(2)}, u32[]{:S(2)}) collective-permute-start(f32[8,64,128]{2,1,0:T(8,128)} %bitcast.8), channel_id=1, source_target_pairs={{1,2},{2,1},{5,6},{6,5},{9,10},{10,9},{13,14},{14,13},{17,18},{18,... | collective-permute-start | bytes 786440 | tf_op jit(solution)/shard_map/ppermute | solution.py:398
  5.1 1.5 %shard_map.113 = (f32[14,64,128]{2,1,0:T(8,128)S(1)}, f32[14,64,128]{2,1,0:T(8,128)S(1)}, f32[8,64,128]{2,1,0:T(8,128)S(1)}, f32[8,64,128]{2,1,0:T(8,128)S(1)}, f32[8,64,128]{2,1,0:T(8,128)S(1)}) custom-call(f32[8,64,128]{2,1,0:T(8,128)} %bitcast.7, f32[8,64,128]{2,1,0:T(8,128)} %refs_1_.1, f32[8,64,128]{2,1,0:T(8,128)} %bitcast.9), custom_call_target="tpu_custom_call" | custom-call | bytes 1835008 | tf_op jit(solution)/shard_map/pallas_call | solution.py:370
  6.7 2.0 %collective-permute-start.5 = (f32[14,64,128]{2,1,0:T(8,128)S(1)}, f32[14,64,128]{2,1,0:T(8,128)S(1)}, u32[]{:S(2)}, u32[]{:S(2)}) collective-permute-start(f32[14,64,128]{2,1,0:T(8,128)S(1)} %get-tuple-element.47), channel_id=1, source_target_pairs={{1,2},{2,1},{5,6},{6,5},{9,10},{10,9},{13,14},{14,13},{17,18},{18,... | collective-permute-start | bytes 1376264 | tf_op jit(solution)/shard_map/ppermute | solution.py:398
  8.7 1.5 %shard_map.112 = (f32[13,64,128]{2,1,0:T(8,128)S(1)}, f32[13,64,128]{2,1,0:T(8,128)S(1)}, f32[8,64,128]{2,1,0:T(8,128)S(1)}, f32[8,64,128]{2,1,0:T(8,128)S(1)}, ...) custom-call(f32[8,64,128]{2,1,0:T(8,128)} %bitcast.11, f32[8,64,128]{2,1,0:T(8,128)} %bitcast.12, s32[1,128]{1,0:T(1,128)} %refs_2_.1, ...), custom_call_target="tpu_custom_call" | custom-call | bytes 1703936 | tf_op jit(solution)/shard_map/pallas_call | solution.py:370
  10.2 3.6 %collective-permute-start.1 = (f32[13,64,128]{2,1,0:T(8,128)S(1)}, f32[13,64,128]{2,1,0:T(8,128)S(1)}, u32[]{:S(2)}, u32[]{:S(2)}) collective-permute-start(f32[13,64,128]{2,1,0:T(8,128)S(1)} %get-tuple-element.40), channel_id=1, source_target_pairs={{1,2},{2,1},{5,6},{6,5},{9,10},{10,9},{13,14},{14,13},{17,18},{18,... | collective-permute-start | bytes 1277960 | tf_op jit(solution)/shard_map/ppermute | solution.py:398
  14.5 1.1 %collective-permute-done.2.ua_in = f32[8,64,128]{2,1,0:T(8,128)S(1)} collective-permute-done((f32[8,64,128]{2,1,0:T(8,128)}, f32[8,64,128]{2,1,0:T(8,128)S(1)}, u32[]{:S(2)}, u32[]{:S(2)}) %collective-permute-start.2) | collective-permute-done | bytes 262176 | tf_op jit(solution)/shard_map/ppermute | solution.py:399
  15.6 0.8 %collective-permute-done.5.hb_in = f32[14,64,128]{2,1,0:T(8,128)S(1)} collective-permute-done((f32[14,64,128]{2,1,0:T(8,128)S(1)}, f32[14,64,128]{2,1,0:T(8,128)S(1)}, u32[]{:S(2)}, u32[]{:S(2)}) %collective-permute-start.5) | collective-permute-done | bytes 458784 | tf_op jit(solution)/shard_map/ppermute | solution.py:398
  16.5 4.2 %shard_map.114 = (f32[8,64,128]{2,1,0:T(8,128)S(1)}, f32[8,64,128]{2,1,0:T(8,128)S(1)}, f32[8,8,64,128]{3,2,1,0:T(8,128)S(1)}, f32[64,128]{1,0:T(8,128)S(1)}, f3...) custom-call(f32[1,8]{1,0:T(1,128)} %wavelet.1, ...), custom_call_target="tpu_custom_call" | custom-call | flops 15728640 | bytes 5242880 | tf_op jit(solution)/shard_map/pallas_call | solution.py:370
  21.0 2.3 %shard_map.115 = (f32[8,64,128]{2,1,0:T(8,128)S(1)}, f32[8,64,128]{2,1,0:T(8,128)S(1)}, f32[2,64,128]{2,1,0:T(8,128)S(1)}, f32[2,64,128]{2,1,0:T(8,128)S(1)}, f3...) custom-call(f32[8,64,128]{2,1,0:T(8,128)S(1)} %get-tuple-element.37.now, ...), custom_call_target="tpu_custom_call" | custom-call | flops 18874368 | bytes 5242880 | tf_op jit(solution)/shard_map/pallas_call | solution.py:370
  23.4 1.4 %collective-permute-start.6 = (f32[128,128]{1,0:T(8,128)S(1)}, f32[128,128]{1,0:T(8,128)S(1)}, u32[]{:S(2)}, u32[]{:S(2)}) collective-permute-start(f32[128,128]{1,0:T(8,128)S(1)} %get-tuple-element.55), channel_id=1, source_target_pairs={{0,4},{4,0},{8,12},{12,8},{1,5},{5,1},{9,13},{13,9},{2,6},{6,2},{1... | collective-permute-start | bytes 196616 | tf_op jit(solution)/shard_map/ppermute | solution.py:446
  24.7 2.3 %collective-permute-start.7 = (f32[128,128]{1,0:T(8,128)S(1)}, f32[128,128]{1,0:T(8,128)S(1)}, u32[]{:S(2)}, u32[]{:S(2)}) collective-permute-start(f32[128,128]{1,0:T(8,128)S(1)} %get-tuple-element.56), channel_id=1, source_target_pairs={{0,8},{4,12},{8,0},{12,4},{1,9},{5,13},{9,1},{13,5},{2,10},{6,14},... | collective-permute-start | bytes 196616 | tf_op jit(solution)/shard_map/ppermute | solution.py:446
  27.0 3.8 %collective-permute-done.7.refs_2_ = f32[128,128]{1,0:T(8,128)S(1)} collective-permute-done((f32[128,128]{1,0:T(8,128)S(1)}, f32[128,128]{1,0:T(8,128)S(1)}, u32[]{:S(2)}, u32[]{:S(2)}) %collective-permute-start.7) | collective-permute-done | bytes 65568 | tf_op jit(solution)/shard_map/ppermute | solution.py:446
  30.8 2.1 %collective-permute-done.8.refs_3_ = f32[128,128]{1,0:T(8,128)S(1)} collective-permute-done((f32[128,128]{1,0:T(8,128)S(1)}, f32[128,128]{1,0:T(8,128)S(1)}, u32[]{:S(2)}, u32[]{:S(2)}) %collective-permute-start.8) | collective-permute-done | bytes 65568 | tf_op jit(solution)/shard_map/ppermute | solution.py:446
  32.9 1.1 %collective-permute-start.11 = (f32[8,128]{1,0:T(8,128)S(1)}, f32[8,128]{1,0:T(8,128)S(1)}, u32[]{:S(2)}, u32[]{:S(2)}) collective-permute-start(f32[8,128]{1,0:T(8,128)S(1)} %get-tuple-element.59.refs_0_), channel_id=1, source_target_pairs={{0,3},{1,2},{2,1},{3,0},{4,7},{5,6},{6,5},{7,4},{8,11},{9,10},{10,... | collective-permute-start | bytes 12296 | tf_op jit(solution)/shard_map/ppermute | solution.py:446
  34.0 0.7 %collective-permute-start.10 = (f32[8,128]{1,0:T(8,128)S(1)}, f32[8,128]{1,0:T(8,128)S(1)}, u32[]{:S(2)}, u32[]{:S(2)}) collective-permute-start(f32[8,128]{1,0:T(8,128)S(1)} %get-tuple-element.59.refs_0_), channel_id=1, source_target_pairs={{0,2},{1,3},{2,0},{3,1},{4,6},{5,7},{6,4},{7,5},{8,10},{9,11},{10,... | collective-permute-start | bytes 12296 | tf_op jit(solution)/shard_map/ppermute | solution.py:446
  35.1 0.9 %collective-permute-done.11.refs_3_ = f32[8,128]{1,0:T(8,128)S(1)} collective-permute-done((f32[8,128]{1,0:T(8,128)S(1)}, f32[8,128]{1,0:T(8,128)S(1)}, u32[]{:S(2)}, u32[]{:S(2)}) %collective-permute-start.11) | collective-permute-done | bytes 4128 | tf_op jit(solution)/shard_map/ppermute | solution.py:446
  36.1 0.7 %collective-permute-done.10.refs_2_ = f32[8,128]{1,0:T(8,128)S(1)} collective-permute-done((f32[8,128]{1,0:T(8,128)S(1)}, f32[8,128]{1,0:T(8,128)S(1)}, u32[]{:S(2)}, u32[]{:S(2)}) %collective-permute-start.10) | collective-permute-done | bytes 4128 | tf_op jit(solution)/shard_map/ppermute | solution.py:446
  36.7 0.9 %collective-permute-start.14 = (f32[136,128]{1,0:T(8,128)S(1)}, f32[136,128]{1,0:T(8,128)S(1)}, u32[]{:S(2)}, u32[]{:S(2)}) collective-permute-start(f32[136,128]{1,0:T(8,128)S(1)} %shard_map.117.refs_0_), channel_id=1, source_target_pairs={{0,12},{4,8},{8,4},{12,0},{1,13},{5,9},{9,5},{13,1},{2,14},{6,10},... | collective-permute-start | bytes 208904 | tf_op jit(solution)/shard_map/ppermute | solution.py:446
  38.0 2.4 %collective-permute-start.12 = (f32[136,128]{1,0:T(8,128)S(1)}, f32[136,128]{1,0:T(8,128)S(1)}, u32[]{:S(2)}, u32[]{:S(2)}) collective-permute-start(f32[136,128]{1,0:T(8,128)S(1)} %shard_map.117.refs_0_), channel_id=1, source_target_pairs={{0,4},{4,0},{8,12},{12,8},{1,5},{5,1},{9,13},{13,9},{2,6},{6,2},{1... | collective-permute-start | bytes 208904 | tf_op jit(solution)/shard_map/ppermute | solution.py:446
  40.4 1.2 %collective-permute-start.15 = (f32[2,64,128]{2,1,0:T(8,128)S(1)}, f32[2,64,128]{2,1,0:T(8,128)S(1)}, u32[]{:S(2)}, u32[]{:S(2)}) collective-permute-start(f32[2,64,128]{2,1,0:T(8,128)S(1)} %get-tuple-element.64), channel_id=1, source_target_pairs={{0,1},{2,3},{1,0},{3,2},{4,5},{6,7},{5,4},{7,6},{8,9},{10,11},{9,8... | collective-permute-start | bytes 196616 | tf_op jit(solution)/shard_map/ppermute | solution.py:399
  41.6 3.1 %collective-permute-start.16 = (f32[2,64,128]{2,1,0:T(8,128)S(1)}, f32[2,64,128]{2,1,0:T(8,128)S(1)}, u32[]{:S(2)}, u32[]{:S(2)}) collective-permute-start(f32[2,64,128]{2,1,0:T(8,128)S(1)} %get-tuple-element.65), channel_id=1, source_target_pairs={{1,2},{2,1},{5,6},{6,5},{9,10},{10,9},{13,14},{14,13},{17,18},{18,... | collective-permute-start | bytes 196616 | tf_op jit(solution)/shard_map/ppermute | solution.py:398
  44.7 2.4 %collective-permute-done.16.b_in = f32[2,64,128]{2,1,0:T(8,128)S(1)} collective-permute-done((f32[2,64,128]{2,1,0:T(8,128)S(1)}, f32[2,64,128]{2,1,0:T(8,128)S(1)}, u32[]{:S(2)}, u32[]{:S(2)}) %collective-permute-start.16) | collective-permute-done | bytes 65568 | tf_op jit(solution)/shard_map/ppermute | solution.py:398
  47.2 1.1 %shard_map.118 = (f32[8,64,128]{2,1,0:T(8,128)S(1)}, f32[8,64,128]{2,1,0:T(8,128)S(1)}, f32[8,64,128]{2,1,0:T(8,128)}) custom-call(f32[8,64,128]{2,1,0:T(8,128)S(1)} %get-tuple-element.60.u, f32[8,64,128]{2,1,0:T(8,128)S(1)} %get-tuple-element.61.u_later, f32[8,64,128]{2,1,0:T(8,128)S(1)} %get-tuple-element.62.a, ...), custom_call_target="tpu_custom_call" | custom-call | flops 1966080 | bytes 2097152 | tf_op jit(solution)/shard_map/pallas_call | solution.py:370
  48.3 1.1 %shard_map.119 = (f32[8,64,128]{2,1,0:T(8,128)}, f32[8,64,128]{2,1,0:T(8,128)}) custom-call(f32[136,128]{1,0:T(8,128)S(1)} %shard_map.117.refs_0_, f32[136,128]{1,0:T(8,128)S(1)} %collective-permute-done.12.refs_1_, f32[136,128]{1,0:T(8,128)S(1)} %collective-permute-done.13.refs_2_, f32[136,128]{1,0:T(8,128)S(1)} %collective-permute-done.14.refs_3_, ...), custom_call_target="tpu_custom_call" | custom-call | flops 655360 | bytes 1572864 | tf_op jit(solution)/shard_map/pallas_call | solution.py:370
  (18 shorter events, 1.3 us)
Async XLA Ops:
  0.6 13.2 %collective-permute-start.3 = (f32[8,64,128]{2,1,0:T(8,128)}, f32[8,64,128]{2,1,0:T(8,128)S(1)}, u32[]{:S(2)}, u32[]{:S(2)}) collective-permute-start(f32[8,64,128]{2,1,0:T(8,128)} %bitcast.8), channel_id=1, source_target_pairs={{1,2},{2,1},{5,6},{6,5},{9,10},{10,9},{13,14},{14,13},{17,18},{18,... | collective-permute-start | bytes 786440 | tf_op jit(solution)/shard_map/ppermute | solution.py:398
  6.6 9.0 %collective-permute-start.4 = (f32[14,64,128]{2,1,0:T(8,128)S(1)}, f32[14,64,128]{2,1,0:T(8,128)S(1)}, u32[]{:S(2)}, u32[]{:S(2)}) collective-permute-start(f32[14,64,128]{2,1,0:T(8,128)S(1)} %get-tuple-element.46), channel_id=1, source_target_pairs={{0,1},{2,3},{1,0},{3,2},{4,5},{6,7},{5,4},{7,6},{8,9},{10,11},{9,8... | collective-permute-start | bytes 1376264 | tf_op jit(solution)/shard_map/ppermute | solution.py:399
  6.7 9.8 %collective-permute-start.5 = (f32[14,64,128]{2,1,0:T(8,128)S(1)}, f32[14,64,128]{2,1,0:T(8,128)S(1)}, u32[]{:S(2)}, u32[]{:S(2)}) collective-permute-start(f32[14,64,128]{2,1,0:T(8,128)S(1)} %get-tuple-element.47), channel_id=1, source_target_pairs={{1,2},{2,1},{5,6},{6,5},{9,10},{10,9},{13,14},{14,13},{17,18},{18,... | collective-permute-start | bytes 1376264 | tf_op jit(solution)/shard_map/ppermute | solution.py:398
  10.1 10.6 %collective-permute-start = (f32[13,64,128]{2,1,0:T(8,128)S(1)}, f32[13,64,128]{2,1,0:T(8,128)S(1)}, u32[]{:S(2)}, u32[]{:S(2)}) collective-permute-start(f32[13,64,128]{2,1,0:T(8,128)S(1)} %get-tuple-element.39), channel_id=1, source_target_pairs={{0,1},{2,3},{1,0},{3,2},{4,5},{6,7},{5,4},{7,6},{8,9},{10,11},{9,8... | collective-permute-start | bytes 1277960 | tf_op jit(solution)/shard_map/ppermute | solution.py:399
  10.2 10.9 %collective-permute-start.1 = (f32[13,64,128]{2,1,0:T(8,128)S(1)}, f32[13,64,128]{2,1,0:T(8,128)S(1)}, u32[]{:S(2)}, u32[]{:S(2)}) collective-permute-start(f32[13,64,128]{2,1,0:T(8,128)S(1)} %get-tuple-element.40), channel_id=1, source_target_pairs={{1,2},{2,1},{5,6},{6,5},{9,10},{10,9},{13,14},{14,13},{17,18},{18,... | collective-permute-start | bytes 1277960 | tf_op jit(solution)/shard_map/ppermute | solution.py:398
  13.8 1.8 %collective-permute-start.2 = (f32[8,64,128]{2,1,0:T(8,128)}, f32[8,64,128]{2,1,0:T(8,128)S(1)}, u32[]{:S(2)}, u32[]{:S(2)}) collective-permute-start(f32[8,64,128]{2,1,0:T(8,128)} %bitcast.10), channel_id=1, source_target_pairs={{0,1},{2,3},{1,0},{3,2},{4,5},{6,7},{5,4},{7,6},{8,9},{10,11},{9,8... | collective-permute-start | bytes 786440 | tf_op jit(solution)/shard_map/ppermute | solution.py:399
  23.4 3.7 %collective-permute-start.6 = (f32[128,128]{1,0:T(8,128)S(1)}, f32[128,128]{1,0:T(8,128)S(1)}, u32[]{:S(2)}, u32[]{:S(2)}) collective-permute-start(f32[128,128]{1,0:T(8,128)S(1)} %get-tuple-element.55), channel_id=1, source_target_pairs={{0,4},{4,0},{8,12},{12,8},{1,5},{5,1},{9,13},{13,9},{2,6},{6,2},{1... | collective-permute-start | bytes 196616 | tf_op jit(solution)/shard_map/ppermute | solution.py:446
  24.7 6.1 %collective-permute-start.7 = (f32[128,128]{1,0:T(8,128)S(1)}, f32[128,128]{1,0:T(8,128)S(1)}, u32[]{:S(2)}, u32[]{:S(2)}) collective-permute-start(f32[128,128]{1,0:T(8,128)S(1)} %get-tuple-element.56), channel_id=1, source_target_pairs={{0,8},{4,12},{8,0},{12,4},{1,9},{5,13},{9,1},{13,5},{2,10},{6,14},... | collective-permute-start | bytes 196616 | tf_op jit(solution)/shard_map/ppermute | solution.py:446
  27.0 5.9 %collective-permute-start.8 = (f32[128,128]{1,0:T(8,128)S(1)}, f32[128,128]{1,0:T(8,128)S(1)}, u32[]{:S(2)}, u32[]{:S(2)}) collective-permute-start(f32[128,128]{1,0:T(8,128)S(1)} %get-tuple-element.57), channel_id=1, source_target_pairs={{0,12},{4,8},{8,4},{12,0},{1,13},{5,9},{9,5},{13,1},{2,14},{6,10},... | collective-permute-start | bytes 196616 | tf_op jit(solution)/shard_map/ppermute | solution.py:446
  32.9 3.2 %collective-permute-start.11 = (f32[8,128]{1,0:T(8,128)S(1)}, f32[8,128]{1,0:T(8,128)S(1)}, u32[]{:S(2)}, u32[]{:S(2)}) collective-permute-start(f32[8,128]{1,0:T(8,128)S(1)} %get-tuple-element.59.refs_0_), channel_id=1, source_target_pairs={{0,3},{1,2},{2,1},{3,0},{4,7},{5,6},{6,5},{7,4},{8,11},{9,10},{10,... | collective-permute-start | bytes 12296 | tf_op jit(solution)/shard_map/ppermute | solution.py:446
  34.0 2.7 %collective-permute-start.10 = (f32[8,128]{1,0:T(8,128)S(1)}, f32[8,128]{1,0:T(8,128)S(1)}, u32[]{:S(2)}, u32[]{:S(2)}) collective-permute-start(f32[8,128]{1,0:T(8,128)S(1)} %get-tuple-element.59.refs_0_), channel_id=1, source_target_pairs={{0,2},{1,3},{2,0},{3,1},{4,6},{5,7},{6,4},{7,5},{8,10},{9,11},{10,... | collective-permute-start | bytes 12296 | tf_op jit(solution)/shard_map/ppermute | solution.py:446
  34.8 1.9 %collective-permute-start.9 = (f32[8,128]{1,0:T(8,128)S(1)}, f32[8,128]{1,0:T(8,128)S(1)}, u32[]{:S(2)}, u32[]{:S(2)}) collective-permute-start(f32[8,128]{1,0:T(8,128)S(1)} %get-tuple-element.59.refs_0_), channel_id=1, source_target_pairs={{0,1},{1,0},{2,3},{3,2},{4,5},{5,4},{6,7},{7,6},{8,9},{9,8},{10,11... | collective-permute-start | bytes 12296 | tf_op jit(solution)/shard_map/ppermute | solution.py:446
  36.7 11.5 %collective-permute-start.14 = (f32[136,128]{1,0:T(8,128)S(1)}, f32[136,128]{1,0:T(8,128)S(1)}, u32[]{:S(2)}, u32[]{:S(2)}) collective-permute-start(f32[136,128]{1,0:T(8,128)S(1)} %shard_map.117.refs_0_), channel_id=1, source_target_pairs={{0,12},{4,8},{8,4},{12,0},{1,13},{5,9},{9,5},{13,1},{2,14},{6,10},... | collective-permute-start | bytes 208904 | tf_op jit(solution)/shard_map/ppermute | solution.py:446
  37.7 10.6 %collective-permute-start.13 = (f32[136,128]{1,0:T(8,128)S(1)}, f32[136,128]{1,0:T(8,128)S(1)}, u32[]{:S(2)}, u32[]{:S(2)}) collective-permute-start(f32[136,128]{1,0:T(8,128)S(1)} %shard_map.117.refs_0_), channel_id=1, source_target_pairs={{0,8},{4,12},{8,0},{12,4},{1,9},{5,13},{9,1},{13,5},{2,10},{6,14},... | collective-permute-start | bytes 208904 | tf_op jit(solution)/shard_map/ppermute | solution.py:446
  38.0 10.3 %collective-permute-start.12 = (f32[136,128]{1,0:T(8,128)S(1)}, f32[136,128]{1,0:T(8,128)S(1)}, u32[]{:S(2)}, u32[]{:S(2)}) collective-permute-start(f32[136,128]{1,0:T(8,128)S(1)} %shard_map.117.refs_0_), channel_id=1, source_target_pairs={{0,4},{4,0},{8,12},{12,8},{1,5},{5,1},{9,13},{13,9},{2,6},{6,2},{1... | collective-permute-start | bytes 208904 | tf_op jit(solution)/shard_map/ppermute | solution.py:446
  40.4 4.4 %collective-permute-start.15 = (f32[2,64,128]{2,1,0:T(8,128)S(1)}, f32[2,64,128]{2,1,0:T(8,128)S(1)}, u32[]{:S(2)}, u32[]{:S(2)}) collective-permute-start(f32[2,64,128]{2,1,0:T(8,128)S(1)} %get-tuple-element.64), channel_id=1, source_target_pairs={{0,1},{2,3},{1,0},{3,2},{4,5},{6,7},{5,4},{7,6},{8,9},{10,11},{9,8... | collective-permute-start | bytes 196616 | tf_op jit(solution)/shard_map/ppermute | solution.py:399
  41.6 5.6 %collective-permute-start.16 = (f32[2,64,128]{2,1,0:T(8,128)S(1)}, f32[2,64,128]{2,1,0:T(8,128)S(1)}, u32[]{:S(2)}, u32[]{:S(2)}) collective-permute-start(f32[2,64,128]{2,1,0:T(8,128)S(1)} %get-tuple-element.65), channel_id=1, source_target_pairs={{1,2},{2,1},{5,6},{6,5},{9,10},{10,9},{13,14},{14,13},{17,18},{18,... | collective-permute-start | bytes 196616 | tf_op jit(solution)/shard_map/ppermute | solution.py:398
